TPU v7x, 512 devices: a whole 4x8x8 slice. The times are simulated.
512 devices in a mesh: scen: 8 (over x, core), bus: 64 (over y, z).
Axes of the slice: x: 4, y: 8, z: 8, core: 2. Of those that a mesh axis runs over, the one named last changes fastest.
Arguments:
- injections: bfloat16 [1024, 16384], P(('scen', 'bus')), may hold values from -6 to 6
- tile_values: bfloat16 [4096, 128, 128], P('bus', 'scen'), may hold values from -0.109375 to 0.109375
- tile_line: int32 [4096], P('bus'), may hold values from 0 to 191, as said below
- tile_bus: int32 [4096], P('bus'), may hold values from 0 to 1
- flow_pred: bfloat16 [1024, 24576], P('scen', 'bus'), may hold values from -6 to 6
- line_limit: int32 [24576], P('bus'), may hold values from 50 to 199
Outputs:
- grad_injections: bfloat16 [1024, 16384], P(('scen', 'bus'))
- flows: float32 [1024, 24576], P('scen', 'bus')
Inputs may be any that keep to these rules, and one draw needn't show every extreme that they name: `tile_line`: tile t is held by bus index t // 64; line block b is owned by bus index b // 3. Of the 64 tiles of one bus index at most 2 have line blocks of one owner, and in every draw some owner gets exactly 2 tiles from every bus index. A pair of line block and bus block may occur in several tiles; their values add.
All inputs are finite; a program needn't handle non-finite values.
Results may differ from a plain program's by a relative error of at most 0.0039.
Values may be sent and summed in bfloat16 or wider, within the bound.
No kernel may reach another device: no remote copies, remote signals or barrier semaphores. Data moves between devices by JAX's collectives and lax.ppermute only.
A program may use at most 64 MiB of HBM per device.

v0:
```python
import jax
import jax.numpy as jnp
from jax import lax
from jax.sharding import PartitionSpec as P


def per_device(injections, tile_values, tile_line, tile_bus, flow_pred, line_limit):
    bus_count = lax.axis_size("bus")
    local_inj = lax.all_to_all(injections, "bus", split_axis=1, concat_axis=0, tiled=True)
    tile_full = lax.all_gather(tile_values, "scen", axis=1, tiled=True)
    tile_count = tile_full.shape[0]
    tile_size = tile_full.shape[1]
    row_count = local_inj.shape[0]
    blocks_here = local_inj.shape[1] // tile_size
    line_blocks = flow_pred.shape[1] // tile_size
    per_owner = tile_count // bus_count
    capacity = per_owner + max(1, tile_count // (2 * bus_count))
    slot_total = bus_count * capacity
    inj_blocks = local_inj.reshape(row_count, blocks_here, tile_size)
    per_tile_inj = jnp.take(inj_blocks, tile_bus, axis=1)
    partial_flows = jnp.einsum(
        "stb,tlb->tsl", per_tile_inj, tile_full, preferred_element_type=jnp.float32
    )
    owner_index = tile_line // line_blocks
    within_owner = tile_line % line_blocks
    owner_hits = (owner_index[:, None] == jnp.arange(bus_count, dtype=jnp.int32)[None, :]).astype(
        jnp.int32
    )
    rank_within = jnp.sum(jnp.cumsum(owner_hits, axis=0) * owner_hits, axis=1) - 1
    slot_index = owner_index * capacity + rank_within
    send_buffer = (
        jnp.zeros((slot_total, row_count, tile_size), jnp.float32).at[slot_index].set(partial_flows)
    )
    slot_label = jnp.full((slot_total,), -1, jnp.int32).at[slot_index].set(within_owner)
    received, received_label = (
        lax.all_to_all(send_buffer, "bus", split_axis=0, concat_axis=0, tiled=True),
        lax.all_to_all(slot_label, "bus", split_axis=0, concat_axis=0, tiled=True),
    )
    select_mask = (
        received_label[None, :] == jnp.arange(line_blocks, dtype=jnp.int32)[:, None]
    ).astype(jnp.float32)
    flow_blocks = jnp.einsum("ms,srl->rml", select_mask, received, precision=lax.Precision.HIGHEST)
    flows = flow_blocks.reshape(row_count, line_blocks * tile_size)
    line_cap = line_limit.astype(jnp.float32) * 0.01
    residual = flows - flow_pred.astype(jnp.float32)
    grad_flow = (
        residual
        + jax.nn.sigmoid(4.0 * (flows - line_cap))
        - jax.nn.sigmoid(4.0 * (-flows - line_cap))
    ).astype(jnp.bfloat16)
    gathered = lax.all_gather(grad_flow, "bus", axis=1, tiled=True)
    gathered_blocks = gathered.reshape(row_count, gathered.shape[1] // tile_size, tile_size)
    per_tile_grad = jnp.take(gathered_blocks, tile_line, axis=1)
    contrib = jnp.einsum(
        "stl,tlb->stb", per_tile_grad, tile_full, preferred_element_type=jnp.float32
    )
    bus_select = (tile_bus[:, None] == jnp.arange(blocks_here, dtype=jnp.int32)[None, :]).astype(
        jnp.float32
    )
    grad_blocks_bus = jnp.einsum(
        "stb,tk->skb", contrib, bus_select, precision=lax.Precision.HIGHEST
    )
    grad_local = grad_blocks_bus.reshape(row_count, blocks_here * tile_size).astype(jnp.bfloat16)
    grad_injections = lax.all_to_all(grad_local, "bus", split_axis=0, concat_axis=1, tiled=True)
    return (grad_injections, flows)


def solution(mesh):
    return jax.shard_map(
        per_device,
        mesh=mesh,
        in_specs=(
            P(("scen", "bus"), None),
            P("bus", "scen", None),
            P("bus"),
            P("bus"),
            P("scen", "bus"),
            P("bus"),
        ),
        out_specs=(P(("scen", "bus"), None), P("scen", "bus")),
        check_vma=False,
    )
```

profile of v0, /device:TPU:6, one launch (start us, length us, event | category | flops | bytes accessed | tf_op | source)
XLA Modules:
  0.0 534.9 jit_solution(14193557377811817124)
XLA Ops:
  7.2 0.7 all-gather.3.cloned.1.call-update
  7.9 16.6 %all-to-all-start = ((bf16[2,64,256]{2,0,1:T(2,128)(2,1)}), bf16[2,64,256]{2,0,1:T(2,128)(2,1)S(1)}, u32[]{:S(2)}, u32[]{:S(2)}) async-start(bf16[2,64,256]{2,0,1:T(2,128)(2,1)} %bitcast.34), calls=%async_computation | async-start | bytes 131072 | tf_op jit(solution)/shard_map/all_to_all | solution.py:9
  26.9 0.8 scatter_custom_fusion.1
  27.6 0.8 all_to_all.37
  28.4 8.4 %all-to-all-done = bf16[2,64,256]{2,0,1:T(2,128)(2,1)S(1)} async-done(((bf16[2,64,256]{2,0,1:T(2,128)(2,1)}), bf16[2,64,256]{2,0,1:T(2,128)(2,1)S(1)}, u32[]{:S(2)}, u32[]{:S(2)}) %all-to-all-start) | async-done | bytes 65568 | tf_op jit(solution)/shard_map/all_to_all | solution.py:9
  36.8 4.6 all-to-all-start.2
  41.4 1.0 gather_fusion
  42.4 4.3 all-gather.3.cloned.1.call-done
  46.7 5.2 fusion.5
  51.9 4.3 broadcast_in_dim.41
  56.1 12.1 %scatter_fusion = f32[128,128,128]{2,1,0:T(8,128)} fusion(f32[128,128,128]{2,1,0:T(8,128)} %broadcast_in_dim.41, s32[64]{0:T(128)S(1)} %compare_select_fusion.1, f32[64,128,128]{2,1,0:T(8,128)} %fusion.5), kind=kCustom, calls=%fused_computation.2 | custom fusion | bytes 12583168 | tf_op jit(solution)/shard_map/scatter | solution.py:32
  68.2 13.7 %all-to-all-start.1 = ((f32[128,128,128]{2,1,0:T(8,128)}), f32[128,128,128]{2,1,0:T(8,128)}, u32[]{:S(2)}, u32[]{:S(2)}) async-start(f32[128,128,128]{2,1,0:T(8,128)} %scatter_fusion), calls=%async_computation.1 | async-start | bytes 16777216 | tf_op jit(solution)/shard_map/all_to_all | solution.py:36
  82.9 0.7 reduce.3
  83.7 245.9 %all-to-all-done.1 = f32[128,128,128]{2,1,0:T(8,128)} async-done(((f32[128,128,128]{2,1,0:T(8,128)}), f32[128,128,128]{2,1,0:T(8,128)}, u32[]{:S(2)}, u32[]{:S(2)}) %all-to-all-start.1) | async-done | bytes 8388640 | tf_op jit(solution)/shard_map/all_to_all | solution.py:36
  329.7 10.4 %fusion.11 = f32[128,3,128]{2,1,0:T(4,128)S(1)} fusion(f32[128,128,128]{2,1,0:T(8,128)} %all-to-all-done.1, s32[128]{0:T(128)S(1)} %eq.49), kind=kOutput, calls=%fused_computation.16 | convolution fusion | flops 75497856 | bytes 8585728 | tf_op jit(solution)/shard_map/ms,srl->rml/dot_general | solution.py:42
  340.2 0.8 subtract_convert_fusion
  341.1 146.2 %all-gather.5.cloned.1.call-done = bf16[128,24576]{0,1:T(8,128)(2,1)} async-done(((bf16[128,384]{0,1:T(8,128)(2,1)}), bf16[128,24576]{0,1:T(8,128)(2,1)}) %all-gather.5.cloned.1.call-update) | async-done | bytes 6291472 | tf_op jit(solution)/shard_map/all_gather | solution.py:51
  487.3 8.7 %copy.31 = bf16[128,192,128]{2,0,1:T(8,128)(2,1)} copy(bf16[128,192,128]{0,2,1:T(8,128)(2,1)} %bitcast.30) | data formatting | bytes 12582912 | tf_op jit(solution)/shard_map/reshape | solution.py:52
  496.0 3.7 gather_fusion.1
  499.7 2.4 convolution_bitcast_fusion
  502.1 3.8 fusion.17
  506.6 8.6 %all-to-all-start.3 = ((bf16[64,2,256]{2,1,0:T(2,128)(2,1)}), bf16[64,2,256]{2,1,0:T(2,128)(2,1)S(1)}, u32[]{:S(2)}, u32[]{:S(2)}) async-start(bf16[64,2,256]{2,1,0:T(2,128)(2,1)} %convert_element_type.30), calls=%async_computation.3 | async-start | bytes 131072 | tf_op jit(solution)/shard_map/all_to_all | solution.py:64
  515.2 0.8 copy.34
  516.0 11.5 %all-to-all-done.3 = bf16[64,2,256]{2,1,0:T(2,128)(2,1)S(1)} async-done(((bf16[64,2,256]{2,1,0:T(2,128)(2,1)}), bf16[64,2,256]{2,1,0:T(2,128)(2,1)S(1)}, u32[]{:S(2)}, u32[]{:S(2)}) %all-to-all-start.3) | async-done | bytes 65568 | tf_op jit(solution)/shard_map/all_to_all | solution.py:64
  (31 shorter events, 4.9 us)
Async XLA Ops:
  7.2 39.5 %all-gather.3.cloned.1.call-start = ((), (), s32[]{:S(2)}) async-start(), calls=%async_computation.4 | async-start | bytes 2359296 | tf_op jit(solution)/shard_map/all_gather | solution.py:10
  7.9 28.9 %all-to-all-start = ((bf16[2,64,256]{2,0,1:T(2,128)(2,1)}), bf16[2,64,256]{2,0,1:T(2,128)(2,1)S(1)}, u32[]{:S(2)}, u32[]{:S(2)}) async-start(bf16[2,64,256]{2,0,1:T(2,128)(2,1)} %bitcast.34), calls=%async_computation | async-start | bytes 131072 | tf_op jit(solution)/shard_map/all_to_all | solution.py:9
  36.8 31.4 %all-to-all-start.2 = ((s32[64,2,1]{1,2,0:T(1,128)}), s32[64,2,1]{1,2,0:T(1,128)S(1)}, u32[]{:S(2)}, u32[]{:S(2)}) async-start(s32[64,2,1]{1,2,0:T(1,128)} %bitcast.4), calls=%async_computation.2 | async-start | bytes 65536 | tf_op jit(solution)/shard_map/all_to_all | solution.py:37
  68.2 14.0 %copy-start = (bf16[128,384]{1,0:T(8,128)(2,1)S(1)}, bf16[128,384]{1,0:T(8,128)(2,1)}, u32[]{:S(2)}) copy-start(bf16[128,384]{1,0:T(8,128)(2,1)} %param.10) | copy-start | bytes 294916
  68.2 14.1 %copy-start.1 = (s32[384]{0:T(512)S(1)}, s32[384]{0:T(512)}, u32[]{:S(2)}) copy-start(s32[384]{0:T(512)} %param.11) | copy-start | bytes 4612
  68.2 261.5 %all-to-all-start.1 = ((f32[128,128,128]{2,1,0:T(8,128)}), f32[128,128,128]{2,1,0:T(8,128)}, u32[]{:S(2)}, u32[]{:S(2)}) async-start(f32[128,128,128]{2,1,0:T(8,128)} %scatter_fusion), calls=%async_computation.1 | async-start | bytes 16777216 | tf_op jit(solution)/shard_map/all_to_all | solution.py:36
  82.0 405.3 %all-gather.5.cloned.1.call-start = ((), (), s32[]{:S(2)}) async-start(), calls=%async_computation.5 | async-start | bytes 6389760 | tf_op jit(solution)/shard_map/all_gather | solution.py:51
  83.7 257.4 %copy-start.3 = (s32[64]{0:T(128)S(1)}, s32[64]{0:T(128)}, u32[]{:S(2)}) copy-start(s32[64]{0:T(128)} %param.8) | copy-start | bytes 772
  499.7 2.4 copy-start.2
  506.6 20.9 %all-to-all-start.3 = ((bf16[64,2,256]{2,1,0:T(2,128)(2,1)}), bf16[64,2,256]{2,1,0:T(2,128)(2,1)S(1)}, u32[]{:S(2)}, u32[]{:S(2)}) async-start(bf16[64,2,256]{2,1,0:T(2,128)(2,1)} %convert_element_type.30), calls=%async_computation.3 | async-start | bytes 131072 | tf_op jit(solution)/shard_map/all_to_all | solution.py:64
Sparse Core Ops, SparseCore 0:
  10.1 36.5 all-gather.2
  341.2 146.0 all-gather.4
where the time goes:
time: 536 us; the launch traced here: 535 us
  waiting for transfers between devices  417 us (78%)
  starting transfers between devices  43.8 us (8%)
  local copies, waits for them, and re-layouts  34.3 us (6%)
  matrix products  21.7 us (4%)
  between operations  14.2 us (3%)
    all_to_all x1, waiting for transfers between devices, per_device(): lax.all_to_all(send_buffer, 'bus', split_axis=0, concat_axis=0, tiled=True)  246 us
    all_gather x1, waiting for transfers between devices, per_device(): gathered = lax.all_gather(grad_flow, 'bus', axis=1, tiled=True)  146 us
    all_to_all x1, starting transfers between devices, per_device(): lax.all_to_all(injections, 'bus', split_axis=1, concat_axis=0, tiled=True)  16.6 us
    all_to_all x1, starting transfers between devices, per_device(): lax.all_to_all(send_buffer, 'bus', split_axis=0, concat_axis=0, tiled=True)  13.7 us
    scatter x1, local copies, waits for them, and re-layouts, per_device(): jnp.zeros((slot_total, row_count, tile_size), jnp.float32).at[slot_index]  12.1 us
    all_to_all x1, waiting for transfers between devices, per_device(): lax.all_to_all(grad_local, 'bus', split_axis=0, concat_axis=1, tiled=True)  11.5 us
  transfers between devices with their start and end apart: 6, of which 5 were waited for; matrix products, arithmetic and copies ran while one was open for 5% of the time, Pallas kernels for 0%

commit v1 on v0

v1 whole, which is shorter than its diff:
```python
import jax
import jax.numpy as jnp
from jax import lax
from jax.experimental import pallas as pl
from jax.experimental.pallas import tpu as pltpu
from jax.sharding import PartitionSpec as P

AXES = ("scen", "bus")
NX = 4
NC = 2
NY = 8
NZ = 8
TILE = 128
LB = 3
BB = 2
CAP = 2
F32 = jnp.float32
BF16 = jnp.bfloat16


def dev(x, c, y, z):
    return ((x % NX) * NC + c) * (NY * NZ) + (y % NY) * NZ + (z % NZ)


def pairs(fn):
    return [
        (dev(x, c, y, z), fn(x, c, y, z))
        for x in range(NX)
        for c in range(NC)
        for y in range(NY)
        for z in range(NZ)
    ]


def ring_groups():
    minor, major = [], []
    for x in range(NX):
        for c in range(NC):
            for q in range(8):
                along_z = [dev(x, c, q, w) for w in range(NZ)]
                along_y = [dev(x, c, w, q) for w in range(NY)]
                minor.append(along_z if c == 0 else along_y)
                major.append(along_y if c == 0 else along_z)
    return minor, major


MINOR, MAJOR = ring_groups()
X_UP = pairs(lambda x, c, y, z: dev(x + 1, c, y, z))
X_DOWN = pairs(lambda x, c, y, z: dev(x - 1, c, y, z))
CORE_SWAP = pairs(lambda x, c, y, z: dev(x, 1 - c, y, z))


def pack_kernel(line_ref, tiles_ref, out_ref, count_ref):
    out_ref[...] = jnp.zeros_like(out_ref)
    owners = count_ref.shape[0]
    for i in range(owners):
        count_ref[i] = 0

    def body(t, carry):
        owner = lax.div(line_ref[t], LB)
        rank = count_ref[owner]
        count_ref[owner] = rank + 1
        out_ref[owner * CAP + rank] = tiles_ref[t]
        return carry

    lax.fori_loop(0, tiles_ref.shape[0], body, 0, unroll=4)


def pack_tiles(tile_line, tile_values, owners):
    rows, lanes = tile_values.shape[1:]
    return pl.pallas_call(
        pack_kernel,
        out_shape=jax.ShapeDtypeStruct((owners * CAP, rows, lanes), tile_values.dtype),
        in_specs=[
            pl.BlockSpec(memory_space=pltpu.SMEM),
            pl.BlockSpec(memory_space=pltpu.VMEM),
        ],
        out_specs=pl.BlockSpec(memory_space=pltpu.VMEM),
        scratch_shapes=[pltpu.SMEM((owners,), jnp.int32)],
        name="pack_tiles",
    )(tile_line, tile_values)


def dot(a, b, dims):
    return lax.dot_general(a, b, (dims, ((), ())), preferred_element_type=F32)


NN = ((1,), (0,))
NT = ((1,), (1,))


def core_kernel(
    label_ref, x_ref, own_ref, other_ref, pred_ref, limit_ref, rowp_ref, colp_ref,
    flows_ref, c_ref, acc_ref, g_ref,
):
    sources = label_ref.shape[0] // CAP

    def tile(j):
        return jnp.concatenate(
            [own_ref[d, j] for d in range(NX)] + [other_ref[d, j] for d in range(NX)], axis=0
        )

    acc_ref[...] = jnp.zeros_like(acc_ref)

    def forward(s, carry):
        for r in range(CAP):
            j = s * CAP + r
            code = label_ref[j]
            line = code >> 1
            bus = code & 1
            start = pl.multiple_of((s * BB + bus) * TILE, TILE)
            part = dot(x_ref[:, pl.ds(start, TILE)], tile(j), NT)
            acc_ref[line] = acc_ref[line] + part
        return carry

    lax.fori_loop(0, sources, forward, 0, unroll=2)

    rowp = rowp_ref[...]
    colp = colp_ref[...]
    for b in range(LB):
        rest = acc_ref[b]
        flow = None
        for k in range(3):
            piece = rest.astype(BF16)
            rest = rest - piece.astype(F32)
            moved = dot(dot(rowp, piece, NN).astype(BF16), colp, NN)
            flow = moved if flow is None else flow + moved
        lanes = slice(b * TILE, (b + 1) * TILE)
        flows_ref[:, lanes] = flow
        cap = limit_ref[:, lanes].astype(F32) * 0.01
        grad = (
            (flow - pred_ref[:, lanes].astype(F32))
            + jax.nn.sigmoid(4.0 * (flow - cap))
            - jax.nn.sigmoid(4.0 * (-flow - cap))
        ).astype(BF16)
        grad = dot(rowp, grad, ((0,), (0,))).astype(BF16)
        g_ref[b] = dot(grad, colp, NT).astype(BF16)

    def backward(s, carry):
        low = jnp.zeros((g_ref.shape[1], TILE), F32)
        high = low
        for r in range(CAP):
            j = s * CAP + r
            code = label_ref[j]
            line = code >> 1
            bus = code & 1
            part = dot(g_ref[line], tile(j), NN)
            low = low + jnp.where(bus == 0, part, 0.0)
            high = high + jnp.where(bus == 1, part, 0.0)
        start = pl.multiple_of(s * BB * TILE, BB * TILE)
        c_ref[:, pl.ds(start, BB * TILE)] = jnp.concatenate([low, high], axis=1).astype(BF16)
        return carry

    lax.fori_loop(0, sources, backward, 0, unroll=2)


def core_call(labels, x, own, other, pred, limit, rowp, colp, nbus):
    rows, lines = pred.shape
    vmem = pl.BlockSpec(memory_space=pltpu.VMEM)
    return pl.pallas_call(
        core_kernel,
        out_shape=(
            jax.ShapeDtypeStruct((rows, lines), F32),
            jax.ShapeDtypeStruct((rows, nbus), BF16),
        ),
        in_specs=[pl.BlockSpec(memory_space=pltpu.SMEM)] + [vmem] * 7,
        out_specs=(vmem, vmem),
        scratch_shapes=[
            pltpu.VMEM((LB, rows, TILE), F32),
            pltpu.VMEM((LB, rows, TILE), BF16),
        ],
        compiler_params=pltpu.CompilerParams(vmem_limit_bytes=32 * 1024 * 1024),
        name="flows_and_grad",
    )(labels, x, own, other, pred, limit, rowp, colp)


def per_device(injections, tile_values, tile_line, tile_bus, flow_pred, line_limit):
    here = lax.axis_index("bus")
    scen = lax.axis_index("scen")
    x_here = scen // NC
    core = scen % NC
    buses = lax.axis_size("bus")
    rows_here, nbus = injections.shape
    count = tile_line.shape[0]

    packed = pack_tiles(tile_line, tile_values, buses)
    mine = lax.all_to_all(
        packed.reshape((buses, CAP) + packed.shape[1:]), "bus", split_axis=0, concat_axis=0, tiled=True
    ).reshape(packed.shape)

    owner = tile_line // LB
    inside = (tile_line % LB) * BB + tile_bus
    codes = jnp.pad(
        jnp.stack([owner, inside]), ((0, 0), (0, TILE - count)), constant_values=255
    ).astype(BF16)
    wide = jnp.concatenate([injections, codes], axis=1)
    near = lax.all_to_all(
        jnp.broadcast_to(wide[None], (8,) + wide.shape),
        AXES, split_axis=0, concat_axis=0, tiled=True, axis_index_groups=MINOR,
    ).reshape(8 * rows_here, wide.shape[1])
    x_all = lax.all_gather(near, AXES, axis=0, tiled=True, axis_index_groups=MAJOR)

    from_below = lax.ppermute(mine, AXES, X_UP)
    from_above = lax.ppermute(mine, AXES, X_DOWN)
    from_far = lax.ppermute(from_below, AXES, X_UP)
    own = jnp.stack([mine, from_above, from_far, from_below])
    other = lax.ppermute(own, AXES, CORE_SWAP)

    tags = x_all[:, nbus:].astype(jnp.int32).reshape(8, 8, rows_here, TILE)
    hit = tags[:, :, 0, :] == here
    inner = tags[:, :, 1, :]
    lane = lax.broadcasted_iota(jnp.int32, hit.shape, 2)
    first = jnp.min(jnp.where(hit, lane, TILE), axis=2, keepdims=True)
    code_first = jnp.sum(jnp.where(lane == first, inner, 0), axis=2)
    code_second = jnp.sum(jnp.where(hit, inner, 0), axis=2) - code_first
    labels = jnp.stack([code_first, code_second], axis=2)
    labels = jnp.where(core == 0, labels, jnp.swapaxes(labels, 0, 1)).reshape(buses * CAP)

    row = lax.broadcasted_iota(jnp.int32, (TILE, TILE), 0)
    col = lax.broadcasted_iota(jnp.int32, (TILE, TILE), 1)
    swapped = ((col // 2) % 8 * 8 + col // 16) * 2 + col % 2
    rowp = (row == jnp.where(core == 0, col, swapped)).astype(BF16)
    chunk = row // 16
    line_of = (((chunk % NX + x_here) % NX) * NC + jnp.where(chunk < NX, core, 1 - core)) * 16 + row % 16
    colp = (col == line_of).astype(BF16)

    flows, contrib = core_call(
        labels, x_all, own, other, flow_pred, line_limit.reshape(1, -1), rowp, colp, nbus
    )

    parts = lax.all_to_all(
        contrib.reshape(8, 8 * rows_here, nbus),
        AXES, split_axis=0, concat_axis=0, tiled=True, axis_index_groups=MAJOR,
    )
    half = jnp.sum(parts.astype(F32), axis=0)
    last = lax.all_to_all(
        half.reshape(8, rows_here, nbus),
        AXES, split_axis=0, concat_axis=0, tiled=True, axis_index_groups=MINOR,
    )
    grad_injections = jnp.sum(last, axis=0).astype(BF16)
    return (grad_injections, flows)


def solution(mesh):
    return jax.shard_map(
        per_device,
        mesh=mesh,
        in_specs=(
            P(("scen", "bus"), None),
            P("bus", "scen", None),
            P("bus"),
            P("bus"),
            P("scen", "bus"),
            P("bus"),
        ),
        out_specs=(P(("scen", "bus"), None), P("scen", "bus")),
        check_vma=False,
    )
```

time: 536 us -> 204 us (0.38)
  waiting for transfers between devices: 417 us -> 18.6 us
  blocking collectives: 0 us -> 131 us
  starting transfers between devices: 43.8 us -> 10.1 us
  local copies, waits for them, and re-layouts: 34.3 us -> 5.27 us
  matrix products: 21.7 us -> 0 us
  Pallas kernels: 0 us -> 18.3 us
    all_to_all x4 -> x0, waiting for transfers between devices: 266 us -> none  [the longest x1 246 us: per_device(): lax.all_to_all(send_buffer, 'bus', split_axis=0, concat_axis=0, tiled=True)]
    all_gather x2 -> x1, waiting for transfers between devices: 150 us -> 0.02 us  [per_device(): lax.all_gather(near, AXES, axis=0, tiled=True, axis_index_groups=MAJOR)]
    all_to_all x0 -> x4, blocking collectives: none -> 131 us  [the longest x1 55.1 us: per_device(): lax.all_to_all(contrib.reshape(8, 8 * rows_here, nbus), AXES, split_axis=...]
    all_to_all x4 -> x0, starting transfers between devices: 43.5 us -> none  [the longest x1 16.6 us: per_device(): lax.all_to_all(injections, 'bus', split_axis=1, concat_axis=0, tiled=True)]
    dot_general x4 -> x0, matrix products: 21.7 us -> none  [the longest x1 10.4 us: per_device(): jnp.einsum('ms,srl->rml', select_mask, received, precision=lax.Precision....]
    ppermute x0 -> x4, waiting for transfers between devices: none -> 18.6 us  [the longest x1 8.78 us: per_device(): from_far = lax.ppermute(from_below, AXES, X_UP)]
    pallas_call x0 -> x2, Pallas kernels: none -> 18.3 us  [the longest x1 16 us: core_call(): pl.pallas_call(core_kernel, out_shape=(jax.ShapeDtypeStruct((rows, lines)...]
    scatter x2 -> x0, local copies, waits for them, and re-layouts: 12.8 us -> none  [the longest x1 12.1 us: per_device(): jnp.zeros((slot_total, row_count, tile_size), jnp.float32).at[slot_index]]
  transfers between devices with their start and end apart: 6 -> 5, of which waited for: 5 -> 3; matrix products, arithmetic and copies ran while one was open for 5% -> 1% of each run, Pallas kernels for 0% -> 1%
where the time goes in v1:
time: 204 us; the launch traced here: 202 us
  blocking collectives  131 us (64%)
  waiting for transfers between devices  18.6 us (9%)
  Pallas kernels  18.3 us (9%)
  between operations  14.2 us (7%)
  starting transfers between devices  10.1 us (5%)
  local copies, waits for them, and re-layouts  5.27 us (3%)
  other arithmetic  4.38 us (2%)
    all_to_all x1, blocking collectives, per_device(): lax.all_to_all(contrib.reshape(8, 8 * rows_here, nbus), AXES, split_axis=...  55.1 us
    all_to_all x1, blocking collectives, per_device(): lax.all_to_all(packed.reshape((buses, CAP) + packed.shape[1:]), 'bus', sp...  28.7 us
    all_to_all x1, blocking collectives, per_device(): lax.all_to_all(jnp.broadcast_to(wide[None], (8,) + wide.shape), AXES, spl...  23.5 us
    all_to_all x1, blocking collectives, per_device(): lax.all_to_all(half.reshape(8, rows_here, nbus), AXES, split_axis=0, conc...  23.4 us
    pallas_call x1, Pallas kernels, core_call(): pl.pallas_call(core_kernel, out_shape=(jax.ShapeDtypeStruct((rows, lines)...  16 us
    ppermute x1, waiting for transfers between devices, per_device(): from_far = lax.ppermute(from_below, AXES, X_UP)  8.78 us
    ppermute x1, waiting for transfers between devices, per_device(): from_below = lax.ppermute(mine, AXES, X_UP)  7.72 us
  transfers between devices with their start and end apart: 5, of which 3 were waited for; matrix products, arithmetic and copies ran while one was open for 1% of the time, Pallas kernels for 1%

profile of v1, /device:TPU:6, one launch (start us, length us, event | category | flops | bytes accessed | tf_op | source)
XLA Modules:
  0.0 201.5 jit_solution(17420436488574567722)
XLA Ops:
  7.2 0.7 convert_bitcast_fusion.1
  7.9 0.9 pad_maximum_fusion.1
  8.8 0.3 broadcast_in_dim.23
  9.1 23.5 %all_to_all.20 = bf16[8,2,16512]{2,1,0:T(2,128)(2,1)S(1)} all-to-all(bf16[8,2,16512]{2,1,0:T(2,128)(2,1)S(1)} %broadcast_in_dim.23), channel_id=1, replica_groups={{0,1,2,3,4,5,6,7},{8,9,10,11,12,13,14,15},{16,17,18,19,20,21,22,23},{24..., dimensions={0} | all-to-all | bytes 1056768 | tf_op jit(solution)/shard_map/all_to_all | solution.py:197
  32.6 1.0 reshape.46
  33.7 2.2 %pack_tiles.1 = bf16[128,16,128]{2,1,0:T(8,128)(2,1)} custom-call(s32[64]{0:T(128)} %line_ref.1, bf16[64,16,128]{2,1,0:T(8,128)(2,1)} %tiles_ref.1), custom_call_target="tpu_custom_call" | custom-call | tf_op jit(solution)/shard_map/pack_tiles/pallas_call | solution.py:71
  35.9 28.7 %all_to_all.21 = bf16[64,2,16,128]{3,2,1,0:T(8,128)(2,1)S(1)} all-to-all(bf16[64,2,16,128]{3,2,1,0:T(8,128)(2,1)} %bitcast.25), channel_id=1, replica_groups=mesh['scen'=8,'bus'=64] {'bus'}, dimensions={0} | all-to-all | bytes 1048576 | tf_op jit(solution)/shard_map/all_to_all | solution.py:187
  64.6 2.4 %collective-permute-start.1 = (bf16[128,16,128]{2,1,0:T(8,128)(2,1)S(1)}, bf16[128,16,128]{2,1,0:T(8,128)(2,1)S(1)}, u32[]{:S(2)}, u32[]{:S(2)}) collective-permute-start(bf16[128,16,128]{2,1,0:T(8,128)(2,1)S(1)} %bitcast.26), channel_id=1, source_target_pairs={{0,128},{1,129},{2,130},{3,131},{4,132},{5,133},{6,134},{7,135},{8... | collective-permute-start | bytes 1572872 | tf_op jit(solution)/shard_map/ppermute | solution.py:203
  67.0 3.5 %collective-permute-start = (bf16[128,16,128]{2,1,0:T(8,128)(2,1)S(1)}, bf16[128,16,128]{2,1,0:T(8,128)(2,1)S(1)}, u32[]{:S(2)}, u32[]{:S(2)}) collective-permute-start(bf16[128,16,128]{2,1,0:T(8,128)(2,1)S(1)} %bitcast.27), channel_id=1, source_target_pairs={{0,384},{1,385},{2,386},{3,387},{4,388},{5,389},{6,390},{7,391},{8... | collective-permute-start | bytes 1572872 | tf_op jit(solution)/shard_map/ppermute | solution.py:204
  70.4 7.7 %collective-permute-done.1 = bf16[128,16,128]{2,1,0:T(8,128)(2,1)S(1)} collective-permute-done((bf16[128,16,128]{2,1,0:T(8,128)(2,1)S(1)}, bf16[128,16,128]{2,1,0:T(8,128)(2,1)S(1)}, u32[]{:S(2)}, u32[]{:S(2)}) %collective-permute-start.1) | collective-permute-done | bytes 524320 | tf_op jit(solution)/shard_map/ppermute | solution.py:203
  78.2 2.3 %collective-permute-start.2 = (bf16[128,16,128]{2,1,0:T(8,128)(2,1)S(1)}, bf16[128,16,128]{2,1,0:T(8,128)(2,1)S(1)}, u32[]{:S(2)}, u32[]{:S(2)}) collective-permute-start(bf16[128,16,128]{2,1,0:T(8,128)(2,1)S(1)} %collective-permute-done.1), channel_id=1, source_target_pairs={{0,128},{1,129},{2,130},{3,131},{4,132},{5,133},{6,134},{7,135},{8... | collective-permute-start | bytes 1572872 | tf_op jit(solution)/shard_map/ppermute | solution.py:205
  80.5 8.8 %collective-permute-done.2 = bf16[128,16,128]{2,1,0:T(8,128)(2,1)S(1)} collective-permute-done((bf16[128,16,128]{2,1,0:T(8,128)(2,1)S(1)}, bf16[128,16,128]{2,1,0:T(8,128)(2,1)S(1)}, u32[]{:S(2)}, u32[]{:S(2)}) %collective-permute-start.2) | collective-permute-done | bytes 524320 | tf_op jit(solution)/shard_map/ppermute | solution.py:205
  89.2 0.3 pad_maximum_fusion.own_ref
  89.5 1.9 collective-permute-start.3
  91.8 0.8 slice.12
  92.8 0.4 select_reduce_fusion.1
  93.6 2.1 %collective-permute-done.3.other_ref = bf16[4,128,16,128]{3,2,1,0:T(8,128)(2,1)} collective-permute-done((bf16[4,128,16,128]{3,2,1,0:T(8,128)(2,1)S(1)}, bf16[4,128,16,128]{3,2,1,0:T(8,128)(2,1)}, u32[]{:S(2)}, u32[]{:S(2)}) %collective-permute-start.3) | collective-permute-done | bytes 2097184 | tf_op jit(solution)/shard_map/ppermute | solution.py:207
  95.7 2.2 %copy-done = bf16[128,16512]{1,0:T(8,128)(2,1)S(1)} copy-done((bf16[128,16512]{1,0:T(8,128)(2,1)S(1)}, bf16[128,16512]{1,0:T(8,128)(2,1)}, u32[]{:S(2)}) %copy-start) | copy-done | bytes 4227096
  97.9 16.0 %flows_and_grad.1 = (f32[128,384]{1,0:T(8,128)}, bf16[128,16384]{1,0:T(8,128)(2,1)S(1)}) custom-call(s32[128]{0:T(128)S(1)} %reshape.49.label_ref, bf16[128,16512]{1,0:T(8,128)(2,1)S(1)} %copy-done, bf16[4,128,16,128]{3,2,1,0:T(8,128)(2,1)S(1)} %pad_maximum_fusion.own_ref, bf16[4,128,16,128]{3,2,1,0:T(8,128)(2,1)} %collective-permute-done.3.other_ref, ...), custom_call_target="tpu_custom_call" | custom-call | tf_op jit(solution)/shard_map/flows_and_grad/pallas_call | solution.py:160
  113.9 55.1 %all_to_all.22 = bf16[8,16,16384]{2,1,0:T(8,128)(2,1)S(1)} all-to-all(bf16[8,16,16384]{2,1,0:T(8,128)(2,1)S(1)} %bitcast.24), channel_id=1, replica_groups={{0,8,16,24,32,40,48,56},{1,9,17,25,33,41,49,57},{2,10,18,26,34,42,50,58..., dimensions={0} | all-to-all | bytes 8388608 | tf_op jit(solution)/shard_map/all_to_all | solution.py:231
  169.0 0.6 convert_reduce_fusion
  169.6 0.6 reshape.54
  170.2 23.4 %all_to_all.23 = f32[8,2,16384]{2,1,0:T(2,128)S(1)} all-to-all(f32[8,2,16384]{2,1,0:T(2,128)S(1)} %reshape.54), channel_id=1, replica_groups={{0,1,2,3,4,5,6,7},{8,9,10,11,12,13,14,15},{16,17,18,19,20,21,22,23},{24..., dimensions={0} | all-to-all | bytes 2097152 | tf_op jit(solution)/shard_map/all_to_all | solution.py:236
  193.6 1.1 reduce_sum.42
  (27 shorter events, 0.9 us)
Async XLA Ops:
  7.2 84.6 %all-gather.2.cloned.1.call-start = ((), (), s32[]{:S(2)}) async-start(), calls=%async_computation.4 | async-start | bytes 4755456 | tf_op jit(solution)/shard_map/all_gather | solution.py:201
  64.6 13.6 %collective-permute-start.1 = (bf16[128,16,128]{2,1,0:T(8,128)(2,1)S(1)}, bf16[128,16,128]{2,1,0:T(8,128)(2,1)S(1)}, u32[]{:S(2)}, u32[]{:S(2)}) collective-permute-start(bf16[128,16,128]{2,1,0:T(8,128)(2,1)S(1)} %bitcast.26), channel_id=1, source_target_pairs={{0,128},{1,129},{2,130},{3,131},{4,132},{5,133},{6,134},{7,135},{8... | collective-permute-start | bytes 1572872 | tf_op jit(solution)/shard_map/ppermute | solution.py:203
  67.0 13.5 %collective-permute-start = (bf16[128,16,128]{2,1,0:T(8,128)(2,1)S(1)}, bf16[128,16,128]{2,1,0:T(8,128)(2,1)S(1)}, u32[]{:S(2)}, u32[]{:S(2)}) collective-permute-start(bf16[128,16,128]{2,1,0:T(8,128)(2,1)S(1)} %bitcast.27), channel_id=1, source_target_pairs={{0,384},{1,385},{2,386},{3,387},{4,388},{5,389},{6,390},{7,391},{8... | collective-permute-start | bytes 1572872 | tf_op jit(solution)/shard_map/ppermute | solution.py:204
  78.2 11.1 %collective-permute-start.2 = (bf16[128,16,128]{2,1,0:T(8,128)(2,1)S(1)}, bf16[128,16,128]{2,1,0:T(8,128)(2,1)S(1)}, u32[]{:S(2)}, u32[]{:S(2)}) collective-permute-start(bf16[128,16,128]{2,1,0:T(8,128)(2,1)S(1)} %collective-permute-done.1), channel_id=1, source_target_pairs={{0,128},{1,129},{2,130},{3,131},{4,132},{5,133},{6,134},{7,135},{8... | collective-permute-start | bytes 1572872 | tf_op jit(solution)/shard_map/ppermute | solution.py:205
  89.2 2.2 %copy-start.2 = (s32[384]{0:T(512)S(1)}, s32[384]{0:T(512)}, u32[]{:S(2)}) copy-start(s32[384]{0:T(512)} %param.11) | copy-start | bytes 4612
  89.2 6.5 %copy-start.1 = (bf16[128,384]{1,0:T(8,128)(2,1)S(1)}, bf16[128,384]{1,0:T(8,128)(2,1)}, u32[]{:S(2)}) copy-start(bf16[128,384]{1,0:T(8,128)(2,1)} %pred_ref.1) | copy-start | bytes 294916
  89.5 6.2 %collective-permute-start.3 = (bf16[4,128,16,128]{3,2,1,0:T(8,128)(2,1)S(1)}, bf16[4,128,16,128]{3,2,1,0:T(8,128)(2,1)}, u32[]{:S(2)}, u32[]{:S(2)}) collective-permute-start(bf16[4,128,16,128]{3,2,1,0:T(8,128)(2,1)S(1)} %pad_maximum_fusion.own_ref), channel_id=1, source_target_pairs={{0,64},{1,65},{2,66},{3,67},{4,68},{5,69},{6,70},{7,71},{8,72},{9,... | collective-permute-start | bytes 6291464 | tf_op jit(solution)/shard_map/ppermute | solution.py:207
  95.7 2.2 %copy-start = (bf16[128,16512]{1,0:T(8,128)(2,1)S(1)}, bf16[128,16512]{1,0:T(8,128)(2,1)}, u32[]{:S(2)}) copy-start(bf16[128,16512]{1,0:T(8,128)(2,1)} %all-gather.2.cloned.1.call-done.x_ref) | copy-start | bytes 12681220
Sparse Core Ops, SparseCore 0:
  33.8 49.2 all-gather.1

commit v2 on v1

--- a/solution.py
+++ b/solution.py
@@ -191,13 +191,17 @@
     owner = tile_line // LB
     inside = (tile_line % LB) * BB + tile_bus
     codes = jnp.pad(
-        jnp.stack([owner, inside]), ((0, 0), (0, TILE - count)), constant_values=255
+        jnp.stack([owner, inside]),
+        ((0, nbus * rows_here // TILE - 2), (0, TILE - count)),
+        constant_values=255,
     ).astype(BF16)
-    wide = jnp.concatenate([injections, codes], axis=1)
-    near = lax.all_to_all(
-        jnp.broadcast_to(wide[None], (8,) + wide.shape),
-        AXES, split_axis=0, concat_axis=0, tiled=True, axis_index_groups=MINOR,
-    ).reshape(8 * rows_here, wide.shape[1])
+    blocks = nbus // TILE
+    flat = injections.reshape(rows_here, blocks, TILE).swapaxes(0, 1).reshape(rows_here * blocks, TILE)
+    wide = jnp.concatenate([flat, codes], axis=0)
+    near = lax.all_gather(wide, AXES, axis=0, tiled=False, axis_index_groups=MINOR)
+    near_x = near[:, : rows_here * blocks].reshape(8, blocks, rows_here, TILE).swapaxes(1, 2)
+    near_code = near[:, rows_here * blocks : rows_here * blocks + 2].reshape(8 * 2, TILE)
+    near = jnp.concatenate([near_x.reshape(8 * rows_here, nbus), near_code], axis=1)
     x_all = lax.all_gather(near, AXES, axis=0, tiled=True, axis_index_groups=MAJOR)
 
     from_below = lax.ppermute(mine, AXES, X_UP)

time: 204 us -> 231 us (1.13)
  waiting for transfers between devices: 18.6 us -> 68.7 us
  blocking collectives: 131 us -> 106 us
    all_gather x0 -> x1, waiting for transfers between devices: none -> 47.4 us  [per_device(): lax.all_gather(wide, AXES, axis=0, tiled=False, axis_index_groups=MINOR)]
    all_to_all x1 -> x0, blocking collectives: 23.5 us -> none  [per_device(): lax.all_to_all(jnp.broadcast_to(wide[None], (8,) + wide.shape), AXES, spl...]
    ppermute x1, waiting for transfers between devices: 7.72 us -> 10.4 us  [per_device(): from_below = lax.ppermute(mine, AXES, X_UP)]
  transfers between devices with their start and end apart: 5 -> 6, of which waited for: 3 -> 4; matrix products, arithmetic and copies ran while one was open for 1% -> 1% of each run, Pallas kernels for 1% -> 1%
where the time goes in v2:
time: 231 us; the launch traced here: 229 us
  blocking collectives  106 us (46%)
  waiting for transfers between devices  68.7 us (30%)
  Pallas kernels  18.3 us (8%)
  between operations  14.3 us (6%)
  starting transfers between devices  10.2 us (4%)
  local copies, waits for them, and re-layouts  6.22 us (3%)
  other arithmetic  5.82 us (3%)
    all_to_all x1, blocking collectives, per_device(): lax.all_to_all(contrib.reshape(8, 8 * rows_here, nbus), AXES, split_axis=...  56.2 us
    all_gather x1, waiting for transfers between devices, per_device(): lax.all_gather(wide, AXES, axis=0, tiled=False, axis_index_groups=MINOR)  47.4 us
    all_to_all x1, blocking collectives, per_device(): lax.all_to_all(packed.reshape((buses, CAP) + packed.shape[1:]), 'bus', sp...  27.7 us
    all_to_all x1, blocking collectives, per_device(): lax.all_to_all(half.reshape(8, rows_here, nbus), AXES, split_axis=0, conc...  21.9 us
    pallas_call x1, Pallas kernels, core_call(): pl.pallas_call(core_kernel, out_shape=(jax.ShapeDtypeStruct((rows, lines)...  16.1 us
    ppermute x1, waiting for transfers between devices, per_device(): from_below = lax.ppermute(mine, AXES, X_UP)  10.4 us
    ppermute x1, waiting for transfers between devices, per_device(): from_far = lax.ppermute(from_below, AXES, X_UP)  8.66 us
  transfers between devices with their start and end apart: 6, of which 4 were waited for; matrix products, arithmetic and copies ran while one was open for 1% of the time, Pallas kernels for 1%

profile of v2, /device:TPU:6, one launch (start us, length us, event | category | flops | bytes accessed | tf_op | source)
XLA Modules:
  0.0 229.3 jit_solution(192898951797118323)
XLA Ops:
  7.2 0.7 convert_bitcast_fusion.1
  7.9 1.5 pad_maximum_fusion.2
  9.5 47.4 %all-gather.6.cloned.1.call-done = bf16[4096,128]{1,0:T(8,128)(2,1)} async-done(((bf16[512,128]{1,0:T(8,128)(2,1)}), bf16[4096,128]{1,0:T(8,128)(2,1)}) %all-gather.6.cloned.1.call-update) | async-done | bytes 1048592 | tf_op jit(solution)/shard_map/all_gather | solution.py:201
  56.9 0.7 slice.21
  57.6 1.1 slice.20
  59.2 0.8 pad_maximum_fusion.1
  60.0 2.2 pack_tiles.1
  62.3 27.7 %all_to_all.15 = bf16[64,2,16,128]{3,2,1,0:T(8,128)(2,1)S(1)} all-to-all(bf16[64,2,16,128]{3,2,1,0:T(8,128)(2,1)} %bitcast.42), channel_id=1, replica_groups=mesh['scen'=8,'bus'=64] {'bus'}, dimensions={0} | all-to-all | bytes 1048576 | tf_op jit(solution)/shard_map/all_to_all | solution.py:187
  90.0 2.5 %collective-permute-start.1 = (bf16[128,16,128]{2,1,0:T(8,128)(2,1)S(1)}, bf16[128,16,128]{2,1,0:T(8,128)(2,1)S(1)}, u32[]{:S(2)}, u32[]{:S(2)}) collective-permute-start(bf16[128,16,128]{2,1,0:T(8,128)(2,1)S(1)} %bitcast.43), channel_id=1, source_target_pairs={{0,128},{1,129},{2,130},{3,131},{4,132},{5,133},{6,134},{7,135},{8... | collective-permute-start | bytes 1572872 | tf_op jit(solution)/shard_map/ppermute | solution.py:207
  92.5 3.4 %collective-permute-start = (bf16[128,16,128]{2,1,0:T(8,128)(2,1)S(1)}, bf16[128,16,128]{2,1,0:T(8,128)(2,1)S(1)}, u32[]{:S(2)}, u32[]{:S(2)}) collective-permute-start(bf16[128,16,128]{2,1,0:T(8,128)(2,1)S(1)} %bitcast.44), channel_id=1, source_target_pairs={{0,384},{1,385},{2,386},{3,387},{4,388},{5,389},{6,390},{7,391},{8... | collective-permute-start | bytes 1572872 | tf_op jit(solution)/shard_map/ppermute | solution.py:208
  95.8 10.4 %collective-permute-done.1 = bf16[128,16,128]{2,1,0:T(8,128)(2,1)S(1)} collective-permute-done((bf16[128,16,128]{2,1,0:T(8,128)(2,1)S(1)}, bf16[128,16,128]{2,1,0:T(8,128)(2,1)S(1)}, u32[]{:S(2)}, u32[]{:S(2)}) %collective-permute-start.1) | collective-permute-done | bytes 524320 | tf_op jit(solution)/shard_map/ppermute | solution.py:207
  106.3 2.4 %collective-permute-start.2 = (bf16[128,16,128]{2,1,0:T(8,128)(2,1)S(1)}, bf16[128,16,128]{2,1,0:T(8,128)(2,1)S(1)}, u32[]{:S(2)}, u32[]{:S(2)}) collective-permute-start(bf16[128,16,128]{2,1,0:T(8,128)(2,1)S(1)} %collective-permute-done.1), channel_id=1, source_target_pairs={{0,128},{1,129},{2,130},{3,131},{4,132},{5,133},{6,134},{7,135},{8... | collective-permute-start | bytes 1572872 | tf_op jit(solution)/shard_map/ppermute | solution.py:209
  108.7 8.7 %collective-permute-done.2 = bf16[128,16,128]{2,1,0:T(8,128)(2,1)S(1)} collective-permute-done((bf16[128,16,128]{2,1,0:T(8,128)(2,1)S(1)}, bf16[128,16,128]{2,1,0:T(8,128)(2,1)S(1)}, u32[]{:S(2)}, u32[]{:S(2)}) %collective-permute-start.2) | collective-permute-done | bytes 524320 | tf_op jit(solution)/shard_map/ppermute | solution.py:209
  117.6 1.9 collective-permute-start.3
  119.9 0.8 slice.22
  121.0 0.4 select_reduce_fusion.1
  121.7 2.1 collective-permute-done.3.other_ref
  123.8 2.2 copy-done
  126.0 16.1 %flows_and_grad.1 = (f32[128,384]{1,0:T(8,128)}, bf16[128,16384]{1,0:T(8,128)(2,1)S(1)}) custom-call(s32[128]{0:T(128)S(1)} %reshape.64.label_ref, bf16[128,16512]{1,0:T(8,128)(2,1)S(1)} %copy-done, bf16[4,128,16,128]{3,2,1,0:T(8,128)(2,1)S(1)} %pad_maximum_fusion.own_ref, bf16[4,128,16,128]{3,2,1,0:T(8,128)(2,1)} %collective-permute-done.3.other_ref, ...), custom_call_target="tpu_custom_call" | custom-call | tf_op jit(solution)/shard_map/flows_and_grad/pallas_call | solution.py:160
  142.1 56.2 %all_to_all.16 = bf16[8,16,16384]{2,1,0:T(8,128)(2,1)S(1)} all-to-all(bf16[8,16,16384]{2,1,0:T(8,128)(2,1)S(1)} %bitcast.38), channel_id=1, replica_groups={{0,8,16,24,32,40,48,56},{1,9,17,25,33,41,49,57},{2,10,18,26,34,42,50,58..., dimensions={0} | all-to-all | bytes 8388608 | tf_op jit(solution)/shard_map/all_to_all | solution.py:235
  198.3 0.6 convert_reduce_fusion
  198.9 0.6 reshape.69
  199.5 21.9 %all_to_all.17 = f32[8,2,16384]{2,1,0:T(2,128)S(1)} all-to-all(f32[8,2,16384]{2,1,0:T(2,128)S(1)} %reshape.69), channel_id=1, replica_groups={{0,1,2,3,4,5,6,7},{8,9,10,11,12,13,14,15},{16,17,18,19,20,21,22,23},{24..., dimensions={0} | all-to-all | bytes 2097152 | tf_op jit(solution)/shard_map/all_to_all | solution.py:240
  221.4 1.1 reduce_sum.42
  (32 shorter events, 1.7 us)
Async XLA Ops:
  7.2 49.8 %all-gather.6.cloned.1.call-start = ((), (), s32[]{:S(2)}) async-start(), calls=%async_computation.4 | async-start | bytes 1179648 | tf_op jit(solution)/shard_map/all_gather | solution.py:201
  9.4 110.4 %all-gather.4.cloned.1.call-start = ((), (), s32[]{:S(2)}) async-start(), calls=%async_computation.3 | async-start | bytes 4755456 | tf_op jit(solution)/shard_map/all_gather | solution.py:205
  90.0 16.3 %collective-permute-start.1 = (bf16[128,16,128]{2,1,0:T(8,128)(2,1)S(1)}, bf16[128,16,128]{2,1,0:T(8,128)(2,1)S(1)}, u32[]{:S(2)}, u32[]{:S(2)}) collective-permute-start(bf16[128,16,128]{2,1,0:T(8,128)(2,1)S(1)} %bitcast.43), channel_id=1, source_target_pairs={{0,128},{1,129},{2,130},{3,131},{4,132},{5,133},{6,134},{7,135},{8... | collective-permute-start | bytes 1572872 | tf_op jit(solution)/shard_map/ppermute | solution.py:207
  92.5 16.2 %collective-permute-start = (bf16[128,16,128]{2,1,0:T(8,128)(2,1)S(1)}, bf16[128,16,128]{2,1,0:T(8,128)(2,1)S(1)}, u32[]{:S(2)}, u32[]{:S(2)}) collective-permute-start(bf16[128,16,128]{2,1,0:T(8,128)(2,1)S(1)} %bitcast.44), channel_id=1, source_target_pairs={{0,384},{1,385},{2,386},{3,387},{4,388},{5,389},{6,390},{7,391},{8... | collective-permute-start | bytes 1572872 | tf_op jit(solution)/shard_map/ppermute | solution.py:208
  106.3 11.1 %collective-permute-start.2 = (bf16[128,16,128]{2,1,0:T(8,128)(2,1)S(1)}, bf16[128,16,128]{2,1,0:T(8,128)(2,1)S(1)}, u32[]{:S(2)}, u32[]{:S(2)}) collective-permute-start(bf16[128,16,128]{2,1,0:T(8,128)(2,1)S(1)} %collective-permute-done.1), channel_id=1, source_target_pairs={{0,128},{1,129},{2,130},{3,131},{4,132},{5,133},{6,134},{7,135},{8... | collective-permute-start | bytes 1572872 | tf_op jit(solution)/shard_map/ppermute | solution.py:209
  117.3 2.2 copy-start.2
  117.3 6.5 %copy-start.1 = (bf16[128,384]{1,0:T(8,128)(2,1)S(1)}, bf16[128,384]{1,0:T(8,128)(2,1)}, u32[]{:S(2)}) copy-start(bf16[128,384]{1,0:T(8,128)(2,1)} %pred_ref.1) | copy-start | bytes 294916
  117.6 6.2 %collective-permute-start.3 = (bf16[4,128,16,128]{3,2,1,0:T(8,128)(2,1)S(1)}, bf16[4,128,16,128]{3,2,1,0:T(8,128)(2,1)}, u32[]{:S(2)}, u32[]{:S(2)}) collective-permute-start(bf16[4,128,16,128]{3,2,1,0:T(8,128)(2,1)S(1)} %pad_maximum_fusion.own_ref), channel_id=1, source_target_pairs={{0,64},{1,65},{2,66},{3,67},{4,68},{5,69},{6,70},{7,71},{8,72},{9,... | collective-permute-start | bytes 6291464 | tf_op jit(solution)/shard_map/ppermute | solution.py:211
  123.8 2.2 copy-start
Sparse Core Ops, SparseCore 0:
  10.7 46.2 all-gather.5
  60.2 47.5 all-gather.3

commit v3 on v2

--- a/solution.py
+++ b/solution.py
@@ -50,35 +50,46 @@
 CORE_SWAP = pairs(lambda x, c, y, z: dev(x, 1 - c, y, z))
 
 
-def pack_kernel(line_ref, tiles_ref, out_ref, count_ref):
-    out_ref[...] = jnp.zeros_like(out_ref)
-    owners = count_ref.shape[0]
-    for i in range(owners):
+def pack_kernel(core_ref, line_ref, tiles_ref, x_ref, code_ref, out_ref, count_ref):
+    x_rows = x_ref.shape[0]
+    head = x_rows + code_ref.shape[0]
+    for m in range(out_ref.shape[0]):
+        out_ref[m, :x_rows] = x_ref[...]
+        out_ref[m, x_rows:head] = code_ref[...]
+        out_ref[m, head:] = jnp.zeros((out_ref.shape[1] - head, TILE), out_ref.dtype)
+    for i in range(count_ref.shape[0]):
         count_ref[i] = 0
+    rows = tiles_ref.shape[1]
+    first_core = core_ref[0] == 0
 
     def body(t, carry):
         owner = lax.div(line_ref[t], LB)
         rank = count_ref[owner]
         count_ref[owner] = rank + 1
-        out_ref[owner * CAP + rank] = tiles_ref[t]
+        y = owner >> 3
+        z = owner & 7
+        minor = jnp.where(first_core, z, y)
+        major = jnp.where(first_core, y, z)
+        at = pl.multiple_of(head + (major * CAP + rank) * rows, rows)
+        out_ref[minor, pl.ds(at, rows)] = tiles_ref[t]
         return carry
 
     lax.fori_loop(0, tiles_ref.shape[0], body, 0, unroll=4)
 
 
-def pack_tiles(tile_line, tile_values, owners):
-    rows, lanes = tile_values.shape[1:]
+def pack(core, tile_line, tile_values, x, codes, owners):
+    rows = tile_values.shape[1]
+    total = x.shape[0] + codes.shape[0] + 8 * CAP * rows
+    smem = pl.BlockSpec(memory_space=pltpu.SMEM)
+    vmem = pl.BlockSpec(memory_space=pltpu.VMEM)
     return pl.pallas_call(
         pack_kernel,
-        out_shape=jax.ShapeDtypeStruct((owners * CAP, rows, lanes), tile_values.dtype),
-        in_specs=[
-            pl.BlockSpec(memory_space=pltpu.SMEM),
-            pl.BlockSpec(memory_space=pltpu.VMEM),
-        ],
-        out_specs=pl.BlockSpec(memory_space=pltpu.VMEM),
+        out_shape=jax.ShapeDtypeStruct((8, total, TILE), BF16),
+        in_specs=[smem, smem, vmem, vmem, vmem],
+        out_specs=vmem,
         scratch_shapes=[pltpu.SMEM((owners,), jnp.int32)],
-        name="pack_tiles",
-    )(tile_line, tile_values)
+        name="pack",
+    )(core.reshape(1), tile_line, tile_values, x, codes)
 
 
 def dot(a, b, dims):
@@ -95,9 +106,11 @@
 ):
     sources = label_ref.shape[0] // CAP
 
-    def tile(j):
+    def tile(s, r):
+        here = s * CAP + r
+        there = ((s & 7) * 8 + (s >> 3)) * CAP + r
         return jnp.concatenate(
-            [own_ref[d, j] for d in range(NX)] + [other_ref[d, j] for d in range(NX)], axis=0
+            [own_ref[d, here] for d in range(NX)] + [other_ref[d, there] for d in range(NX)], axis=0
         )
 
     acc_ref[...] = jnp.zeros_like(acc_ref)
@@ -106,10 +119,9 @@
         for r in range(CAP):
             j = s * CAP + r
             code = label_ref[j]
-            line = code >> 1
-            bus = code & 1
-            start = pl.multiple_of((s * BB + bus) * TILE, TILE)
-            part = dot(x_ref[:, pl.ds(start, TILE)], tile(j), NT)
+            line = code & 3
+            start = pl.multiple_of((code >> 2) * TILE, TILE)
+            part = dot(x_ref[:, pl.ds(start, TILE)], tile(s, r), NT)
             acc_ref[line] = acc_ref[line] + part
         return carry
 
@@ -142,12 +154,12 @@
         for r in range(CAP):
             j = s * CAP + r
             code = label_ref[j]
-            line = code >> 1
-            bus = code & 1
-            part = dot(g_ref[line], tile(j), NN)
+            line = code & 3
+            bus = (code >> 2) & 1
+            part = dot(g_ref[line], tile(s, r), NN)
             low = low + jnp.where(bus == 0, part, 0.0)
             high = high + jnp.where(bus == 1, part, 0.0)
-        start = pl.multiple_of(s * BB * TILE, BB * TILE)
+        start = pl.multiple_of((label_ref[s * CAP] >> 3) * (BB * TILE), BB * TILE)
         c_ref[:, pl.ds(start, BB * TILE)] = jnp.concatenate([low, high], axis=1).astype(BF16)
         return carry
 
@@ -183,42 +195,44 @@
     rows_here, nbus = injections.shape
     count = tile_line.shape[0]
 
-    packed = pack_tiles(tile_line, tile_values, buses)
-    mine = lax.all_to_all(
-        packed.reshape((buses, CAP) + packed.shape[1:]), "bus", split_axis=0, concat_axis=0, tiled=True
-    ).reshape(packed.shape)
-
     owner = tile_line // LB
     inside = (tile_line % LB) * BB + tile_bus
     codes = jnp.pad(
-        jnp.stack([owner, inside]),
-        ((0, nbus * rows_here // TILE - 2), (0, TILE - count)),
-        constant_values=255,
+        jnp.stack([owner, inside]), ((0, 14), (0, TILE - count)), constant_values=255
     ).astype(BF16)
     blocks = nbus // TILE
-    flat = injections.reshape(rows_here, blocks, TILE).swapaxes(0, 1).reshape(rows_here * blocks, TILE)
-    wide = jnp.concatenate([flat, codes], axis=0)
-    near = lax.all_gather(wide, AXES, axis=0, tiled=False, axis_index_groups=MINOR)
-    near_x = near[:, : rows_here * blocks].reshape(8, blocks, rows_here, TILE).swapaxes(1, 2)
-    near_code = near[:, rows_here * blocks : rows_here * blocks + 2].reshape(8 * 2, TILE)
+    x_rows = rows_here * blocks
+    flat = injections.reshape(rows_here, blocks, TILE).swapaxes(0, 1).reshape(x_rows, TILE)
+    packed = pack(core, tile_line, tile_values, flat, codes, buses)
+    hop = lax.all_to_all(
+        packed, AXES, split_axis=0, concat_axis=0, tiled=True, axis_index_groups=MINOR
+    )
+    near_x = hop[:, :x_rows].reshape(8, blocks, rows_here, TILE).swapaxes(1, 2)
+    near_code = hop[:, x_rows : x_rows + rows_here].reshape(8 * rows_here, TILE)
     near = jnp.concatenate([near_x.reshape(8 * rows_here, nbus), near_code], axis=1)
     x_all = lax.all_gather(near, AXES, axis=0, tiled=True, axis_index_groups=MAJOR)
 
+    slots = hop[:, x_rows + codes.shape[0] :].reshape((8, 8, CAP) + tile_values.shape[1:])
+    mine = lax.all_to_all(
+        slots.swapaxes(0, 1), AXES, split_axis=0, concat_axis=0, tiled=True, axis_index_groups=MAJOR
+    ).reshape((buses * CAP,) + tile_values.shape[1:])
     from_below = lax.ppermute(mine, AXES, X_UP)
     from_above = lax.ppermute(mine, AXES, X_DOWN)
     from_far = lax.ppermute(from_below, AXES, X_UP)
     own = jnp.stack([mine, from_above, from_far, from_below])
     other = lax.ppermute(own, AXES, CORE_SWAP)
 
-    tags = x_all[:, nbus:].astype(jnp.int32).reshape(8, 8, rows_here, TILE)
-    hit = tags[:, :, 0, :] == here
-    inner = tags[:, :, 1, :]
-    lane = lax.broadcasted_iota(jnp.int32, hit.shape, 2)
-    first = jnp.min(jnp.where(hit, lane, TILE), axis=2, keepdims=True)
-    code_first = jnp.sum(jnp.where(lane == first, inner, 0), axis=2)
-    code_second = jnp.sum(jnp.where(hit, inner, 0), axis=2) - code_first
-    labels = jnp.stack([code_first, code_second], axis=2)
-    labels = jnp.where(core == 0, labels, jnp.swapaxes(labels, 0, 1)).reshape(buses * CAP)
+    tags = x_all[:, nbus:].astype(jnp.int32).reshape(buses, rows_here, TILE)
+    hit = tags[:, 0, :] == here
+    inner = tags[:, 1, :]
+    lane = lax.broadcasted_iota(jnp.int32, hit.shape, 1)
+    first = jnp.min(jnp.where(hit, lane, TILE), axis=1, keepdims=True)
+    code_first = jnp.sum(jnp.where(lane == first, inner, 0), axis=1, keepdims=True)
+    code_second = jnp.sum(jnp.where(hit, inner, 0), axis=1, keepdims=True) - code_first
+    inner = jnp.concatenate([code_first, code_second], axis=1)
+    order = lax.broadcasted_iota(jnp.int32, inner.shape, 0)
+    source = jnp.where(core == 0, order, (order & 7) * 8 + (order >> 3))
+    labels = (((source * BB + (inner & 1)) << 2) + (inner >> 1)).reshape(buses * CAP)
 
     row = lax.broadcasted_iota(jnp.int32, (TILE, TILE), 0)
     col = lax.broadcasted_iota(jnp.int32, (TILE, TILE), 1)
@@ -236,12 +250,12 @@
         contrib.reshape(8, 8 * rows_here, nbus),
         AXES, split_axis=0, concat_axis=0, tiled=True, axis_index_groups=MAJOR,
     )
-    half = jnp.sum(parts.astype(F32), axis=0)
+    half = jnp.sum(parts.astype(F32), axis=0).astype(BF16)
     last = lax.all_to_all(
         half.reshape(8, rows_here, nbus),
         AXES, split_axis=0, concat_axis=0, tiled=True, axis_index_groups=MINOR,
     )
-    grad_injections = jnp.sum(last, axis=0).astype(BF16)
+    grad_injections = jnp.sum(last.astype(F32), axis=0).astype(BF16)
     return (grad_injections, flows)
 
 

time: 231 us -> 198 us (0.86)
  waiting for transfers between devices: 68.7 us -> 17.2 us
  blocking collectives: 106 us -> 123 us
    all_gather x1 -> x0, waiting for transfers between devices: 47.4 us -> none  [per_device(): lax.all_gather(wide, AXES, axis=0, tiled=False, axis_index_groups=MINOR)]
    all_to_all x1 -> x2, blocking collectives: 27.7 us -> 51.6 us  [the longest x1 29.6 us: per_device(): lax.all_to_all(packed, AXES, split_axis=0, concat_axis=0, tiled=True, axi...]
    all_to_all x1, blocking collectives: 21.9 us -> 15.7 us  [per_device(): lax.all_to_all(half.reshape(8, rows_here, nbus), AXES, split_axis=0, conc...]
    ppermute x1, waiting for transfers between devices: 10.4 us -> 6.25 us  [per_device(): from_below = lax.ppermute(mine, AXES, X_UP)]
  transfers between devices with their start and end apart: 6 -> 5, of which waited for: 4 -> 3; matrix products, arithmetic and copies ran while one was open for 1% -> 1% of each run, Pallas kernels for 1% -> 0%
where the time goes in v3:
time: 198 us; the launch traced here: 196 us
  blocking collectives  123 us (62%)
  Pallas kernels  19.5 us (10%)
  waiting for transfers between devices  17.2 us (9%)
  between operations  14.3 us (7%)
  starting transfers between devices  10.4 us (5%)
  other arithmetic  7.08 us (4%)
  local copies, waits for them, and re-layouts  4.18 us (2%)
    all_to_all x1, blocking collectives, per_device(): lax.all_to_all(contrib.reshape(8, 8 * rows_here, nbus), AXES, split_axis=...  55.9 us
    all_to_all x1, blocking collectives, per_device(): lax.all_to_all(packed, AXES, split_axis=0, concat_axis=0, tiled=True, axi...  29.6 us
    all_to_all x1, blocking collectives, per_device(): lax.all_to_all(slots.swapaxes(0, 1), AXES, split_axis=0, concat_axis=0, t...  22 us
    pallas_call x1, Pallas kernels, core_call(): pl.pallas_call(core_kernel, out_shape=(jax.ShapeDtypeStruct((rows, lines)...  16.9 us
    all_to_all x1, blocking collectives, per_device(): lax.all_to_all(half.reshape(8, rows_here, nbus), AXES, split_axis=0, conc...  15.7 us
    ppermute x1, waiting for transfers between devices, per_device(): from_far = lax.ppermute(from_below, AXES, X_UP)  8.42 us
    ppermute x1, waiting for transfers between devices, per_device(): from_below = lax.ppermute(mine, AXES, X_UP)  6.25 us
  transfers between devices with their start and end apart: 5, of which 3 were waited for; matrix products, arithmetic and copies ran while one was open for 1% of the time, Pallas kernels for 0%

profile of v3, /device:TPU:6, one launch (start us, length us, event | category | flops | bytes accessed | tf_op | source)
XLA Modules:
  0.0 195.8 jit_solution(9032796281820912211)
XLA Ops:
  7.2 0.7 convert_bitcast_fusion.1
  7.9 0.6 fusion.22.code_ref
  8.5 2.6 %pack.1 = bf16[8,528,128]{2,1,0:T(8,128)(2,1)} custom-call(s32[1]{0:T(128)} %bitcast.core_ref, s32[64]{0:T(128)} %line_ref.1, bf16[64,16,128]{2,1,0:T(8,128)(2,1)} %tiles_ref.1, bf16[256,128]{1,0:T(8,128)(2,1)} %bitcast.54, bf16[16,128]{1,0:T(8,128)(2,1)} %fusion.22.code_ref), custom_call_target="tpu_custom_call" | custom-call | tf_op jit(solution)/shard_map/pack/pallas_call | solution.py:85
  11.2 29.6 %all_to_all.20 = bf16[8,528,128]{2,1,0:T(8,128)(2,1)S(1)} all-to-all(bf16[8,528,128]{2,1,0:T(8,128)(2,1)} %pack.1), channel_id=1, replica_groups={{0,1,2,3,4,5,6,7},{8,9,10,11,12,13,14,15},{16,17,18,19,20,21,22,23},{24..., dimensions={0} | all-to-all | bytes 2162688 | tf_op jit(solution)/shard_map/all_to_all | solution.py:207
  40.9 0.3 copy.34
  41.3 0.9 pad_maximum_fusion.1
  42.2 22.0 %all_to_all.21 = bf16[8,8,2,16,128]{4,3,2,1,0:T(8,128)(2,1)S(1)} all-to-all(bf16[8,8,2,16,128]{4,3,2,1,0:T(8,128)(2,1)S(1)} %bitcast.42), channel_id=1, replica_groups={{0,8,16,24,32,40,48,56},{1,9,17,25,33,41,49,57},{2,10,18,26,34,42,50,58..., dimensions={0} | all-to-all | bytes 1048576 | tf_op jit(solution)/shard_map/all_to_all | solution.py:216
  64.2 2.4 %collective-permute-start.1 = (bf16[128,16,128]{2,1,0:T(8,128)(2,1)S(1)}, bf16[128,16,128]{2,1,0:T(8,128)(2,1)S(1)}, u32[]{:S(2)}, u32[]{:S(2)}) collective-permute-start(bf16[128,16,128]{2,1,0:T(8,128)(2,1)S(1)} %bitcast.45), channel_id=1, source_target_pairs={{0,128},{1,129},{2,130},{3,131},{4,132},{5,133},{6,134},{7,135},{8... | collective-permute-start | bytes 1572872 | tf_op jit(solution)/shard_map/ppermute | solution.py:219
  66.6 3.5 %collective-permute-start = (bf16[128,16,128]{2,1,0:T(8,128)(2,1)S(1)}, bf16[128,16,128]{2,1,0:T(8,128)(2,1)S(1)}, u32[]{:S(2)}, u32[]{:S(2)}) collective-permute-start(bf16[128,16,128]{2,1,0:T(8,128)(2,1)S(1)} %bitcast.46), channel_id=1, source_target_pairs={{0,384},{1,385},{2,386},{3,387},{4,388},{5,389},{6,390},{7,391},{8... | collective-permute-start | bytes 1572872 | tf_op jit(solution)/shard_map/ppermute | solution.py:220
  70.1 6.2 %collective-permute-done.1 = bf16[128,16,128]{2,1,0:T(8,128)(2,1)S(1)} collective-permute-done((bf16[128,16,128]{2,1,0:T(8,128)(2,1)S(1)}, bf16[128,16,128]{2,1,0:T(8,128)(2,1)S(1)}, u32[]{:S(2)}, u32[]{:S(2)}) %collective-permute-start.1) | collective-permute-done | bytes 524320 | tf_op jit(solution)/shard_map/ppermute | solution.py:219
  76.3 2.6 %collective-permute-start.2 = (bf16[128,16,128]{2,1,0:T(8,128)(2,1)S(1)}, bf16[128,16,128]{2,1,0:T(8,128)(2,1)S(1)}, u32[]{:S(2)}, u32[]{:S(2)}) collective-permute-start(bf16[128,16,128]{2,1,0:T(8,128)(2,1)S(1)} %collective-permute-done.1), channel_id=1, source_target_pairs={{0,128},{1,129},{2,130},{3,131},{4,132},{5,133},{6,134},{7,135},{8... | collective-permute-start | bytes 1572872 | tf_op jit(solution)/shard_map/ppermute | solution.py:221
  79.0 8.4 %collective-permute-done.2 = bf16[128,16,128]{2,1,0:T(8,128)(2,1)S(1)} collective-permute-done((bf16[128,16,128]{2,1,0:T(8,128)(2,1)S(1)}, bf16[128,16,128]{2,1,0:T(8,128)(2,1)S(1)}, u32[]{:S(2)}, u32[]{:S(2)}) %collective-permute-start.2) | collective-permute-done | bytes 524320 | tf_op jit(solution)/shard_map/ppermute | solution.py:221
  87.4 0.3 pad_maximum_fusion.own_ref
  87.7 1.9 collective-permute-start.3
  89.9 0.8 slice.26
  90.9 0.2 select_reduce_fusion.1
  91.4 2.5 %collective-permute-done.3.other_ref = bf16[4,128,16,128]{3,2,1,0:T(8,128)(2,1)} collective-permute-done((bf16[4,128,16,128]{3,2,1,0:T(8,128)(2,1)S(1)}, bf16[4,128,16,128]{3,2,1,0:T(8,128)(2,1)}, u32[]{:S(2)}, u32[]{:S(2)}) %collective-permute-start.3) | collective-permute-done | bytes 2097184 | tf_op jit(solution)/shard_map/ppermute | solution.py:223
  93.8 2.2 %copy-done = bf16[128,16512]{1,0:T(8,128)(2,1)S(1)} copy-done((bf16[128,16512]{1,0:T(8,128)(2,1)S(1)}, bf16[128,16512]{1,0:T(8,128)(2,1)}, u32[]{:S(2)}) %copy-start) | copy-done | bytes 4227096
  96.0 16.9 %flows_and_grad.1 = (f32[128,384]{1,0:T(8,128)}, bf16[128,16384]{1,0:T(8,128)(2,1)S(1)}) custom-call(s32[128]{0:T(128)S(1)} %reshape.88.label_ref, bf16[128,16512]{1,0:T(8,128)(2,1)S(1)} %copy-done, bf16[4,128,16,128]{3,2,1,0:T(8,128)(2,1)S(1)} %pad_maximum_fusion.own_ref, bf16[4,128,16,128]{3,2,1,0:T(8,128)(2,1)} %collective-permute-done.3.other_ref, ...), custom_call_target="tpu_custom_call" | custom-call | tf_op jit(solution)/shard_map/flows_and_grad/pallas_call | solution.py:172
  112.9 55.9 %all_to_all.22 = bf16[8,16,16384]{2,1,0:T(8,128)(2,1)} all-to-all(bf16[8,16,16384]{2,1,0:T(8,128)(2,1)S(1)} %bitcast.39), channel_id=1, replica_groups={{0,8,16,24,32,40,48,56},{1,9,17,25,33,41,49,57},{2,10,18,26,34,42,50,58..., dimensions={0} | all-to-all | bytes 8388608 | tf_op jit(solution)/shard_map/all_to_all | solution.py:249
  168.8 2.9 %reduce_sum.47 = bf16[16,16384]{1,0:T(8,128)(2,1)S(1)} reduce(bf16[8,16,16384]{2,1,0:T(8,128)(2,1)} %all_to_all.22, bf16[]{:T(256)} %constant.149.clone.1), dimensions={0}, to_apply=%region_3.4 | reduce | flops 1835008 | bytes 4718594 | tf_op jit(solution)/shard_map/reduce_sum | solution.py:253
  171.7 0.3 reshape.85
  172.0 15.7 %all_to_all.23 = bf16[8,2,16384]{2,1,0:T(2,128)(2,1)S(1)} all-to-all(bf16[8,2,16384]{2,1,0:T(2,128)(2,1)S(1)} %reshape.85), channel_id=1, replica_groups={{0,1,2,3,4,5,6,7},{8,9,10,11,12,13,14,15},{16,17,18,19,20,21,22,23},{24..., dimensions={0} | all-to-all | bytes 1048576 | tf_op jit(solution)/shard_map/all_to_all | solution.py:254
  187.7 1.2 reduce_sum.48
  (29 shorter events, 1.0 us)
Async XLA Ops:
  7.2 82.8 %all-gather.2.cloned.1.call-start = ((), (), s32[]{:S(2)}) async-start(), calls=%async_computation.4 | async-start | bytes 4755456 | tf_op jit(solution)/shard_map/all_gather | solution.py:213
  64.2 12.1 %collective-permute-start.1 = (bf16[128,16,128]{2,1,0:T(8,128)(2,1)S(1)}, bf16[128,16,128]{2,1,0:T(8,128)(2,1)S(1)}, u32[]{:S(2)}, u32[]{:S(2)}) collective-permute-start(bf16[128,16,128]{2,1,0:T(8,128)(2,1)S(1)} %bitcast.45), channel_id=1, source_target_pairs={{0,128},{1,129},{2,130},{3,131},{4,132},{5,133},{6,134},{7,135},{8... | collective-permute-start | bytes 1572872 | tf_op jit(solution)/shard_map/ppermute | solution.py:219
  66.6 12.4 %collective-permute-start = (bf16[128,16,128]{2,1,0:T(8,128)(2,1)S(1)}, bf16[128,16,128]{2,1,0:T(8,128)(2,1)S(1)}, u32[]{:S(2)}, u32[]{:S(2)}) collective-permute-start(bf16[128,16,128]{2,1,0:T(8,128)(2,1)S(1)} %bitcast.46), channel_id=1, source_target_pairs={{0,384},{1,385},{2,386},{3,387},{4,388},{5,389},{6,390},{7,391},{8... | collective-permute-start | bytes 1572872 | tf_op jit(solution)/shard_map/ppermute | solution.py:220
  76.3 11.1 %collective-permute-start.2 = (bf16[128,16,128]{2,1,0:T(8,128)(2,1)S(1)}, bf16[128,16,128]{2,1,0:T(8,128)(2,1)S(1)}, u32[]{:S(2)}, u32[]{:S(2)}) collective-permute-start(bf16[128,16,128]{2,1,0:T(8,128)(2,1)S(1)} %collective-permute-done.1), channel_id=1, source_target_pairs={{0,128},{1,129},{2,130},{3,131},{4,132},{5,133},{6,134},{7,135},{8... | collective-permute-start | bytes 1572872 | tf_op jit(solution)/shard_map/ppermute | solution.py:221
  87.4 2.2 %copy-start.2 = (s32[384]{0:T(512)S(1)}, s32[384]{0:T(512)}, u32[]{:S(2)}) copy-start(s32[384]{0:T(512)} %param.11) | copy-start | bytes 4612
  87.4 6.5 %copy-start.1 = (bf16[128,384]{1,0:T(8,128)(2,1)S(1)}, bf16[128,384]{1,0:T(8,128)(2,1)}, u32[]{:S(2)}) copy-start(bf16[128,384]{1,0:T(8,128)(2,1)} %pred_ref.1) | copy-start | bytes 294916
  87.7 6.2 %collective-permute-start.3 = (bf16[4,128,16,128]{3,2,1,0:T(8,128)(2,1)S(1)}, bf16[4,128,16,128]{3,2,1,0:T(8,128)(2,1)}, u32[]{:S(2)}, u32[]{:S(2)}) collective-permute-start(bf16[4,128,16,128]{3,2,1,0:T(8,128)(2,1)S(1)} %pad_maximum_fusion.own_ref), channel_id=1, source_target_pairs={{0,64},{1,65},{2,66},{3,67},{4,68},{5,69},{6,70},{7,71},{8,72},{9,... | collective-permute-start | bytes 6291464 | tf_op jit(solution)/shard_map/ppermute | solution.py:223
  93.8 2.2 %copy-start = (bf16[128,16512]{1,0:T(8,128)(2,1)S(1)}, bf16[128,16512]{1,0:T(8,128)(2,1)}, u32[]{:S(2)}) copy-start(bf16[128,16512]{1,0:T(8,128)(2,1)} %all-gather.2.cloned.1.call-done.x_ref) | copy-start | bytes 12681220
Sparse Core Ops, SparseCore 0:
  42.3 43.9 all-gather.1

commit v4 on v3

--- a/solution.py
+++ b/solution.py
@@ -125,7 +125,7 @@
             acc_ref[line] = acc_ref[line] + part
         return carry
 
-    lax.fori_loop(0, sources, forward, 0, unroll=2)
+    lax.fori_loop(0, sources, forward, 0, unroll=8)
 
     rowp = rowp_ref[...]
     colp = colp_ref[...]
@@ -163,7 +163,7 @@
         c_ref[:, pl.ds(start, BB * TILE)] = jnp.concatenate([low, high], axis=1).astype(BF16)
         return carry
 
-    lax.fori_loop(0, sources, backward, 0, unroll=2)
+    lax.fori_loop(0, sources, backward, 0, unroll=8)
 
 
 def core_call(labels, x, own, other, pred, limit, rowp, colp, nbus):
@@ -186,6 +186,13 @@
     )(labels, x, own, other, pred, limit, rowp, colp)
 
 
+def add_up(parts):
+    total = parts[0].astype(F32)
+    for k in range(1, parts.shape[0]):
+        total = total + parts[k].astype(F32)
+    return total.astype(BF16)
+
+
 def per_device(injections, tile_values, tile_line, tile_bus, flow_pred, line_limit):
     here = lax.axis_index("bus")
     scen = lax.axis_index("scen")
@@ -250,12 +257,12 @@
         contrib.reshape(8, 8 * rows_here, nbus),
         AXES, split_axis=0, concat_axis=0, tiled=True, axis_index_groups=MAJOR,
     )
-    half = jnp.sum(parts.astype(F32), axis=0).astype(BF16)
+    half = add_up(parts)
     last = lax.all_to_all(
         half.reshape(8, rows_here, nbus),
         AXES, split_axis=0, concat_axis=0, tiled=True, axis_index_groups=MINOR,
     )
-    grad_injections = jnp.sum(last.astype(F32), axis=0).astype(BF16)
+    grad_injections = add_up(last)
     return (grad_injections, flows)
 
 

time: 198 us -> 188 us (0.949)
  Pallas kernels: 19.5 us -> 13.2 us
  other arithmetic: 7.08 us -> 4.39 us
    pallas_call x1, Pallas kernels: 16.9 us -> 10.6 us  [core_call(): pl.pallas_call(core_kernel, out_shape=(jax.ShapeDtypeStruct((rows, lines)...]
    reduce_sum x2 -> x0, other arithmetic: 4.11 us -> none  [the longest x1 2.94 us: per_device(): half = jnp.sum(parts.astype(F32), axis=0).astype(BF16)]
where the time goes in v4:
time: 188 us; the launch traced here: 187 us
  blocking collectives  123 us (65%)
  waiting for transfers between devices  17.2 us (9%)
  between operations  14.3 us (8%)
  Pallas kernels  13.2 us (7%)
  starting transfers between devices  10.4 us (6%)
  other arithmetic  4.39 us (2%)
  local copies, waits for them, and re-layouts  4.18 us (2%)
    all_to_all x1, blocking collectives, per_device(): lax.all_to_all(contrib.reshape(8, 8 * rows_here, nbus), AXES, split_axis=...  55.1 us
    all_to_all x1, blocking collectives, per_device(): lax.all_to_all(packed, AXES, split_axis=0, concat_axis=0, tiled=True, axi...  29.6 us
    all_to_all x1, blocking collectives, per_device(): lax.all_to_all(slots.swapaxes(0, 1), AXES, split_axis=0, concat_axis=0, t...  22 us
    all_to_all x1, blocking collectives, per_device(): lax.all_to_all(half.reshape(8, rows_here, nbus), AXES, split_axis=0, conc...  16.2 us
    pallas_call x1, Pallas kernels, core_call(): pl.pallas_call(core_kernel, out_shape=(jax.ShapeDtypeStruct((rows, lines)...  10.6 us
    ppermute x1, waiting for transfers between devices, per_device(): from_far = lax.ppermute(from_below, AXES, X_UP)  8.42 us
    ppermute x1, waiting for transfers between devices, per_device(): from_below = lax.ppermute(mine, AXES, X_UP)  6.25 us
  transfers between devices with their start and end apart: 5, of which 3 were waited for; matrix products, arithmetic and copies ran while one was open for 1% of the time, Pallas kernels for 0%

profile of v4, /device:TPU:6, one launch (start us, length us, event | category | flops | bytes accessed | tf_op | source)
XLA Modules:
  0.0 186.5 jit_solution(12276867861453192713)
XLA Ops:
  7.2 0.7 convert_bitcast_fusion.1
  7.9 0.6 fusion.23.code_ref
  8.5 2.6 %pack.1 = bf16[8,528,128]{2,1,0:T(8,128)(2,1)} custom-call(s32[1]{0:T(128)} %bitcast.core_ref, s32[64]{0:T(128)} %line_ref.1, bf16[64,16,128]{2,1,0:T(8,128)(2,1)} %tiles_ref.1, bf16[256,128]{1,0:T(8,128)(2,1)} %bitcast.56, bf16[16,128]{1,0:T(8,128)(2,1)} %fusion.23.code_ref), custom_call_target="tpu_custom_call" | custom-call | tf_op jit(solution)/shard_map/pack/pallas_call | solution.py:85
  11.2 29.6 %all_to_all.20 = bf16[8,528,128]{2,1,0:T(8,128)(2,1)S(1)} all-to-all(bf16[8,528,128]{2,1,0:T(8,128)(2,1)} %pack.1), channel_id=1, replica_groups={{0,1,2,3,4,5,6,7},{8,9,10,11,12,13,14,15},{16,17,18,19,20,21,22,23},{24..., dimensions={0} | all-to-all | bytes 2162688 | tf_op jit(solution)/shard_map/all_to_all | solution.py:214
  40.9 0.3 copy.22
  41.3 0.8 pad_maximum_fusion.1
  42.2 22.0 %all_to_all.21 = bf16[8,8,2,16,128]{4,3,2,1,0:T(8,128)(2,1)S(1)} all-to-all(bf16[8,8,2,16,128]{4,3,2,1,0:T(8,128)(2,1)S(1)} %bitcast.44), channel_id=1, replica_groups={{0,8,16,24,32,40,48,56},{1,9,17,25,33,41,49,57},{2,10,18,26,34,42,50,58..., dimensions={0} | all-to-all | bytes 1048576 | tf_op jit(solution)/shard_map/all_to_all | solution.py:223
  64.2 2.4 %collective-permute-start.1 = (bf16[128,16,128]{2,1,0:T(8,128)(2,1)S(1)}, bf16[128,16,128]{2,1,0:T(8,128)(2,1)S(1)}, u32[]{:S(2)}, u32[]{:S(2)}) collective-permute-start(bf16[128,16,128]{2,1,0:T(8,128)(2,1)S(1)} %bitcast.47), channel_id=1, source_target_pairs={{0,128},{1,129},{2,130},{3,131},{4,132},{5,133},{6,134},{7,135},{8... | collective-permute-start | bytes 1572872 | tf_op jit(solution)/shard_map/ppermute | solution.py:226
  66.6 3.5 %collective-permute-start = (bf16[128,16,128]{2,1,0:T(8,128)(2,1)S(1)}, bf16[128,16,128]{2,1,0:T(8,128)(2,1)S(1)}, u32[]{:S(2)}, u32[]{:S(2)}) collective-permute-start(bf16[128,16,128]{2,1,0:T(8,128)(2,1)S(1)} %bitcast.48), channel_id=1, source_target_pairs={{0,384},{1,385},{2,386},{3,387},{4,388},{5,389},{6,390},{7,391},{8... | collective-permute-start | bytes 1572872 | tf_op jit(solution)/shard_map/ppermute | solution.py:227
  70.1 6.2 %collective-permute-done.1 = bf16[128,16,128]{2,1,0:T(8,128)(2,1)S(1)} collective-permute-done((bf16[128,16,128]{2,1,0:T(8,128)(2,1)S(1)}, bf16[128,16,128]{2,1,0:T(8,128)(2,1)S(1)}, u32[]{:S(2)}, u32[]{:S(2)}) %collective-permute-start.1) | collective-permute-done | bytes 524320 | tf_op jit(solution)/shard_map/ppermute | solution.py:226
  76.3 2.6 %collective-permute-start.2 = (bf16[128,16,128]{2,1,0:T(8,128)(2,1)S(1)}, bf16[128,16,128]{2,1,0:T(8,128)(2,1)S(1)}, u32[]{:S(2)}, u32[]{:S(2)}) collective-permute-start(bf16[128,16,128]{2,1,0:T(8,128)(2,1)S(1)} %collective-permute-done.1), channel_id=1, source_target_pairs={{0,128},{1,129},{2,130},{3,131},{4,132},{5,133},{6,134},{7,135},{8... | collective-permute-start | bytes 1572872 | tf_op jit(solution)/shard_map/ppermute | solution.py:228
  79.0 8.4 %collective-permute-done.2 = bf16[128,16,128]{2,1,0:T(8,128)(2,1)S(1)} collective-permute-done((bf16[128,16,128]{2,1,0:T(8,128)(2,1)S(1)}, bf16[128,16,128]{2,1,0:T(8,128)(2,1)S(1)}, u32[]{:S(2)}, u32[]{:S(2)}) %collective-permute-start.2) | collective-permute-done | bytes 524320 | tf_op jit(solution)/shard_map/ppermute | solution.py:228
  87.4 0.3 pad_maximum_fusion.own_ref
  87.6 1.9 %collective-permute-start.3 = (bf16[4,128,16,128]{3,2,1,0:T(8,128)(2,1)S(1)}, bf16[4,128,16,128]{3,2,1,0:T(8,128)(2,1)}, u32[]{:S(2)}, u32[]{:S(2)}) collective-permute-start(bf16[4,128,16,128]{3,2,1,0:T(8,128)(2,1)S(1)} %pad_maximum_fusion.own_ref), channel_id=1, source_target_pairs={{0,64},{1,65},{2,66},{3,67},{4,68},{5,69},{6,70},{7,71},{8,72},{9,... | collective-permute-start | bytes 6291464 | tf_op jit(solution)/shard_map/ppermute | solution.py:230
  89.9 0.8 slice.90
  90.9 0.2 select_reduce_fusion.1
  91.3 2.5 %collective-permute-done.3.other_ref = bf16[4,128,16,128]{3,2,1,0:T(8,128)(2,1)} collective-permute-done((bf16[4,128,16,128]{3,2,1,0:T(8,128)(2,1)S(1)}, bf16[4,128,16,128]{3,2,1,0:T(8,128)(2,1)}, u32[]{:S(2)}, u32[]{:S(2)}) %collective-permute-start.3) | collective-permute-done | bytes 2097184 | tf_op jit(solution)/shard_map/ppermute | solution.py:230
  93.8 2.2 %copy-done = bf16[128,16512]{1,0:T(8,128)(2,1)S(1)} copy-done((bf16[128,16512]{1,0:T(8,128)(2,1)S(1)}, bf16[128,16512]{1,0:T(8,128)(2,1)}, u32[]{:S(2)}) %copy-start) | copy-done | bytes 4227096
  96.0 10.6 %flows_and_grad.1 = (f32[128,384]{1,0:T(8,128)}, bf16[128,16384]{1,0:T(8,128)(2,1)S(1)}) custom-call(s32[128]{0:T(128)S(1)} %reshape.123.label_ref, bf16[128,16512]{1,0:T(8,128)(2,1)S(1)} %copy-done, bf16[4,128,16,128]{3,2,1,0:T(8,128)(2,1)S(1)} %pad_maximum_fusion.own_ref, bf16[4,128,16,128]{3,2,1,0:T(8,128)(2,1)} %collective-permute-done.3.other_ref, ...), custom_call_target="tpu_custom_call" | custom-call | tf_op jit(solution)/shard_map/flows_and_grad/pallas_call | solution.py:172
  106.6 55.1 %all_to_all.22 = bf16[8,16,16384]{2,1,0:T(8,128)(2,1)S(1)} all-to-all(bf16[8,16,16384]{2,1,0:T(8,128)(2,1)S(1)} %bitcast.41), channel_id=1, replica_groups={{0,8,16,24,32,40,48,56},{1,9,17,25,33,41,49,57},{2,10,18,26,34,42,50,58..., dimensions={0} | all-to-all | bytes 8388608 | tf_op jit(solution)/shard_map/all_to_all | solution.py:256
  161.7 0.5 add_convert_fusion
  162.3 0.3 reshape.140
  162.6 16.2 %all_to_all.23 = bf16[8,2,16384]{2,1,0:T(2,128)(2,1)S(1)} all-to-all(bf16[8,2,16384]{2,1,0:T(2,128)(2,1)S(1)} %reshape.140), channel_id=1, replica_groups={{0,1,2,3,4,5,6,7},{8,9,10,11,12,13,14,15},{16,17,18,19,20,21,22,23},{24..., dimensions={0} | all-to-all | bytes 1048576 | tf_op jit(solution)/shard_map/all_to_all | solution.py:261
  178.8 0.9 fusion.17
  (29 shorter events, 1.0 us)
Async XLA Ops:
  7.2 82.7 %all-gather.2.cloned.1.call-start = ((), (), s32[]{:S(2)}) async-start(), calls=%async_computation.4 | async-start | bytes 4755456 | tf_op jit(solution)/shard_map/all_gather | solution.py:220
  64.2 12.1 %collective-permute-start.1 = (bf16[128,16,128]{2,1,0:T(8,128)(2,1)S(1)}, bf16[128,16,128]{2,1,0:T(8,128)(2,1)S(1)}, u32[]{:S(2)}, u32[]{:S(2)}) collective-permute-start(bf16[128,16,128]{2,1,0:T(8,128)(2,1)S(1)} %bitcast.47), channel_id=1, source_target_pairs={{0,128},{1,129},{2,130},{3,131},{4,132},{5,133},{6,134},{7,135},{8... | collective-permute-start | bytes 1572872 | tf_op jit(solution)/shard_map/ppermute | solution.py:226
  66.6 12.4 %collective-permute-start = (bf16[128,16,128]{2,1,0:T(8,128)(2,1)S(1)}, bf16[128,16,128]{2,1,0:T(8,128)(2,1)S(1)}, u32[]{:S(2)}, u32[]{:S(2)}) collective-permute-start(bf16[128,16,128]{2,1,0:T(8,128)(2,1)S(1)} %bitcast.48), channel_id=1, source_target_pairs={{0,384},{1,385},{2,386},{3,387},{4,388},{5,389},{6,390},{7,391},{8... | collective-permute-start | bytes 1572872 | tf_op jit(solution)/shard_map/ppermute | solution.py:227
  76.3 11.1 %collective-permute-start.2 = (bf16[128,16,128]{2,1,0:T(8,128)(2,1)S(1)}, bf16[128,16,128]{2,1,0:T(8,128)(2,1)S(1)}, u32[]{:S(2)}, u32[]{:S(2)}) collective-permute-start(bf16[128,16,128]{2,1,0:T(8,128)(2,1)S(1)} %collective-permute-done.1), channel_id=1, source_target_pairs={{0,128},{1,129},{2,130},{3,131},{4,132},{5,133},{6,134},{7,135},{8... | collective-permute-start | bytes 1572872 | tf_op jit(solution)/shard_map/ppermute | solution.py:228
  87.4 2.2 %copy-start.2 = (s32[384]{0:T(512)S(1)}, s32[384]{0:T(512)}, u32[]{:S(2)}) copy-start(s32[384]{0:T(512)} %param.11) | copy-start | bytes 4612
  87.4 6.5 %copy-start.1 = (bf16[128,384]{1,0:T(8,128)(2,1)S(1)}, bf16[128,384]{1,0:T(8,128)(2,1)}, u32[]{:S(2)}) copy-start(bf16[128,384]{1,0:T(8,128)(2,1)} %pred_ref.1) | copy-start | bytes 294916
  87.6 6.2 %collective-permute-start.3 = (bf16[4,128,16,128]{3,2,1,0:T(8,128)(2,1)S(1)}, bf16[4,128,16,128]{3,2,1,0:T(8,128)(2,1)}, u32[]{:S(2)}, u32[]{:S(2)}) collective-permute-start(bf16[4,128,16,128]{3,2,1,0:T(8,128)(2,1)S(1)} %pad_maximum_fusion.own_ref), channel_id=1, source_target_pairs={{0,64},{1,65},{2,66},{3,67},{4,68},{5,69},{6,70},{7,71},{8,72},{9,... | collective-permute-start | bytes 6291464 | tf_op jit(solution)/shard_map/ppermute | solution.py:230
  93.8 2.2 %copy-start = (bf16[128,16512]{1,0:T(8,128)(2,1)S(1)}, bf16[128,16512]{1,0:T(8,128)(2,1)}, u32[]{:S(2)}) copy-start(bf16[128,16512]{1,0:T(8,128)(2,1)} %all-gather.2.cloned.1.call-done.x_ref) | copy-start | bytes 12681220
Sparse Core Ops, SparseCore 0:
  42.3 43.9 all-gather.1

commit v5 on v4

--- a/solution.py
+++ b/solution.py
@@ -253,11 +253,9 @@
         labels, x_all, own, other, flow_pred, line_limit.reshape(1, -1), rowp, colp, nbus
     )
 
-    parts = lax.all_to_all(
-        contrib.reshape(8, 8 * rows_here, nbus),
-        AXES, split_axis=0, concat_axis=0, tiled=True, axis_index_groups=MAJOR,
-    )
-    half = add_up(parts)
+    half = lax.psum_scatter(
+        contrib, AXES, scatter_dimension=0, tiled=True, axis_index_groups=MAJOR
+    )
     last = lax.all_to_all(
         half.reshape(8, rows_here, nbus),
         AXES, split_axis=0, concat_axis=0, tiled=True, axis_index_groups=MINOR,

time: 188 us -> 178 us (0.947)
  blocking collectives: 123 us -> 72 us
  waiting for transfers between devices: 17.2 us -> 56.6 us
  local copies, waits for them, and re-layouts: 4.18 us -> 7.18 us
    all_to_all x1 -> x0, blocking collectives: 55.1 us -> none  [per_device(): lax.all_to_all(contrib.reshape(8, 8 * rows_here, nbus), AXES, split_axis=...]
    reduce_scatter x0 -> x1, waiting for transfers between devices: none -> 39.4 us  [per_device(): lax.psum_scatter(contrib, AXES, scatter_dimension=0, tiled=True, axis_ind...]
    all_to_all x1, blocking collectives: 16.2 us -> 20.5 us  [per_device(): lax.all_to_all(half.reshape(8, rows_here, nbus), AXES, split_axis=0, conc...]
    unnamed x7 -> x9, local copies, waits for them, and re-layouts: 2.55 us -> 4.5 us
  transfers between devices with their start and end apart: 5 -> 6, of which waited for: 3 -> 4; matrix products, arithmetic and copies ran while one was open for 1% -> 1% of each run, Pallas kernels for 0% -> 0%
where the time goes in v5:
time: 178 us
  blocking collectives  72 us (40%)
  waiting for transfers between devices  56.6 us (32%)
  between operations  14.3 us (8%)
  Pallas kernels  13.3 us (7%)
  starting transfers between devices  10.4 us (6%)
  local copies, waits for them, and re-layouts  7.18 us (4%)
  other arithmetic  3.85 us (2%)
    reduce_scatter x1, waiting for transfers between devices, per_device(): lax.psum_scatter(contrib, AXES, scatter_dimension=0, tiled=True, axis_ind...  39.4 us
    all_to_all x1, blocking collectives, per_device(): lax.all_to_all(packed, AXES, split_axis=0, concat_axis=0, tiled=True, axi...  29.6 us
    all_to_all x1, blocking collectives, per_device(): lax.all_to_all(slots.swapaxes(0, 1), AXES, split_axis=0, concat_axis=0, t...  22 us
    all_to_all x1, blocking collectives, per_device(): lax.all_to_all(half.reshape(8, rows_here, nbus), AXES, split_axis=0, conc...  20.5 us
    pallas_call x1, Pallas kernels, core_call(): pl.pallas_call(core_kernel, out_shape=(jax.ShapeDtypeStruct((rows, lines)...  10.6 us
    ppermute x1, waiting for transfers between devices, per_device(): from_far = lax.ppermute(from_below, AXES, X_UP)  8.45 us
    ppermute x1, waiting for transfers between devices, per_device(): from_below = lax.ppermute(mine, AXES, X_UP)  6.3 us
    unnamed x9, local copies, waits for them, and re-layouts  4.5 us
  transfers between devices with their start and end apart: 6, of which 4 were waited for; matrix products, arithmetic and copies ran while one was open for 1% of the time, Pallas kernels for 0%

profile of v5, /device:TPU:6, one launch (start us, length us, event | category | flops | bytes accessed | tf_op | source)
XLA Modules:
  0.0 177.7 jit_solution(3125898921127539317)
XLA Ops:
  7.2 0.7 convert_bitcast_fusion.1
  7.9 0.6 fusion.23.code_ref
  8.5 2.6 %pack.1 = bf16[8,528,128]{2,1,0:T(8,128)(2,1)} custom-call(s32[1]{0:T(128)} %bitcast.core_ref, s32[64]{0:T(128)} %line_ref.1, bf16[64,16,128]{2,1,0:T(8,128)(2,1)} %tiles_ref.1, bf16[256,128]{1,0:T(8,128)(2,1)} %bitcast.54, bf16[16,128]{1,0:T(8,128)(2,1)} %fusion.23.code_ref), custom_call_target="tpu_custom_call" | custom-call | tf_op jit(solution)/shard_map/pack/pallas_call | solution.py:85
  11.2 29.6 %all_to_all.15 = bf16[8,528,128]{2,1,0:T(8,128)(2,1)S(1)} all-to-all(bf16[8,528,128]{2,1,0:T(8,128)(2,1)} %pack.1), channel_id=1, replica_groups={{0,1,2,3,4,5,6,7},{8,9,10,11,12,13,14,15},{16,17,18,19,20,21,22,23},{24..., dimensions={0} | all-to-all | bytes 2162688 | tf_op jit(solution)/shard_map/all_to_all | solution.py:214
  41.0 0.3 copy.22
  41.3 0.8 pad_maximum_fusion.1
  42.3 22.0 %all_to_all.16 = bf16[8,8,2,16,128]{4,3,2,1,0:T(8,128)(2,1)S(1)} all-to-all(bf16[8,8,2,16,128]{4,3,2,1,0:T(8,128)(2,1)S(1)} %bitcast.42), channel_id=1, replica_groups={{0,8,16,24,32,40,48,56},{1,9,17,25,33,41,49,57},{2,10,18,26,34,42,50,58..., dimensions={0} | all-to-all | bytes 1048576 | tf_op jit(solution)/shard_map/all_to_all | solution.py:223
  64.3 2.4 %collective-permute-start.1 = (bf16[128,16,128]{2,1,0:T(8,128)(2,1)S(1)}, bf16[128,16,128]{2,1,0:T(8,128)(2,1)S(1)}, u32[]{:S(2)}, u32[]{:S(2)}) collective-permute-start(bf16[128,16,128]{2,1,0:T(8,128)(2,1)S(1)} %bitcast.45), channel_id=1, source_target_pairs={{0,128},{1,129},{2,130},{3,131},{4,132},{5,133},{6,134},{7,135},{8... | collective-permute-start | bytes 1572872 | tf_op jit(solution)/shard_map/ppermute | solution.py:226
  66.6 3.5 %collective-permute-start = (bf16[128,16,128]{2,1,0:T(8,128)(2,1)S(1)}, bf16[128,16,128]{2,1,0:T(8,128)(2,1)S(1)}, u32[]{:S(2)}, u32[]{:S(2)}) collective-permute-start(bf16[128,16,128]{2,1,0:T(8,128)(2,1)S(1)} %bitcast.46), channel_id=1, source_target_pairs={{0,384},{1,385},{2,386},{3,387},{4,388},{5,389},{6,390},{7,391},{8... | collective-permute-start | bytes 1572872 | tf_op jit(solution)/shard_map/ppermute | solution.py:227
  70.1 6.3 %collective-permute-done.1 = bf16[128,16,128]{2,1,0:T(8,128)(2,1)S(1)} collective-permute-done((bf16[128,16,128]{2,1,0:T(8,128)(2,1)S(1)}, bf16[128,16,128]{2,1,0:T(8,128)(2,1)S(1)}, u32[]{:S(2)}, u32[]{:S(2)}) %collective-permute-start.1) | collective-permute-done | bytes 524320 | tf_op jit(solution)/shard_map/ppermute | solution.py:226
  76.4 2.6 %collective-permute-start.2 = (bf16[128,16,128]{2,1,0:T(8,128)(2,1)S(1)}, bf16[128,16,128]{2,1,0:T(8,128)(2,1)S(1)}, u32[]{:S(2)}, u32[]{:S(2)}) collective-permute-start(bf16[128,16,128]{2,1,0:T(8,128)(2,1)S(1)} %collective-permute-done.1), channel_id=1, source_target_pairs={{0,128},{1,129},{2,130},{3,131},{4,132},{5,133},{6,134},{7,135},{8... | collective-permute-start | bytes 1572872 | tf_op jit(solution)/shard_map/ppermute | solution.py:228
  79.0 8.4 %collective-permute-done.2 = bf16[128,16,128]{2,1,0:T(8,128)(2,1)S(1)} collective-permute-done((bf16[128,16,128]{2,1,0:T(8,128)(2,1)S(1)}, bf16[128,16,128]{2,1,0:T(8,128)(2,1)S(1)}, u32[]{:S(2)}, u32[]{:S(2)}) %collective-permute-start.2) | collective-permute-done | bytes 524320 | tf_op jit(solution)/shard_map/ppermute | solution.py:228
  87.5 0.3 pad_maximum_fusion.own_ref
  87.8 1.9 %collective-permute-start.3 = (bf16[4,128,16,128]{3,2,1,0:T(8,128)(2,1)S(1)}, bf16[4,128,16,128]{3,2,1,0:T(8,128)(2,1)}, u32[]{:S(2)}, u32[]{:S(2)}) collective-permute-start(bf16[4,128,16,128]{3,2,1,0:T(8,128)(2,1)S(1)} %pad_maximum_fusion.own_ref), channel_id=1, source_target_pairs={{0,64},{1,65},{2,66},{3,67},{4,68},{5,69},{6,70},{7,71},{8,72},{9,... | collective-permute-start | bytes 6291464 | tf_op jit(solution)/shard_map/ppermute | solution.py:230
  90.0 0.8 slice.58
  91.0 0.2 select_reduce_fusion.1
  91.5 2.5 %collective-permute-done.3.other_ref = bf16[4,128,16,128]{3,2,1,0:T(8,128)(2,1)} collective-permute-done((bf16[4,128,16,128]{3,2,1,0:T(8,128)(2,1)S(1)}, bf16[4,128,16,128]{3,2,1,0:T(8,128)(2,1)}, u32[]{:S(2)}, u32[]{:S(2)}) %collective-permute-start.3) | collective-permute-done | bytes 2097184 | tf_op jit(solution)/shard_map/ppermute | solution.py:230
  93.9 2.2 %copy-done = bf16[128,16512]{1,0:T(8,128)(2,1)S(1)} copy-done((bf16[128,16512]{1,0:T(8,128)(2,1)S(1)}, bf16[128,16512]{1,0:T(8,128)(2,1)}, u32[]{:S(2)}) %copy-start) | copy-done | bytes 4227096
  96.1 10.6 %flows_and_grad.1 = (f32[128,384]{1,0:T(8,128)}, bf16[128,16384]{1,0:T(8,128)(2,1)S(1)}) custom-call(s32[128]{0:T(128)S(1)} %reshape.99.label_ref, bf16[128,16512]{1,0:T(8,128)(2,1)S(1)} %copy-done, bf16[4,128,16,128]{3,2,1,0:T(8,128)(2,1)S(1)} %pad_maximum_fusion.own_ref, bf16[4,128,16,128]{3,2,1,0:T(8,128)(2,1)} %collective-permute-done.3.other_ref, ...), custom_call_target="tpu_custom_call" | custom-call | tf_op jit(solution)/shard_map/flows_and_grad/pallas_call | solution.py:172
  106.8 2.0 %copy-done.1 = bf16[128,16384]{1,0:T(8,128)(2,1)} copy-done((bf16[128,16384]{1,0:T(8,128)(2,1)}, bf16[128,16384]{1,0:T(8,128)(2,1)S(1)}, u32[]{:S(2)}) %copy-start.1) | copy-done | bytes 4194328
  108.7 39.4 %reduce-scatter.2.cloned.1.call-done = bf16[16,16384]{1,0:T(8,128)(2,1)} async-done(((bf16[128,16384]{1,0:T(8,128)(2,1)}), bf16[16,16384]{1,0:T(8,128)(2,1)}) %reduce-scatter.2.cloned.1.call-update) | async-done | bytes 524304 | tf_op jit(solution)/shard_map/reduce_scatter | solution.py:256
  148.1 1.4 reshape.96
  149.5 20.5 %all_to_all.17 = bf16[8,2,16384]{2,1,0:T(2,128)(2,1)S(1)} all-to-all(bf16[8,2,16384]{2,1,0:T(2,128)(2,1)S(1)} %reshape.96), channel_id=1, replica_groups={{0,1,2,3,4,5,6,7},{8,9,10,11,12,13,14,15},{16,17,18,19,20,21,22,23},{24..., dimensions={0} | all-to-all | bytes 1048576 | tf_op jit(solution)/shard_map/all_to_all | solution.py:259
  170.0 0.9 fusion.17
  (32 shorter events, 1.1 us)
Async XLA Ops:
  7.2 82.9 %all-gather.2.cloned.1.call-start = ((), (), s32[]{:S(2)}) async-start(), calls=%async_computation.4 | async-start | bytes 4755456 | tf_op jit(solution)/shard_map/all_gather | solution.py:220
  42.2 105.9 %reduce-scatter.2.cloned.1.call-start = ((), (), s32[]{:S(2)}) async-start(), calls=%async_computation.5 | async-start | bytes 4718592 | tf_op jit(solution)/shard_map/reduce_scatter | solution.py:256
  64.3 12.1 %collective-permute-start.1 = (bf16[128,16,128]{2,1,0:T(8,128)(2,1)S(1)}, bf16[128,16,128]{2,1,0:T(8,128)(2,1)S(1)}, u32[]{:S(2)}, u32[]{:S(2)}) collective-permute-start(bf16[128,16,128]{2,1,0:T(8,128)(2,1)S(1)} %bitcast.45), channel_id=1, source_target_pairs={{0,128},{1,129},{2,130},{3,131},{4,132},{5,133},{6,134},{7,135},{8... | collective-permute-start | bytes 1572872 | tf_op jit(solution)/shard_map/ppermute | solution.py:226
  66.6 12.4 %collective-permute-start = (bf16[128,16,128]{2,1,0:T(8,128)(2,1)S(1)}, bf16[128,16,128]{2,1,0:T(8,128)(2,1)S(1)}, u32[]{:S(2)}, u32[]{:S(2)}) collective-permute-start(bf16[128,16,128]{2,1,0:T(8,128)(2,1)S(1)} %bitcast.46), channel_id=1, source_target_pairs={{0,384},{1,385},{2,386},{3,387},{4,388},{5,389},{6,390},{7,391},{8... | collective-permute-start | bytes 1572872 | tf_op jit(solution)/shard_map/ppermute | solution.py:227
  76.4 11.1 %collective-permute-start.2 = (bf16[128,16,128]{2,1,0:T(8,128)(2,1)S(1)}, bf16[128,16,128]{2,1,0:T(8,128)(2,1)S(1)}, u32[]{:S(2)}, u32[]{:S(2)}) collective-permute-start(bf16[128,16,128]{2,1,0:T(8,128)(2,1)S(1)} %collective-permute-done.1), channel_id=1, source_target_pairs={{0,128},{1,129},{2,130},{3,131},{4,132},{5,133},{6,134},{7,135},{8... | collective-permute-start | bytes 1572872 | tf_op jit(solution)/shard_map/ppermute | solution.py:228
  87.5 2.2 %copy-start.3 = (s32[384]{0:T(512)S(1)}, s32[384]{0:T(512)}, u32[]{:S(2)}) copy-start(s32[384]{0:T(512)} %param.11) | copy-start | bytes 4612
  87.5 6.5 %copy-start.2 = (bf16[128,384]{1,0:T(8,128)(2,1)S(1)}, bf16[128,384]{1,0:T(8,128)(2,1)}, u32[]{:S(2)}) copy-start(bf16[128,384]{1,0:T(8,128)(2,1)} %pred_ref.1) | copy-start | bytes 294916
  87.8 6.2 %collective-permute-start.3 = (bf16[4,128,16,128]{3,2,1,0:T(8,128)(2,1)S(1)}, bf16[4,128,16,128]{3,2,1,0:T(8,128)(2,1)}, u32[]{:S(2)}, u32[]{:S(2)}) collective-permute-start(bf16[4,128,16,128]{3,2,1,0:T(8,128)(2,1)S(1)} %pad_maximum_fusion.own_ref), channel_id=1, source_target_pairs={{0,64},{1,65},{2,66},{3,67},{4,68},{5,69},{6,70},{7,71},{8,72},{9,... | collective-permute-start | bytes 6291464 | tf_op jit(solution)/shard_map/ppermute | solution.py:230
  93.9 2.2 %copy-start = (bf16[128,16512]{1,0:T(8,128)(2,1)S(1)}, bf16[128,16512]{1,0:T(8,128)(2,1)}, u32[]{:S(2)}) copy-start(bf16[128,16512]{1,0:T(8,128)(2,1)} %all-gather.2.cloned.1.call-done.x_ref) | copy-start | bytes 12681220
  106.8 2.0 %copy-start.1 = (bf16[128,16384]{1,0:T(8,128)(2,1)}, bf16[128,16384]{1,0:T(8,128)(2,1)S(1)}, u32[]{:S(2)}) copy-start(bf16[128,16384]{1,0:T(8,128)(2,1)S(1)} %get-tuple-element.4) | copy-start | bytes 12582916
Sparse Core Ops, SparseCore 0:
  42.3 43.9 all-gather.1
  108.9 39.1 reduce-scatter.1

commit v6 on v5

--- a/solution.py
+++ b/solution.py
@@ -14,6 +14,8 @@
 LB = 3
 BB = 2
 CAP = 2
+CODE_ROWS = 16
+CHUNKS = 8
 F32 = jnp.float32
 BF16 = jnp.bfloat16
 
@@ -50,12 +52,16 @@
 CORE_SWAP = pairs(lambda x, c, y, z: dev(x, 1 - c, y, z))
 
 
-def pack_kernel(core_ref, line_ref, tiles_ref, x_ref, code_ref, out_ref, count_ref):
+def pack_kernel(core_ref, line_ref, linev_ref, busv_ref, tiles_ref, x_ref, out_ref, count_ref):
     x_rows = x_ref.shape[0]
-    head = x_rows + code_ref.shape[0]
+    head = x_rows + CODE_ROWS
+    count = linev_ref.shape[1]
+    row = lax.broadcasted_iota(jnp.int32, (CODE_ROWS, count), 0)
+    code = jnp.where(row == 0, linev_ref[...], busv_ref[...]).astype(F32).astype(BF16)
     for m in range(out_ref.shape[0]):
         out_ref[m, :x_rows] = x_ref[...]
-        out_ref[m, x_rows:head] = code_ref[...]
+        out_ref[m, x_rows:head] = jnp.zeros((CODE_ROWS, TILE), BF16)
+        out_ref[m, x_rows:head, :count] = code
         out_ref[m, head:] = jnp.zeros((out_ref.shape[1] - head, TILE), out_ref.dtype)
     for i in range(count_ref.shape[0]):
         count_ref[i] = 0
@@ -77,19 +83,19 @@
     lax.fori_loop(0, tiles_ref.shape[0], body, 0, unroll=4)
 
 
-def pack(core, tile_line, tile_values, x, codes, owners):
+def pack(core, tile_line, tile_bus, tile_values, x, owners):
     rows = tile_values.shape[1]
-    total = x.shape[0] + codes.shape[0] + 8 * CAP * rows
+    total = x.shape[0] + CODE_ROWS + 8 * CAP * rows
     smem = pl.BlockSpec(memory_space=pltpu.SMEM)
     vmem = pl.BlockSpec(memory_space=pltpu.VMEM)
     return pl.pallas_call(
         pack_kernel,
         out_shape=jax.ShapeDtypeStruct((8, total, TILE), BF16),
-        in_specs=[smem, smem, vmem, vmem, vmem],
+        in_specs=[smem, smem, vmem, vmem, vmem, vmem],
         out_specs=vmem,
         scratch_shapes=[pltpu.SMEM((owners,), jnp.int32)],
         name="pack",
-    )(core.reshape(1), tile_line, tile_values, x, codes)
+    )(core.reshape(1), tile_line, tile_line.reshape(1, -1), tile_bus.reshape(1, -1), tile_values, x)
 
 
 def dot(a, b, dims):
@@ -101,31 +107,50 @@
 
 
 def core_kernel(
-    label_ref, x_ref, own_ref, other_ref, pred_ref, limit_ref, rowp_ref, colp_ref,
-    flows_ref, c_ref, acc_ref, g_ref,
+    core_ref, label_ref, x_hbm, own_ref, other_ref, pred_ref, limit_ref, rowp_ref, colp_ref,
+    flows_ref, c_hbm, x_ref, c_ref, acc_ref, g_ref, in_sem, out_sem,
 ):
     sources = label_ref.shape[0] // CAP
-
-    def tile(s, r):
-        here = s * CAP + r
-        there = ((s & 7) * 8 + (s >> 3)) * CAP + r
+    step = sources // CHUNKS
+    width = step * BB * TILE
+
+    def bring(k):
+        lanes = pl.ds(pl.multiple_of(k * width, width), width)
+        return pltpu.make_async_copy(x_hbm.at[:, lanes], x_ref.at[:, lanes], in_sem.at[k])
+
+    def leave(k):
+        lanes = pl.ds(pl.multiple_of(k * width, width), width)
+        return pltpu.make_async_copy(c_ref.at[:, lanes], c_hbm.at[:, lanes], out_sem.at[k])
+
+    for k in range(CHUNKS):
+        bring(k).start()
+
+    first_core = core_ref[0] == 0
+
+    def places(b):
+        swapped = (b & 7) * 8 + (b >> 3)
+        return jnp.where(first_core, b, swapped) * CAP, jnp.where(first_core, swapped, b) * CAP
+
+    def tile(here, there):
         return jnp.concatenate(
             [own_ref[d, here] for d in range(NX)] + [other_ref[d, there] for d in range(NX)], axis=0
         )
 
     acc_ref[...] = jnp.zeros_like(acc_ref)
 
-    def forward(s, carry):
-        for r in range(CAP):
-            j = s * CAP + r
-            code = label_ref[j]
-            line = code & 3
-            start = pl.multiple_of((code >> 2) * TILE, TILE)
-            part = dot(x_ref[:, pl.ds(start, TILE)], tile(s, r), NT)
-            acc_ref[line] = acc_ref[line] + part
+    def forward(k, carry):
+        bring(k).wait()
+        for i in range(step):
+            here, there = places(k * step + i)
+            for r in range(CAP):
+                code = label_ref[here + r]
+                line = code & 3
+                start = pl.multiple_of((code >> 2) * TILE, TILE)
+                part = dot(x_ref[:, pl.ds(start, TILE)], tile(here + r, there + r), NT)
+                acc_ref[line] = acc_ref[line] + part
         return carry
 
-    lax.fori_loop(0, sources, forward, 0, unroll=8)
+    lax.fori_loop(0, CHUNKS, forward, 0)
 
     rowp = rowp_ref[...]
     colp = colp_ref[...]
@@ -148,42 +173,52 @@
         grad = dot(rowp, grad, ((0,), (0,))).astype(BF16)
         g_ref[b] = dot(grad, colp, NT).astype(BF16)
 
-    def backward(s, carry):
-        low = jnp.zeros((g_ref.shape[1], TILE), F32)
-        high = low
-        for r in range(CAP):
-            j = s * CAP + r
-            code = label_ref[j]
-            line = code & 3
-            bus = (code >> 2) & 1
-            part = dot(g_ref[line], tile(s, r), NN)
-            low = low + jnp.where(bus == 0, part, 0.0)
-            high = high + jnp.where(bus == 1, part, 0.0)
-        start = pl.multiple_of((label_ref[s * CAP] >> 3) * (BB * TILE), BB * TILE)
-        c_ref[:, pl.ds(start, BB * TILE)] = jnp.concatenate([low, high], axis=1).astype(BF16)
+    def backward(k, carry):
+        for i in range(step):
+            here, there = places(k * step + i)
+            low = jnp.zeros((g_ref.shape[1], TILE), F32)
+            high = low
+            for r in range(CAP):
+                code = label_ref[here + r]
+                line = code & 3
+                bus = (code >> 2) & 1
+                part = dot(g_ref[line], tile(here + r, there + r), NN)
+                low = low + jnp.where(bus == 0, part, 0.0)
+                high = high + jnp.where(bus == 1, part, 0.0)
+            start = pl.multiple_of((k * step + i) * (BB * TILE), BB * TILE)
+            c_ref[:, pl.ds(start, BB * TILE)] = jnp.concatenate([low, high], axis=1).astype(BF16)
+        leave(k).start()
         return carry
 
-    lax.fori_loop(0, sources, backward, 0, unroll=8)
-
-
-def core_call(labels, x, own, other, pred, limit, rowp, colp, nbus):
+    lax.fori_loop(0, CHUNKS, backward, 0)
+    for k in range(CHUNKS):
+        leave(k).wait()
+
+
+def core_call(core, labels, x, own, other, pred, limit, rowp, colp, nbus):
     rows, lines = pred.shape
+    smem = pl.BlockSpec(memory_space=pltpu.SMEM)
     vmem = pl.BlockSpec(memory_space=pltpu.VMEM)
+    anywhere = pl.BlockSpec(memory_space=pl.ANY)
     return pl.pallas_call(
         core_kernel,
         out_shape=(
             jax.ShapeDtypeStruct((rows, lines), F32),
             jax.ShapeDtypeStruct((rows, nbus), BF16),
         ),
-        in_specs=[pl.BlockSpec(memory_space=pltpu.SMEM)] + [vmem] * 7,
-        out_specs=(vmem, vmem),
+        in_specs=[smem, smem, anywhere] + [vmem] * 6,
+        out_specs=(vmem, anywhere),
         scratch_shapes=[
+            pltpu.VMEM((rows, nbus), BF16),
+            pltpu.VMEM((rows, nbus), BF16),
             pltpu.VMEM((LB, rows, TILE), F32),
             pltpu.VMEM((LB, rows, TILE), BF16),
+            pltpu.SemaphoreType.DMA((CHUNKS,)),
+            pltpu.SemaphoreType.DMA((CHUNKS,)),
         ],
         compiler_params=pltpu.CompilerParams(vmem_limit_bytes=32 * 1024 * 1024),
         name="flows_and_grad",
-    )(labels, x, own, other, pred, limit, rowp, colp)
+    )(core.reshape(1), labels, x, own, other, pred, limit, rowp, colp)
 
 
 def add_up(parts):
@@ -202,15 +237,10 @@
     rows_here, nbus = injections.shape
     count = tile_line.shape[0]
 
-    owner = tile_line // LB
-    inside = (tile_line % LB) * BB + tile_bus
-    codes = jnp.pad(
-        jnp.stack([owner, inside]), ((0, 14), (0, TILE - count)), constant_values=255
-    ).astype(BF16)
     blocks = nbus // TILE
     x_rows = rows_here * blocks
     flat = injections.reshape(rows_here, blocks, TILE).swapaxes(0, 1).reshape(x_rows, TILE)
-    packed = pack(core, tile_line, tile_values, flat, codes, buses)
+    packed = pack(core, tile_line, tile_bus, tile_values, flat, buses)
     hop = lax.all_to_all(
         packed, AXES, split_axis=0, concat_axis=0, tiled=True, axis_index_groups=MINOR
     )
@@ -219,7 +249,7 @@
     near = jnp.concatenate([near_x.reshape(8 * rows_here, nbus), near_code], axis=1)
     x_all = lax.all_gather(near, AXES, axis=0, tiled=True, axis_index_groups=MAJOR)
 
-    slots = hop[:, x_rows + codes.shape[0] :].reshape((8, 8, CAP) + tile_values.shape[1:])
+    slots = hop[:, x_rows + CODE_ROWS :].reshape((8, 8, CAP) + tile_values.shape[1:])
     mine = lax.all_to_all(
         slots.swapaxes(0, 1), AXES, split_axis=0, concat_axis=0, tiled=True, axis_index_groups=MAJOR
     ).reshape((buses * CAP,) + tile_values.shape[1:])
@@ -230,9 +260,10 @@
     other = lax.ppermute(own, AXES, CORE_SWAP)
 
     tags = x_all[:, nbus:].astype(jnp.int32).reshape(buses, rows_here, TILE)
-    hit = tags[:, 0, :] == here
-    inner = tags[:, 1, :]
-    lane = lax.broadcasted_iota(jnp.int32, hit.shape, 1)
+    line = tags[:, 0, :]
+    inner = (line % LB) * BB + tags[:, 1, :]
+    lane = lax.broadcasted_iota(jnp.int32, line.shape, 1)
+    hit = (line // LB == here) & (lane < count)
     first = jnp.min(jnp.where(hit, lane, TILE), axis=1, keepdims=True)
     code_first = jnp.sum(jnp.where(lane == first, inner, 0), axis=1, keepdims=True)
     code_second = jnp.sum(jnp.where(hit, inner, 0), axis=1, keepdims=True) - code_first
@@ -250,7 +281,7 @@
     colp = (col == line_of).astype(BF16)
 
     flows, contrib = core_call(
-        labels, x_all, own, other, flow_pred, line_limit.reshape(1, -1), rowp, colp, nbus
+        core, labels, x_all, own, other, flow_pred, line_limit.reshape(1, -1), rowp, colp, nbus
     )
 
     half = lax.psum_scatter(

time: 178 us -> 180 us (1.011)
    unnamed x9 -> x13, local copies, waits for them, and re-layouts: 4.5 us -> 5.31 us
  transfers between devices with their start and end apart: 6 -> 6, of which waited for: 4 -> 4; matrix products, arithmetic and copies ran while one was open for 1% -> 2% of each run, Pallas kernels for 0% -> 0%
where the time goes in v6:
time: 180 us; the launch traced here: 179 us
  blocking collectives  72 us (40%)
  waiting for transfers between devices  56.6 us (31%)
  between operations  14.3 us (8%)
  Pallas kernels  13.9 us (8%)
  starting transfers between devices  10.4 us (6%)
  local copies, waits for them, and re-layouts  7.99 us (4%)
  other arithmetic  3.81 us (2%)
    reduce_scatter x1, waiting for transfers between devices, per_device(): lax.psum_scatter(contrib, AXES, scatter_dimension=0, tiled=True, axis_ind...  39.4 us
    all_to_all x1, blocking collectives, per_device(): lax.all_to_all(packed, AXES, split_axis=0, concat_axis=0, tiled=True, axi...  29.6 us
    all_to_all x1, blocking collectives, per_device(): lax.all_to_all(slots.swapaxes(0, 1), AXES, split_axis=0, concat_axis=0, t...  22 us
    all_to_all x1, blocking collectives, per_device(): lax.all_to_all(half.reshape(8, rows_here, nbus), AXES, split_axis=0, conc...  20.5 us
    pallas_call x1, Pallas kernels, core_call(): pl.pallas_call(core_kernel, out_shape=(jax.ShapeDtypeStruct((rows, lines)...  11.3 us
    ppermute x1, waiting for transfers between devices, per_device(): from_far = lax.ppermute(from_below, AXES, X_UP)  8.38 us
    ppermute x1, waiting for transfers between devices, per_device(): from_below = lax.ppermute(mine, AXES, X_UP)  6.29 us
    unnamed x13, local copies, waits for them, and re-layouts  5.31 us
  transfers between devices with their start and end apart: 6, of which 4 were waited for; matrix products, arithmetic and copies ran while one was open for 2% of the time, Pallas kernels for 0%

profile of v6, /device:TPU:6, one launch (start us, length us, event | category | flops | bytes accessed | tf_op | source)
XLA Modules:
  0.0 179.2 jit_solution(8984662007645278952)
XLA Ops:
  7.2 2.6 %pack.1 = bf16[8,528,128]{2,1,0:T(8,128)(2,1)} custom-call(s32[1]{0:T(128)} %bitcast.core_ref, s32[64]{0:T(128)} %line_ref.1, s32[1,64]{1,0:T(1,128)} %bitcast.83, s32[1,64]{1,0:T(1,128)} %bitcast.85, bf16[64,16,128]{2,1,0:T(8,128)(2,1)} %tiles_ref.1, bf16[256,128]{1,0:T(8,128)(2,1)} %bitcast.81), custom_call_target="tpu_custom_call" | custom-call | tf_op jit(solution)/shard_map/pack/pallas_call | solution.py:91
  9.9 29.6 %all_to_all.15 = bf16[8,528,128]{2,1,0:T(8,128)(2,1)S(1)} all-to-all(bf16[8,528,128]{2,1,0:T(8,128)(2,1)} %pack.1), channel_id=1, replica_groups={{0,1,2,3,4,5,6,7},{8,9,10,11,12,13,14,15},{16,17,18,19,20,21,22,23},{24..., dimensions={0} | all-to-all | bytes 2162688 | tf_op jit(solution)/shard_map/all_to_all | solution.py:244
  39.7 0.3 copy.22
  40.0 0.8 pad_maximum_fusion.1
  41.0 22.0 %all_to_all.16 = bf16[8,8,2,16,128]{4,3,2,1,0:T(8,128)(2,1)S(1)} all-to-all(bf16[8,8,2,16,128]{4,3,2,1,0:T(8,128)(2,1)S(1)} %bitcast.68), channel_id=1, replica_groups={{0,8,16,24,32,40,48,56},{1,9,17,25,33,41,49,57},{2,10,18,26,34,42,50,58..., dimensions={0} | all-to-all | bytes 1048576 | tf_op jit(solution)/shard_map/all_to_all | solution.py:253
  63.0 2.4 %collective-permute-start.1 = (bf16[128,16,128]{2,1,0:T(8,128)(2,1)S(1)}, bf16[128,16,128]{2,1,0:T(8,128)(2,1)S(1)}, u32[]{:S(2)}, u32[]{:S(2)}) collective-permute-start(bf16[128,16,128]{2,1,0:T(8,128)(2,1)S(1)} %bitcast.71), channel_id=1, source_target_pairs={{0,128},{1,129},{2,130},{3,131},{4,132},{5,133},{6,134},{7,135},{8... | collective-permute-start | bytes 1572872 | tf_op jit(solution)/shard_map/ppermute | solution.py:256
  65.4 3.5 %collective-permute-start = (bf16[128,16,128]{2,1,0:T(8,128)(2,1)S(1)}, bf16[128,16,128]{2,1,0:T(8,128)(2,1)S(1)}, u32[]{:S(2)}, u32[]{:S(2)}) collective-permute-start(bf16[128,16,128]{2,1,0:T(8,128)(2,1)S(1)} %bitcast.72), channel_id=1, source_target_pairs={{0,384},{1,385},{2,386},{3,387},{4,388},{5,389},{6,390},{7,391},{8... | collective-permute-start | bytes 1572872 | tf_op jit(solution)/shard_map/ppermute | solution.py:257
  68.8 6.3 %collective-permute-done.1 = bf16[128,16,128]{2,1,0:T(8,128)(2,1)S(1)} collective-permute-done((bf16[128,16,128]{2,1,0:T(8,128)(2,1)S(1)}, bf16[128,16,128]{2,1,0:T(8,128)(2,1)S(1)}, u32[]{:S(2)}, u32[]{:S(2)}) %collective-permute-start.1) | collective-permute-done | bytes 524320 | tf_op jit(solution)/shard_map/ppermute | solution.py:256
  75.1 2.6 %collective-permute-start.2 = (bf16[128,16,128]{2,1,0:T(8,128)(2,1)S(1)}, bf16[128,16,128]{2,1,0:T(8,128)(2,1)S(1)}, u32[]{:S(2)}, u32[]{:S(2)}) collective-permute-start(bf16[128,16,128]{2,1,0:T(8,128)(2,1)S(1)} %collective-permute-done.1), channel_id=1, source_target_pairs={{0,128},{1,129},{2,130},{3,131},{4,132},{5,133},{6,134},{7,135},{8... | collective-permute-start | bytes 1572872 | tf_op jit(solution)/shard_map/ppermute | solution.py:258
  77.8 8.4 %collective-permute-done.2 = bf16[128,16,128]{2,1,0:T(8,128)(2,1)S(1)} collective-permute-done((bf16[128,16,128]{2,1,0:T(8,128)(2,1)S(1)}, bf16[128,16,128]{2,1,0:T(8,128)(2,1)S(1)}, u32[]{:S(2)}, u32[]{:S(2)}) %collective-permute-start.2) | collective-permute-done | bytes 524320 | tf_op jit(solution)/shard_map/ppermute | solution.py:258
  86.2 0.8 copy-done.4
  87.0 1.5 pad_maximum_fusion.own_ref
  88.5 1.9 %collective-permute-start.3 = (bf16[4,128,16,128]{3,2,1,0:T(8,128)(2,1)S(1)}, bf16[4,128,16,128]{3,2,1,0:T(8,128)(2,1)}, u32[]{:S(2)}, u32[]{:S(2)}) collective-permute-start(bf16[4,128,16,128]{3,2,1,0:T(8,128)(2,1)S(1)} %pad_maximum_fusion.own_ref), channel_id=1, source_target_pairs={{0,64},{1,65},{2,66},{3,67},{4,68},{5,69},{6,70},{7,71},{8,72},{9,... | collective-permute-start | bytes 6291464 | tf_op jit(solution)/shard_map/ppermute | solution.py:260
  90.5 0.2 fusion.15
  90.7 0.8 slice.58
  91.7 0.2 select_reduce_fusion.1
  92.2 2.5 %collective-permute-done.3.other_ref = bf16[4,128,16,128]{3,2,1,0:T(8,128)(2,1)} collective-permute-done((bf16[4,128,16,128]{3,2,1,0:T(8,128)(2,1)S(1)}, bf16[4,128,16,128]{3,2,1,0:T(8,128)(2,1)}, u32[]{:S(2)}, u32[]{:S(2)}) %collective-permute-start.3) | collective-permute-done | bytes 2097184 | tf_op jit(solution)/shard_map/ppermute | solution.py:260
  94.7 2.2 %copy-done = bf16[128,16512]{1,0:T(8,128)(2,1)S(1)} copy-done((bf16[128,16512]{1,0:T(8,128)(2,1)S(1)}, bf16[128,16512]{1,0:T(8,128)(2,1)}, u32[]{:S(2)}) %copy-start) | copy-done | bytes 4227096
  96.9 11.3 %flows_and_grad.1 = (f32[128,384]{1,0:T(8,128)}, bf16[128,16384]{1,0:T(8,128)(2,1)S(1)}) custom-call(s32[1]{0:T(128)} %bitcast.core_ref, s32[128]{0:T(128)S(1)} %reshape.113.label_ref, bf16[128,16512]{1,0:T(8,128)(2,1)S(1)} %copy-done, bf16[4,128,16,128]{3,2,1,0:T(8,128)(2,1)S(1)} %pad_maximum_fusion.own_ref, ...), custom_call_target="tpu_custom_call" | custom-call | tf_op jit(solution)/shard_map/flows_and_grad/pallas_call | solution.py:203
  108.2 2.0 %copy-done.1 = bf16[128,16384]{1,0:T(8,128)(2,1)} copy-done((bf16[128,16384]{1,0:T(8,128)(2,1)}, bf16[128,16384]{1,0:T(8,128)(2,1)S(1)}, u32[]{:S(2)}) %copy-start.1) | copy-done | bytes 4194328
  110.2 39.4 %reduce-scatter.2.cloned.1.call-done = bf16[16,16384]{1,0:T(8,128)(2,1)} async-done(((bf16[128,16384]{1,0:T(8,128)(2,1)}), bf16[16,16384]{1,0:T(8,128)(2,1)}) %reduce-scatter.2.cloned.1.call-update) | async-done | bytes 524304 | tf_op jit(solution)/shard_map/reduce_scatter | solution.py:287
  149.6 1.4 reshape.110
  150.9 20.5 %all_to_all.17 = bf16[8,2,16384]{2,1,0:T(2,128)(2,1)S(1)} all-to-all(bf16[8,2,16384]{2,1,0:T(2,128)(2,1)S(1)} %reshape.110), channel_id=1, replica_groups={{0,1,2,3,4,5,6,7},{8,9,10,11,12,13,14,15},{16,17,18,19,20,21,22,23},{24..., dimensions={0} | all-to-all | bytes 1048576 | tf_op jit(solution)/shard_map/all_to_all | solution.py:290
  171.4 0.9 fusion.17
  (35 shorter events, 0.9 us)
Async XLA Ops:
  7.2 83.6 %all-gather.2.cloned.1.call-start = ((), (), s32[]{:S(2)}) async-start(), calls=%async_computation.4 | async-start | bytes 4755456 | tf_op jit(solution)/shard_map/all_gather | solution.py:250
  40.0 37.8 %copy-start.5 = (s32[384]{0:T(512)S(1)}, s32[384]{0:T(512)}, u32[]{:S(2)}) copy-start(s32[384]{0:T(512)} %param.11) | copy-start | bytes 4612
  40.9 108.7 %reduce-scatter.2.cloned.1.call-start = ((), (), s32[]{:S(2)}) async-start(), calls=%async_computation.5 | async-start | bytes 4718592 | tf_op jit(solution)/shard_map/reduce_scatter | solution.py:287
  63.0 12.1 %collective-permute-start.1 = (bf16[128,16,128]{2,1,0:T(8,128)(2,1)S(1)}, bf16[128,16,128]{2,1,0:T(8,128)(2,1)S(1)}, u32[]{:S(2)}, u32[]{:S(2)}) collective-permute-start(bf16[128,16,128]{2,1,0:T(8,128)(2,1)S(1)} %bitcast.71), channel_id=1, source_target_pairs={{0,128},{1,129},{2,130},{3,131},{4,132},{5,133},{6,134},{7,135},{8... | collective-permute-start | bytes 1572872 | tf_op jit(solution)/shard_map/ppermute | solution.py:256
  65.4 12.4 %collective-permute-start = (bf16[128,16,128]{2,1,0:T(8,128)(2,1)S(1)}, bf16[128,16,128]{2,1,0:T(8,128)(2,1)S(1)}, u32[]{:S(2)}, u32[]{:S(2)}) collective-permute-start(bf16[128,16,128]{2,1,0:T(8,128)(2,1)S(1)} %bitcast.72), channel_id=1, source_target_pairs={{0,384},{1,385},{2,386},{3,387},{4,388},{5,389},{6,390},{7,391},{8... | collective-permute-start | bytes 1572872 | tf_op jit(solution)/shard_map/ppermute | solution.py:257
  75.1 11.1 %collective-permute-start.2 = (bf16[128,16,128]{2,1,0:T(8,128)(2,1)S(1)}, bf16[128,16,128]{2,1,0:T(8,128)(2,1)S(1)}, u32[]{:S(2)}, u32[]{:S(2)}) collective-permute-start(bf16[128,16,128]{2,1,0:T(8,128)(2,1)S(1)} %collective-permute-done.1), channel_id=1, source_target_pairs={{0,128},{1,129},{2,130},{3,131},{4,132},{5,133},{6,134},{7,135},{8... | collective-permute-start | bytes 1572872 | tf_op jit(solution)/shard_map/ppermute | solution.py:258
  77.8 8.4 %copy-start.3 = (bf16[128,16,128]{2,1,0:T(8,128)(2,1)}, bf16[128,16,128]{2,1,0:T(8,128)(2,1)S(1)}, u32[]{:S(2)}) copy-start(bf16[128,16,128]{2,1,0:T(8,128)(2,1)S(1)} %collective-permute-done) | copy-start | bytes 1572868
  86.2 0.8 copy-start.4
  87.0 7.7 %copy-start.2 = (bf16[128,384]{1,0:T(8,128)(2,1)S(1)}, bf16[128,384]{1,0:T(8,128)(2,1)}, u32[]{:S(2)}) copy-start(bf16[128,384]{1,0:T(8,128)(2,1)} %pred_ref.1) | copy-start | bytes 294916
  88.5 6.2 %collective-permute-start.3 = (bf16[4,128,16,128]{3,2,1,0:T(8,128)(2,1)S(1)}, bf16[4,128,16,128]{3,2,1,0:T(8,128)(2,1)}, u32[]{:S(2)}, u32[]{:S(2)}) collective-permute-start(bf16[4,128,16,128]{3,2,1,0:T(8,128)(2,1)S(1)} %pad_maximum_fusion.own_ref), channel_id=1, source_target_pairs={{0,64},{1,65},{2,66},{3,67},{4,68},{5,69},{6,70},{7,71},{8,72},{9,... | collective-permute-start | bytes 6291464 | tf_op jit(solution)/shard_map/ppermute | solution.py:260
  94.7 2.2 %copy-start = (bf16[128,16512]{1,0:T(8,128)(2,1)S(1)}, bf16[128,16512]{1,0:T(8,128)(2,1)}, u32[]{:S(2)}) copy-start(bf16[128,16512]{1,0:T(8,128)(2,1)} %all-gather.2.cloned.1.call-done.x_hbm) | copy-start | bytes 12681220
  108.2 2.0 %copy-start.1 = (bf16[128,16384]{1,0:T(8,128)(2,1)}, bf16[128,16384]{1,0:T(8,128)(2,1)S(1)}, u32[]{:S(2)}) copy-start(bf16[128,16384]{1,0:T(8,128)(2,1)S(1)} %get-tuple-element.4) | copy-start | bytes 12582916
Sparse Core Ops, SparseCore 0:
  41.0 43.9 all-gather.1
  110.3 39.2 reduce-scatter.1

commit v7 on v6

--- a/solution.py
+++ b/solution.py
@@ -107,7 +107,7 @@
 
 
 def core_kernel(
-    core_ref, label_ref, x_hbm, own_ref, other_ref, pred_ref, limit_ref, rowp_ref, colp_ref,
+    core_ref, label_ref, x_hbm, own_ref, own_far_ref, other_ref, other_far_ref, pred_ref, limit_ref, rowp_ref, colp_ref,
     flows_ref, c_hbm, x_ref, c_ref, acc_ref, g_ref, in_sem, out_sem,
 ):
     sources = label_ref.shape[0] // CAP
@@ -133,7 +133,11 @@
 
     def tile(here, there):
         return jnp.concatenate(
-            [own_ref[d, here] for d in range(NX)] + [other_ref[d, there] for d in range(NX)], axis=0
+            [own_ref[d, here] for d in range(NX - 1)]
+            + [own_far_ref[here]]
+            + [other_ref[d, there] for d in range(NX - 1)]
+            + [other_far_ref[there]],
+            axis=0,
         )
 
     acc_ref[...] = jnp.zeros_like(acc_ref)
@@ -195,18 +199,18 @@
         leave(k).wait()
 
 
-def core_call(core, labels, x, own, other, pred, limit, rowp, colp, nbus):
+def core_call(core, labels, x, own, own_far, other, other_far, pred, limit, rowp, colp, nbus):
     rows, lines = pred.shape
     smem = pl.BlockSpec(memory_space=pltpu.SMEM)
     vmem = pl.BlockSpec(memory_space=pltpu.VMEM)
-    anywhere = pl.BlockSpec(memory_space=pl.ANY)
+    anywhere = pl.BlockSpec(memory_space=pltpu.HBM)
     return pl.pallas_call(
         core_kernel,
         out_shape=(
             jax.ShapeDtypeStruct((rows, lines), F32),
             jax.ShapeDtypeStruct((rows, nbus), BF16),
         ),
-        in_specs=[smem, smem, anywhere] + [vmem] * 6,
+        in_specs=[smem, smem, anywhere] + [vmem] * 8,
         out_specs=(vmem, anywhere),
         scratch_shapes=[
             pltpu.VMEM((rows, nbus), BF16),
@@ -216,9 +220,9 @@
             pltpu.SemaphoreType.DMA((CHUNKS,)),
             pltpu.SemaphoreType.DMA((CHUNKS,)),
         ],
-        compiler_params=pltpu.CompilerParams(vmem_limit_bytes=32 * 1024 * 1024),
+        compiler_params=pltpu.CompilerParams(vmem_limit_bytes=50 * 1024 * 1024),
         name="flows_and_grad",
-    )(core.reshape(1), labels, x, own, other, pred, limit, rowp, colp)
+    )(core.reshape(1), labels, x, own, own_far, other, other_far, pred, limit, rowp, colp)
 
 
 def add_up(parts):
@@ -253,11 +257,19 @@
     mine = lax.all_to_all(
         slots.swapaxes(0, 1), AXES, split_axis=0, concat_axis=0, tiled=True, axis_index_groups=MAJOR
     ).reshape((buses * CAP,) + tile_values.shape[1:])
+    half_slots = mine.shape[0] // 2
+    from_above = lax.ppermute(mine, AXES, X_DOWN)
     from_below = lax.ppermute(mine, AXES, X_UP)
-    from_above = lax.ppermute(mine, AXES, X_DOWN)
-    from_far = lax.ppermute(from_below, AXES, X_UP)
-    own = jnp.stack([mine, from_above, from_far, from_below])
-    other = lax.ppermute(own, AXES, CORE_SWAP)
+    far = jnp.concatenate(
+        [
+            lax.ppermute(from_below[:half_slots], AXES, X_UP),
+            lax.ppermute(from_above[half_slots:], AXES, X_DOWN),
+        ],
+        axis=0,
+    )
+    near3 = jnp.stack([mine, from_above, from_below])
+    other3 = lax.ppermute(near3, AXES, CORE_SWAP)
+    other_far = lax.ppermute(far, AXES, CORE_SWAP)
 
     tags = x_all[:, nbus:].astype(jnp.int32).reshape(buses, rows_here, TILE)
     line = tags[:, 0, :]
@@ -277,11 +289,13 @@
     swapped = ((col // 2) % 8 * 8 + col // 16) * 2 + col % 2
     rowp = (row == jnp.where(core == 0, col, swapped)).astype(BF16)
     chunk = row // 16
-    line_of = (((chunk % NX + x_here) % NX) * NC + jnp.where(chunk < NX, core, 1 - core)) * 16 + row % 16
+    piece = chunk % NX
+    offset = jnp.where(piece < 2, piece, 5 - piece)
+    line_of = (((offset + x_here) % NX) * NC + jnp.where(chunk < NX, core, 1 - core)) * 16 + row % 16
     colp = (col == line_of).astype(BF16)
 
     flows, contrib = core_call(
-        core, labels, x_all, own, other, flow_pred, line_limit.reshape(1, -1), rowp, colp, nbus
+        core, labels, x_all, near3, far, other3, other_far, flow_pred, line_limit.reshape(1, -1), rowp, colp, nbus
     )
 
     half = lax.psum_scatter(

time: 180 us -> 178 us (0.989)
  blocking collectives: 72 us -> 50 us
  starting transfers between devices: 10.4 us -> 22.8 us
  waiting for transfers between devices: 56.6 us -> 68.3 us
  local copies, waits for them, and re-layouts: 7.99 us -> 3.94 us
    all_to_all x1 -> x0, blocking collectives: 22 us -> none  [per_device(): lax.all_to_all(slots.swapaxes(0, 1), AXES, split_axis=0, concat_axis=0, t...]
    all_to_all x0 -> x1, waiting for transfers between devices: none -> 15.9 us  [per_device(): lax.all_to_all(slots.swapaxes(0, 1), AXES, split_axis=0, concat_axis=0, t...]
    all_to_all x0 -> x1, starting transfers between devices: none -> 7.1 us  [per_device(): lax.all_to_all(slots.swapaxes(0, 1), AXES, split_axis=0, concat_axis=0, t...]
    ppermute x2 -> x4, starting transfers between devices: 4.53 us -> 9.82 us  [the longest x1 3.56 us: per_device(): lax.ppermute(from_above[half_slots:], AXES, X_DOWN)]
    unnamed x13 -> x6, local copies, waits for them, and re-layouts: 5.31 us -> 0.38 us
    ppermute x2 -> x4, waiting for transfers between devices: 10.9 us -> 8.57 us  [the longest x1 8.17 us: per_device(): lax.ppermute(from_above[half_slots:], AXES, X_DOWN)]
    reduce_scatter x1, waiting for transfers between devices: 39.4 us -> 37.2 us  [per_device(): lax.psum_scatter(contrib, AXES, scatter_dimension=0, tiled=True, axis_ind...]
  transfers between devices with their start and end apart: 6 -> 9, of which waited for: 4 -> 5; matrix products, arithmetic and copies ran while one was open for 2% -> 2% of each run, Pallas kernels for 0% -> 0%
where the time goes in v7:
time: 178 us; the launch traced here: 177 us
  waiting for transfers between devices  68.3 us (38%)
  blocking collectives  50 us (28%)
  starting transfers between devices  22.8 us (13%)
  Pallas kernels  15 us (8%)
  between operations  14.3 us (8%)
  local copies, waits for them, and re-layouts  3.94 us (2%)
  other arithmetic  2.5 us (1%)
    reduce_scatter x1, waiting for transfers between devices, per_device(): lax.psum_scatter(contrib, AXES, scatter_dimension=0, tiled=True, axis_ind...  37.2 us
    all_to_all x1, blocking collectives, per_device(): lax.all_to_all(packed, AXES, split_axis=0, concat_axis=0, tiled=True, axi...  29.6 us
    all_to_all x1, blocking collectives, per_device(): lax.all_to_all(half.reshape(8, rows_here, nbus), AXES, split_axis=0, conc...  20.5 us
    all_to_all x1, waiting for transfers between devices, per_device(): lax.all_to_all(slots.swapaxes(0, 1), AXES, split_axis=0, concat_axis=0, t...  15.9 us
    pallas_call x1, Pallas kernels, core_call(): pl.pallas_call(core_kernel, out_shape=(jax.ShapeDtypeStruct((rows, lines)...  12.4 us
    ppermute x1, waiting for transfers between devices, per_device(): lax.ppermute(from_above[half_slots:], AXES, X_DOWN)  8.17 us
    all_to_all x1, starting transfers between devices, per_device(): lax.all_to_all(slots.swapaxes(0, 1), AXES, split_axis=0, concat_axis=0, t...  7.1 us
    ppermute x1, waiting for transfers between devices, per_device(): from_below = lax.ppermute(mine, AXES, X_UP)  6.53 us
  transfers between devices with their start and end apart: 9, of which 5 were waited for; matrix products, arithmetic and copies ran while one was open for 2% of the time, Pallas kernels for 0%

profile of v7, /device:TPU:6, one launch (start us, length us, event | category | flops | bytes accessed | tf_op | source)
XLA Modules:
  0.0 177.0 jit_solution(15118097297190792405)
XLA Ops:
  7.2 2.6 %pack.1 = bf16[8,528,128]{2,1,0:T(8,128)(2,1)} custom-call(s32[1]{0:T(128)} %bitcast.core_ref, s32[64]{0:T(128)} %line_ref.1, s32[1,64]{1,0:T(1,128)} %bitcast.80, s32[1,64]{1,0:T(1,128)} %bitcast.82, bf16[64,16,128]{2,1,0:T(8,128)(2,1)} %tiles_ref.1, bf16[256,128]{1,0:T(8,128)(2,1)} %bitcast.78), custom_call_target="tpu_custom_call" | custom-call | tf_op jit(solution)/shard_map/pack/pallas_call | solution.py:91
  9.9 29.6 %all_to_all.15 = bf16[8,528,128]{2,1,0:T(8,128)(2,1)S(1)} all-to-all(bf16[8,528,128]{2,1,0:T(8,128)(2,1)} %pack.1), channel_id=1, replica_groups={{0,1,2,3,4,5,6,7},{8,9,10,11,12,13,14,15},{16,17,18,19,20,21,22,23},{24..., dimensions={0} | all-to-all | bytes 2162688 | tf_op jit(solution)/shard_map/all_to_all | solution.py:248
  39.7 0.3 copy.22
  40.0 0.8 pad_maximum_fusion.1
  40.9 0.9 copy.23
  41.7 7.1 %all-to-all-start.1 = ((bf16[8,8,2,16,128]{4,3,2,1,0:T(8,128)(2,1)}), bf16[8,8,2,16,128]{4,3,2,1,0:T(8,128)(2,1)S(1)}, u32[]{:S(2)}, u32[]{:S(2)}) async-start(bf16[8,8,2,16,128]{4,3,2,1,0:T(8,128)(2,1)} %bitcast.64), calls=%async_computation.1 | async-start | bytes 1048576 | tf_op jit(solution)/shard_map/all_to_all | solution.py:257
  48.9 15.9 %all-to-all-done.1 = bf16[8,8,2,16,128]{4,3,2,1,0:T(8,128)(2,1)S(1)} async-done(((bf16[8,8,2,16,128]{4,3,2,1,0:T(8,128)(2,1)}), bf16[8,8,2,16,128]{4,3,2,1,0:T(8,128)(2,1)S(1)}, u32[]{:S(2)}, u32[]{:S(2)}) %all-to-all-start.1) | async-done | bytes 524320 | tf_op jit(solution)/shard_map/all_to_all | solution.py:257
  64.9 2.4 %collective-permute-start.1 = (bf16[128,16,128]{2,1,0:T(8,128)(2,1)S(1)}, bf16[128,16,128]{2,1,0:T(8,128)(2,1)S(1)}, u32[]{:S(2)}, u32[]{:S(2)}) collective-permute-start(bf16[128,16,128]{2,1,0:T(8,128)(2,1)S(1)} %bitcast.67), channel_id=1, source_target_pairs={{0,128},{1,129},{2,130},{3,131},{4,132},{5,133},{6,134},{7,135},{8... | collective-permute-start | bytes 1572872 | tf_op jit(solution)/shard_map/ppermute | solution.py:262
  67.2 3.5 %collective-permute-start = (bf16[128,16,128]{2,1,0:T(8,128)(2,1)S(1)}, bf16[128,16,128]{2,1,0:T(8,128)(2,1)S(1)}, u32[]{:S(2)}, u32[]{:S(2)}) collective-permute-start(bf16[128,16,128]{2,1,0:T(8,128)(2,1)S(1)} %bitcast.68), channel_id=1, source_target_pairs={{0,384},{1,385},{2,386},{3,387},{4,388},{5,389},{6,390},{7,391},{8... | collective-permute-start | bytes 1572872 | tf_op jit(solution)/shard_map/ppermute | solution.py:261
  70.8 6.5 %collective-permute-done.1 = bf16[128,16,128]{2,1,0:T(8,128)(2,1)S(1)} collective-permute-done((bf16[128,16,128]{2,1,0:T(8,128)(2,1)S(1)}, bf16[128,16,128]{2,1,0:T(8,128)(2,1)S(1)}, u32[]{:S(2)}, u32[]{:S(2)}) %collective-permute-start.1) | collective-permute-done | bytes 524320 | tf_op jit(solution)/shard_map/ppermute | solution.py:262
  77.3 2.3 %collective-permute-start.2 = (bf16[64,16,128]{2,1,0:T(8,128)(2,1)S(1)}, bf16[64,16,128]{2,1,0:T(8,128)(2,1)S(1)}, u32[]{:S(2)}, u32[]{:S(2)}) collective-permute-start(bf16[64,16,128]{2,1,0:T(8,128)(2,1)S(1)} %slice.70), channel_id=1, source_target_pairs={{0,128},{1,129},{2,130},{3,131},{4,132},{5,133},{6,134},{7,135},{8... | collective-permute-start | bytes 786440 | tf_op jit(solution)/shard_map/ppermute | solution.py:265
  79.8 2.1 %collective-permute-start.4 = (bf16[3,128,16,128]{3,2,1,0:T(8,128)(2,1)S(1)}, bf16[3,128,16,128]{3,2,1,0:T(8,128)(2,1)}, u32[]{:S(2)}, u32[]{:S(2)}) collective-permute-start(bf16[3,128,16,128]{3,2,1,0:T(8,128)(2,1)S(1)} %pad_maximum_fusion.own_ref), channel_id=1, source_target_pairs={{0,64},{1,65},{2,66},{3,67},{4,68},{5,69},{6,70},{7,71},{8,72},{9,... | collective-permute-start | bytes 4718600 | tf_op jit(solution)/shard_map/ppermute | solution.py:271
  81.9 0.2 fusion.15
  82.1 3.6 %collective-permute-start.3 = (bf16[64,16,128]{2,1,0:T(8,128)(2,1)S(1)}, bf16[64,16,128]{2,1,0:T(8,128)(2,1)S(1)}, u32[]{:S(2)}, u32[]{:S(2)}) collective-permute-start(bf16[64,16,128]{2,1,0:T(8,128)(2,1)S(1)} %slice.71), channel_id=1, source_target_pairs={{0,384},{1,385},{2,386},{3,387},{4,388},{5,389},{6,390},{7,391},{8... | collective-permute-start | bytes 786440 | tf_op jit(solution)/shard_map/ppermute | solution.py:266
  85.7 8.2 %collective-permute-done.3 = bf16[64,16,128]{2,1,0:T(8,128)(2,1)S(1)} collective-permute-done((bf16[64,16,128]{2,1,0:T(8,128)(2,1)S(1)}, bf16[64,16,128]{2,1,0:T(8,128)(2,1)S(1)}, u32[]{:S(2)}, u32[]{:S(2)}) %collective-permute-start.3) | collective-permute-done | bytes 262176 | tf_op jit(solution)/shard_map/ppermute | solution.py:266
  94.0 1.9 %collective-permute-start.5 = (bf16[128,16,128]{2,1,0:T(8,128)(2,1)S(1)}, bf16[128,16,128]{2,1,0:T(8,128)(2,1)S(1)}, u32[]{:S(2)}, u32[]{:S(2)}) collective-permute-start(bf16[128,16,128]{2,1,0:T(8,128)(2,1)S(1)} %constant_dynamic-update-slice_fusion.own_far_ref), channel_id=1, source_target_pairs={{0,64},{1,65},{2,66},{3,67},{4,68},{5,69},{6,70},{7,71},{8,72},{9,... | collective-permute-start | bytes 1572872 | tf_op jit(solution)/shard_map/ppermute | solution.py:272
  95.9 0.8 slice.66
  96.9 0.2 select_reduce_fusion.1
  97.4 0.4 collective-permute-done.5.other_far_ref
  97.8 12.4 %flows_and_grad.1 = (f32[128,384]{1,0:T(8,128)}, bf16[128,16384]{1,0:T(8,128)(2,1)}) custom-call(s32[1]{0:T(128)} %bitcast.core_ref, s32[128]{0:T(128)S(1)} %reshape.113.label_ref, bf16[128,16512]{1,0:T(8,128)(2,1)} %all-gather.2.cloned.1.call-done.x_hbm, bf16[3,128,16,128]{3,2,1,0:T(8,128)(2,1)S(1)} %pad_maximum_fusion.own_ref, ...), custom_call_target="tpu_custom_call" | custom-call | tf_op jit(solution)/shard_map/flows_and_grad/pallas_call | solution.py:207
  110.2 37.2 %reduce-scatter.2.cloned.1.call-done = bf16[16,16384]{1,0:T(8,128)(2,1)} async-done(((bf16[128,16384]{1,0:T(8,128)(2,1)}), bf16[16,16384]{1,0:T(8,128)(2,1)}) %reduce-scatter.2.cloned.1.call-update) | async-done | bytes 524304 | tf_op jit(solution)/shard_map/reduce_scatter | solution.py:301
  147.4 1.4 reshape.110
  148.8 20.5 %all_to_all.16 = bf16[8,2,16384]{2,1,0:T(2,128)(2,1)S(1)} all-to-all(bf16[8,2,16384]{2,1,0:T(2,128)(2,1)S(1)} %reshape.110), channel_id=1, replica_groups={{0,1,2,3,4,5,6,7},{8,9,10,11,12,13,14,15},{16,17,18,19,20,21,22,23},{24..., dimensions={0} | all-to-all | bytes 1048576 | tf_op jit(solution)/shard_map/all_to_all | solution.py:304
  169.2 0.9 fusion.17
  (36 shorter events, 1.1 us)
Async XLA Ops:
  7.2 88.7 %all-gather.2.cloned.1.call-start = ((), (), s32[]{:S(2)}) async-start(), calls=%async_computation.4 | async-start | bytes 4755456 | tf_op jit(solution)/shard_map/all_gather | solution.py:254
  41.7 23.1 %all-to-all-start.1 = ((bf16[8,8,2,16,128]{4,3,2,1,0:T(8,128)(2,1)}), bf16[8,8,2,16,128]{4,3,2,1,0:T(8,128)(2,1)S(1)}, u32[]{:S(2)}, u32[]{:S(2)}) async-start(bf16[8,8,2,16,128]{4,3,2,1,0:T(8,128)(2,1)} %bitcast.64), calls=%async_computation.1 | async-start | bytes 1048576 | tf_op jit(solution)/shard_map/all_to_all | solution.py:257
  48.8 98.6 %reduce-scatter.2.cloned.1.call-start = ((), (), s32[]{:S(2)}) async-start(), calls=%async_computation.5 | async-start | bytes 4718592 | tf_op jit(solution)/shard_map/reduce_scatter | solution.py:301
  64.9 12.4 %collective-permute-start.1 = (bf16[128,16,128]{2,1,0:T(8,128)(2,1)S(1)}, bf16[128,16,128]{2,1,0:T(8,128)(2,1)S(1)}, u32[]{:S(2)}, u32[]{:S(2)}) collective-permute-start(bf16[128,16,128]{2,1,0:T(8,128)(2,1)S(1)} %bitcast.67), channel_id=1, source_target_pairs={{0,128},{1,129},{2,130},{3,131},{4,132},{5,133},{6,134},{7,135},{8... | collective-permute-start | bytes 1572872 | tf_op jit(solution)/shard_map/ppermute | solution.py:262
  67.2 12.4 %collective-permute-start = (bf16[128,16,128]{2,1,0:T(8,128)(2,1)S(1)}, bf16[128,16,128]{2,1,0:T(8,128)(2,1)S(1)}, u32[]{:S(2)}, u32[]{:S(2)}) collective-permute-start(bf16[128,16,128]{2,1,0:T(8,128)(2,1)S(1)} %bitcast.68), channel_id=1, source_target_pairs={{0,384},{1,385},{2,386},{3,387},{4,388},{5,389},{6,390},{7,391},{8... | collective-permute-start | bytes 1572872 | tf_op jit(solution)/shard_map/ppermute | solution.py:261
  77.3 8.4 %collective-permute-start.2 = (bf16[64,16,128]{2,1,0:T(8,128)(2,1)S(1)}, bf16[64,16,128]{2,1,0:T(8,128)(2,1)S(1)}, u32[]{:S(2)}, u32[]{:S(2)}) collective-permute-start(bf16[64,16,128]{2,1,0:T(8,128)(2,1)S(1)} %slice.70), channel_id=1, source_target_pairs={{0,128},{1,129},{2,130},{3,131},{4,132},{5,133},{6,134},{7,135},{8... | collective-permute-start | bytes 786440 | tf_op jit(solution)/shard_map/ppermute | solution.py:265
  79.6 6.1 %copy-start.1 = (s32[384]{0:T(512)S(1)}, s32[384]{0:T(512)}, u32[]{:S(2)}) copy-start(s32[384]{0:T(512)} %param.11) | copy-start | bytes 4612
  79.8 18.0 %copy-start = (bf16[128,384]{1,0:T(8,128)(2,1)S(1)}, bf16[128,384]{1,0:T(8,128)(2,1)}, u32[]{:S(2)}) copy-start(bf16[128,384]{1,0:T(8,128)(2,1)} %pred_ref.1) | copy-start | bytes 294916
  79.8 17.9 %collective-permute-start.4 = (bf16[3,128,16,128]{3,2,1,0:T(8,128)(2,1)S(1)}, bf16[3,128,16,128]{3,2,1,0:T(8,128)(2,1)}, u32[]{:S(2)}, u32[]{:S(2)}) collective-permute-start(bf16[3,128,16,128]{3,2,1,0:T(8,128)(2,1)S(1)} %pad_maximum_fusion.own_ref), channel_id=1, source_target_pairs={{0,64},{1,65},{2,66},{3,67},{4,68},{5,69},{6,70},{7,71},{8,72},{9,... | collective-permute-start | bytes 4718600 | tf_op jit(solution)/shard_map/ppermute | solution.py:271
  82.1 11.8 %collective-permute-start.3 = (bf16[64,16,128]{2,1,0:T(8,128)(2,1)S(1)}, bf16[64,16,128]{2,1,0:T(8,128)(2,1)S(1)}, u32[]{:S(2)}, u32[]{:S(2)}) collective-permute-start(bf16[64,16,128]{2,1,0:T(8,128)(2,1)S(1)} %slice.71), channel_id=1, source_target_pairs={{0,384},{1,385},{2,386},{3,387},{4,388},{5,389},{6,390},{7,391},{8... | collective-permute-start | bytes 786440 | tf_op jit(solution)/shard_map/ppermute | solution.py:266
  94.0 3.8 %collective-permute-start.5 = (bf16[128,16,128]{2,1,0:T(8,128)(2,1)S(1)}, bf16[128,16,128]{2,1,0:T(8,128)(2,1)S(1)}, u32[]{:S(2)}, u32[]{:S(2)}) collective-permute-start(bf16[128,16,128]{2,1,0:T(8,128)(2,1)S(1)} %constant_dynamic-update-slice_fusion.own_far_ref), channel_id=1, source_target_pairs={{0,64},{1,65},{2,66},{3,67},{4,68},{5,69},{6,70},{7,71},{8,72},{9,... | collective-permute-start | bytes 1572872 | tf_op jit(solution)/shard_map/ppermute | solution.py:272
Sparse Core Ops, SparseCore 0:
  41.0 44.9 all-gather.1
  110.3 37.0 reduce-scatter.1

commit v8 on v7

--- a/solution.py
+++ b/solution.py
@@ -16,6 +16,7 @@
 CAP = 2
 CODE_ROWS = 16
 CHUNKS = 8
+AHEAD = 2
 F32 = jnp.float32
 BF16 = jnp.bfloat16
 
@@ -122,7 +123,7 @@
         lanes = pl.ds(pl.multiple_of(k * width, width), width)
         return pltpu.make_async_copy(c_ref.at[:, lanes], c_hbm.at[:, lanes], out_sem.at[k])
 
-    for k in range(CHUNKS):
+    for k in range(AHEAD):
         bring(k).start()
 
     first_core = core_ref[0] == 0
@@ -144,6 +145,11 @@
 
     def forward(k, carry):
         bring(k).wait()
+
+        @pl.when(k + AHEAD < CHUNKS)
+        def _():
+            bring(k + AHEAD).start()
+
         for i in range(step):
             here, there = places(k * step + i)
             for r in range(CAP):
@@ -257,16 +263,9 @@
     mine = lax.all_to_all(
         slots.swapaxes(0, 1), AXES, split_axis=0, concat_axis=0, tiled=True, axis_index_groups=MAJOR
     ).reshape((buses * CAP,) + tile_values.shape[1:])
-    half_slots = mine.shape[0] // 2
+    from_below = lax.ppermute(mine, AXES, X_UP)
     from_above = lax.ppermute(mine, AXES, X_DOWN)
-    from_below = lax.ppermute(mine, AXES, X_UP)
-    far = jnp.concatenate(
-        [
-            lax.ppermute(from_below[:half_slots], AXES, X_UP),
-            lax.ppermute(from_above[half_slots:], AXES, X_DOWN),
-        ],
-        axis=0,
-    )
+    far = lax.ppermute(from_below, AXES, X_UP)
     near3 = jnp.stack([mine, from_above, from_below])
     other3 = lax.ppermute(near3, AXES, CORE_SWAP)
     other_far = lax.ppermute(far, AXES, CORE_SWAP)

time: 178 us -> 181 us (1.017)
  waiting for transfers between devices: 68.3 us -> 76 us
  starting transfers between devices: 22.8 us -> 19 us
    ppermute x2 -> x1, waiting for transfers between devices: 8.17 us -> 13.8 us  [per_device(): far = lax.ppermute(from_below, AXES, X_UP)]
    ppermute x2 -> x1, starting transfers between devices: 5.84 us -> 2.19 us  [per_device(): far = lax.ppermute(from_below, AXES, X_UP)]
    ppermute x1, waiting for transfers between devices: 0.01 us -> 3.59 us  [per_device(): from_above = lax.ppermute(mine, AXES, X_DOWN)]
  transfers between devices with their start and end apart: 9 -> 8, of which waited for: 5 -> 6; matrix products, arithmetic and copies ran while one was open for 2% -> 1% of each run, Pallas kernels for 0% -> 0%
where the time goes in v8:
time: 181 us
  waiting for transfers between devices  76 us (42%)
  blocking collectives  50.1 us (28%)
  starting transfers between devices  19 us (10%)
  Pallas kernels  14.9 us (8%)
  between operations  14.3 us (8%)
  local copies, waits for them, and re-layouts  3.84 us (2%)
  other arithmetic  2.5 us (1%)
    reduce_scatter x1, waiting for transfers between devices, per_device(): lax.psum_scatter(contrib, AXES, scatter_dimension=0, tiled=True, axis_ind...  37.1 us
    all_to_all x1, blocking collectives, per_device(): lax.all_to_all(packed, AXES, split_axis=0, concat_axis=0, tiled=True, axi...  29.6 us
    all_to_all x1, blocking collectives, per_device(): lax.all_to_all(half.reshape(8, rows_here, nbus), AXES, split_axis=0, conc...  20.5 us
    all_to_all x1, waiting for transfers between devices, per_device(): lax.all_to_all(slots.swapaxes(0, 1), AXES, split_axis=0, concat_axis=0, t...  15.9 us
    ppermute x1, waiting for transfers between devices, per_device(): far = lax.ppermute(from_below, AXES, X_UP)  13.8 us
    pallas_call x1, Pallas kernels, core_call(): pl.pallas_call(core_kernel, out_shape=(jax.ShapeDtypeStruct((rows, lines)...  12.3 us
    all_to_all x1, starting transfers between devices, per_device(): lax.all_to_all(slots.swapaxes(0, 1), AXES, split_axis=0, concat_axis=0, t...  7.1 us
    ppermute x1, waiting for transfers between devices, per_device(): from_below = lax.ppermute(mine, AXES, X_UP)  5.16 us
  transfers between devices with their start and end apart: 8, of which 6 were waited for; matrix products, arithmetic and copies ran while one was open for 1% of the time, Pallas kernels for 0%

profile of v8, /device:TPU:6, one launch (start us, length us, event | category | flops | bytes accessed | tf_op | source)
XLA Modules:
  0.0 180.7 jit_solution(13180182848360531748)
XLA Ops:
  7.2 2.6 %pack.1 = bf16[8,528,128]{2,1,0:T(8,128)(2,1)} custom-call(s32[1]{0:T(128)} %bitcast.core_ref, s32[64]{0:T(128)} %line_ref.1, s32[1,64]{1,0:T(1,128)} %bitcast.80, s32[1,64]{1,0:T(1,128)} %bitcast.82, bf16[64,16,128]{2,1,0:T(8,128)(2,1)} %tiles_ref.1, bf16[256,128]{1,0:T(8,128)(2,1)} %bitcast.78), custom_call_target="tpu_custom_call" | custom-call | tf_op jit(solution)/shard_map/pack/pallas_call | solution.py:92
  9.9 29.6 %all_to_all.15 = bf16[8,528,128]{2,1,0:T(8,128)(2,1)S(1)} all-to-all(bf16[8,528,128]{2,1,0:T(8,128)(2,1)} %pack.1), channel_id=1, replica_groups={{0,1,2,3,4,5,6,7},{8,9,10,11,12,13,14,15},{16,17,18,19,20,21,22,23},{24..., dimensions={0} | all-to-all | bytes 2162688 | tf_op jit(solution)/shard_map/all_to_all | solution.py:254
  39.7 0.3 copy.22
  40.0 0.8 pad_maximum_fusion.1
  40.9 0.9 copy.23
  41.7 7.1 %all-to-all-start.1 = ((bf16[8,8,2,16,128]{4,3,2,1,0:T(8,128)(2,1)}), bf16[8,8,2,16,128]{4,3,2,1,0:T(8,128)(2,1)S(1)}, u32[]{:S(2)}, u32[]{:S(2)}) async-start(bf16[8,8,2,16,128]{4,3,2,1,0:T(8,128)(2,1)} %bitcast.64), calls=%async_computation.1 | async-start | bytes 1048576 | tf_op jit(solution)/shard_map/all_to_all | solution.py:263
  48.9 15.9 %all-to-all-done.1 = bf16[8,8,2,16,128]{4,3,2,1,0:T(8,128)(2,1)S(1)} async-done(((bf16[8,8,2,16,128]{4,3,2,1,0:T(8,128)(2,1)}), bf16[8,8,2,16,128]{4,3,2,1,0:T(8,128)(2,1)S(1)}, u32[]{:S(2)}, u32[]{:S(2)}) %all-to-all-start.1) | async-done | bytes 524320 | tf_op jit(solution)/shard_map/all_to_all | solution.py:263
  64.9 2.4 %collective-permute-start.1 = (bf16[128,16,128]{2,1,0:T(8,128)(2,1)S(1)}, bf16[128,16,128]{2,1,0:T(8,128)(2,1)S(1)}, u32[]{:S(2)}, u32[]{:S(2)}) collective-permute-start(bf16[128,16,128]{2,1,0:T(8,128)(2,1)S(1)} %bitcast.67), channel_id=1, source_target_pairs={{0,128},{1,129},{2,130},{3,131},{4,132},{5,133},{6,134},{7,135},{8... | collective-permute-start | bytes 1572872 | tf_op jit(solution)/shard_map/ppermute | solution.py:266
  67.2 3.5 %collective-permute-start = (bf16[128,16,128]{2,1,0:T(8,128)(2,1)S(1)}, bf16[128,16,128]{2,1,0:T(8,128)(2,1)S(1)}, u32[]{:S(2)}, u32[]{:S(2)}) collective-permute-start(bf16[128,16,128]{2,1,0:T(8,128)(2,1)S(1)} %bitcast.68), channel_id=1, source_target_pairs={{0,384},{1,385},{2,386},{3,387},{4,388},{5,389},{6,390},{7,391},{8... | collective-permute-start | bytes 1572872 | tf_op jit(solution)/shard_map/ppermute | solution.py:267
  70.8 5.2 %collective-permute-done.1 = bf16[128,16,128]{2,1,0:T(8,128)(2,1)S(1)} collective-permute-done((bf16[128,16,128]{2,1,0:T(8,128)(2,1)S(1)}, bf16[128,16,128]{2,1,0:T(8,128)(2,1)S(1)}, u32[]{:S(2)}, u32[]{:S(2)}) %collective-permute-start.1) | collective-permute-done | bytes 524320 | tf_op jit(solution)/shard_map/ppermute | solution.py:266
  75.9 3.6 %collective-permute-done = bf16[128,16,128]{2,1,0:T(8,128)(2,1)S(1)} collective-permute-done((bf16[128,16,128]{2,1,0:T(8,128)(2,1)S(1)}, bf16[128,16,128]{2,1,0:T(8,128)(2,1)S(1)}, u32[]{:S(2)}, u32[]{:S(2)}) %collective-permute-start) | collective-permute-done | bytes 524320 | tf_op jit(solution)/shard_map/ppermute | solution.py:267
  79.7 1.9 %collective-permute-start.3 = (bf16[3,128,16,128]{3,2,1,0:T(8,128)(2,1)S(1)}, bf16[3,128,16,128]{3,2,1,0:T(8,128)(2,1)}, u32[]{:S(2)}, u32[]{:S(2)}) collective-permute-start(bf16[3,128,16,128]{3,2,1,0:T(8,128)(2,1)S(1)} %pad_maximum_fusion.own_ref), channel_id=1, source_target_pairs={{0,64},{1,65},{2,66},{3,67},{4,68},{5,69},{6,70},{7,71},{8,72},{9,... | collective-permute-start | bytes 4718600 | tf_op jit(solution)/shard_map/ppermute | solution.py:270
  81.6 2.2 %collective-permute-start.2 = (bf16[128,16,128]{2,1,0:T(8,128)(2,1)S(1)}, bf16[128,16,128]{2,1,0:T(8,128)(2,1)S(1)}, u32[]{:S(2)}, u32[]{:S(2)}) collective-permute-start(bf16[128,16,128]{2,1,0:T(8,128)(2,1)S(1)} %collective-permute-done.1), channel_id=1, source_target_pairs={{0,128},{1,129},{2,130},{3,131},{4,132},{5,133},{6,134},{7,135},{8... | collective-permute-start | bytes 1572872 | tf_op jit(solution)/shard_map/ppermute | solution.py:268
  83.9 0.2 fusion.15
  84.1 13.8 %collective-permute-done.2.own_far_ref = bf16[128,16,128]{2,1,0:T(8,128)(2,1)S(1)} collective-permute-done((bf16[128,16,128]{2,1,0:T(8,128)(2,1)S(1)}, bf16[128,16,128]{2,1,0:T(8,128)(2,1)S(1)}, u32[]{:S(2)}, u32[]{:S(2)}) %collective-permute-start.2) | collective-permute-done | bytes 524320 | tf_op jit(solution)/shard_map/ppermute | solution.py:268
  97.9 1.9 %collective-permute-start.4 = (bf16[128,16,128]{2,1,0:T(8,128)(2,1)S(1)}, bf16[128,16,128]{2,1,0:T(8,128)(2,1)S(1)}, u32[]{:S(2)}, u32[]{:S(2)}) collective-permute-start(bf16[128,16,128]{2,1,0:T(8,128)(2,1)S(1)} %collective-permute-done.2.own_far_ref), channel_id=1, source_target_pairs={{0,64},{1,65},{2,66},{3,67},{4,68},{5,69},{6,70},{7,71},{8,72},{9,... | collective-permute-start | bytes 1572872 | tf_op jit(solution)/shard_map/ppermute | solution.py:271
  99.8 0.8 slice.58
  100.8 0.2 select_reduce_fusion.1
  101.2 0.4 collective-permute-done.4.other_far_ref
  101.7 12.3 %flows_and_grad.1 = (f32[128,384]{1,0:T(8,128)}, bf16[128,16384]{1,0:T(8,128)(2,1)}) custom-call(s32[1]{0:T(128)} %bitcast.core_ref, s32[128]{0:T(128)S(1)} %reshape.113.label_ref, bf16[128,16512]{1,0:T(8,128)(2,1)} %all-gather.2.cloned.1.call-done.x_hbm, bf16[3,128,16,128]{3,2,1,0:T(8,128)(2,1)S(1)} %pad_maximum_fusion.own_ref, ...), custom_call_target="tpu_custom_call" | custom-call | tf_op jit(solution)/shard_map/flows_and_grad/pallas_call | solution.py:213
  114.0 37.1 %reduce-scatter.2.cloned.1.call-done = bf16[16,16384]{1,0:T(8,128)(2,1)} async-done(((bf16[128,16384]{1,0:T(8,128)(2,1)}), bf16[16,16384]{1,0:T(8,128)(2,1)}) %reduce-scatter.2.cloned.1.call-update) | async-done | bytes 524304 | tf_op jit(solution)/shard_map/reduce_scatter | solution.py:300
  151.0 1.4 reshape.110
  152.4 20.5 %all_to_all.16 = bf16[8,2,16384]{2,1,0:T(2,128)(2,1)S(1)} all-to-all(bf16[8,2,16384]{2,1,0:T(2,128)(2,1)S(1)} %reshape.110), channel_id=1, replica_groups={{0,1,2,3,4,5,6,7},{8,9,10,11,12,13,14,15},{16,17,18,19,20,21,22,23},{24..., dimensions={0} | all-to-all | bytes 1048576 | tf_op jit(solution)/shard_map/all_to_all | solution.py:303
  172.9 0.9 fusion.17
  (30 shorter events, 1.0 us)
Async XLA Ops:
  7.2 92.6 %all-gather.2.cloned.1.call-start = ((), (), s32[]{:S(2)}) async-start(), calls=%async_computation.4 | async-start | bytes 4755456 | tf_op jit(solution)/shard_map/all_gather | solution.py:260
  40.9 8.0 %copy-start.1 = (s32[384]{0:T(512)S(1)}, s32[384]{0:T(512)}, u32[]{:S(2)}) copy-start(s32[384]{0:T(512)} %param.11) | copy-start | bytes 4612
  41.7 23.1 %all-to-all-start.1 = ((bf16[8,8,2,16,128]{4,3,2,1,0:T(8,128)(2,1)}), bf16[8,8,2,16,128]{4,3,2,1,0:T(8,128)(2,1)S(1)}, u32[]{:S(2)}, u32[]{:S(2)}) async-start(bf16[8,8,2,16,128]{4,3,2,1,0:T(8,128)(2,1)} %bitcast.64), calls=%async_computation.1 | async-start | bytes 1048576 | tf_op jit(solution)/shard_map/all_to_all | solution.py:263
  48.8 102.2 %reduce-scatter.2.cloned.1.call-start = ((), (), s32[]{:S(2)}) async-start(), calls=%async_computation.5 | async-start | bytes 4718592 | tf_op jit(solution)/shard_map/reduce_scatter | solution.py:300
  64.9 11.1 %collective-permute-start.1 = (bf16[128,16,128]{2,1,0:T(8,128)(2,1)S(1)}, bf16[128,16,128]{2,1,0:T(8,128)(2,1)S(1)}, u32[]{:S(2)}, u32[]{:S(2)}) collective-permute-start(bf16[128,16,128]{2,1,0:T(8,128)(2,1)S(1)} %bitcast.67), channel_id=1, source_target_pairs={{0,128},{1,129},{2,130},{3,131},{4,132},{5,133},{6,134},{7,135},{8... | collective-permute-start | bytes 1572872 | tf_op jit(solution)/shard_map/ppermute | solution.py:266
  67.2 12.3 %collective-permute-start = (bf16[128,16,128]{2,1,0:T(8,128)(2,1)S(1)}, bf16[128,16,128]{2,1,0:T(8,128)(2,1)S(1)}, u32[]{:S(2)}, u32[]{:S(2)}) collective-permute-start(bf16[128,16,128]{2,1,0:T(8,128)(2,1)S(1)} %bitcast.68), channel_id=1, source_target_pairs={{0,384},{1,385},{2,386},{3,387},{4,388},{5,389},{6,390},{7,391},{8... | collective-permute-start | bytes 1572872 | tf_op jit(solution)/shard_map/ppermute | solution.py:267
  79.5 22.1 %copy-start = (bf16[128,384]{1,0:T(8,128)(2,1)S(1)}, bf16[128,384]{1,0:T(8,128)(2,1)}, u32[]{:S(2)}) copy-start(bf16[128,384]{1,0:T(8,128)(2,1)} %pred_ref.1) | copy-start | bytes 294916
  79.7 21.9 %collective-permute-start.3 = (bf16[3,128,16,128]{3,2,1,0:T(8,128)(2,1)S(1)}, bf16[3,128,16,128]{3,2,1,0:T(8,128)(2,1)}, u32[]{:S(2)}, u32[]{:S(2)}) collective-permute-start(bf16[3,128,16,128]{3,2,1,0:T(8,128)(2,1)S(1)} %pad_maximum_fusion.own_ref), channel_id=1, source_target_pairs={{0,64},{1,65},{2,66},{3,67},{4,68},{5,69},{6,70},{7,71},{8,72},{9,... | collective-permute-start | bytes 4718600 | tf_op jit(solution)/shard_map/ppermute | solution.py:270
  81.6 16.2 %collective-permute-start.2 = (bf16[128,16,128]{2,1,0:T(8,128)(2,1)S(1)}, bf16[128,16,128]{2,1,0:T(8,128)(2,1)S(1)}, u32[]{:S(2)}, u32[]{:S(2)}) collective-permute-start(bf16[128,16,128]{2,1,0:T(8,128)(2,1)S(1)} %collective-permute-done.1), channel_id=1, source_target_pairs={{0,128},{1,129},{2,130},{3,131},{4,132},{5,133},{6,134},{7,135},{8... | collective-permute-start | bytes 1572872 | tf_op jit(solution)/shard_map/ppermute | solution.py:268
  97.9 3.8 %collective-permute-start.4 = (bf16[128,16,128]{2,1,0:T(8,128)(2,1)S(1)}, bf16[128,16,128]{2,1,0:T(8,128)(2,1)S(1)}, u32[]{:S(2)}, u32[]{:S(2)}) collective-permute-start(bf16[128,16,128]{2,1,0:T(8,128)(2,1)S(1)} %collective-permute-done.2.own_far_ref), channel_id=1, source_target_pairs={{0,64},{1,65},{2,66},{3,67},{4,68},{5,69},{6,70},{7,71},{8,72},{9,... | collective-permute-start | bytes 1572872 | tf_op jit(solution)/shard_map/ppermute | solution.py:271
Sparse Core Ops, SparseCore 0:
  41.0 44.9 all-gather.1
  114.1 36.8 reduce-scatter.1

commit v9 on v6

--- a/solution.py
+++ b/solution.py
@@ -107,8 +107,8 @@
 
 
 def core_kernel(
-    core_ref, label_ref, x_hbm, own_ref, other_ref, pred_ref, limit_ref, rowp_ref, colp_ref,
-    flows_ref, c_hbm, x_ref, c_ref, acc_ref, g_ref, in_sem, out_sem,
+    core_ref, label_ref, x_hbm, own0, own1, own2, own3, other0, other1, other2, other3,
+    pred_ref, limit_ref, rowp_ref, colp_ref, flows_ref, c_hbm, x_ref, c_ref, acc_ref, g_ref, in_sem, out_sem,
 ):
     sources = label_ref.shape[0] // CAP
     step = sources // CHUNKS
@@ -133,7 +133,9 @@
 
     def tile(here, there):
         return jnp.concatenate(
-            [own_ref[d, here] for d in range(NX)] + [other_ref[d, there] for d in range(NX)], axis=0
+            [ref[here] for ref in (own0, own1, own2, own3)]
+            + [ref[there] for ref in (other0, other1, other2, other3)],
+            axis=0,
         )
 
     acc_ref[...] = jnp.zeros_like(acc_ref)
@@ -195,18 +197,18 @@
         leave(k).wait()
 
 
-def core_call(core, labels, x, own, other, pred, limit, rowp, colp, nbus):
+def core_call(core, labels, x, pieces, pred, limit, rowp, colp, nbus):
     rows, lines = pred.shape
     smem = pl.BlockSpec(memory_space=pltpu.SMEM)
     vmem = pl.BlockSpec(memory_space=pltpu.VMEM)
-    anywhere = pl.BlockSpec(memory_space=pl.ANY)
+    anywhere = pl.BlockSpec(memory_space=pltpu.HBM)
     return pl.pallas_call(
         core_kernel,
         out_shape=(
             jax.ShapeDtypeStruct((rows, lines), F32),
             jax.ShapeDtypeStruct((rows, nbus), BF16),
         ),
-        in_specs=[smem, smem, anywhere] + [vmem] * 6,
+        in_specs=[smem, smem, anywhere] + [vmem] * (2 * NX + 4),
         out_specs=(vmem, anywhere),
         scratch_shapes=[
             pltpu.VMEM((rows, nbus), BF16),
@@ -216,9 +218,9 @@
             pltpu.SemaphoreType.DMA((CHUNKS,)),
             pltpu.SemaphoreType.DMA((CHUNKS,)),
         ],
-        compiler_params=pltpu.CompilerParams(vmem_limit_bytes=32 * 1024 * 1024),
+        compiler_params=pltpu.CompilerParams(vmem_limit_bytes=46 * 1024 * 1024),
         name="flows_and_grad",
-    )(core.reshape(1), labels, x, own, other, pred, limit, rowp, colp)
+    )(core.reshape(1), labels, x, *pieces, pred, limit, rowp, colp)
 
 
 def add_up(parts):
@@ -255,9 +257,9 @@
     ).reshape((buses * CAP,) + tile_values.shape[1:])
     from_below = lax.ppermute(mine, AXES, X_UP)
     from_above = lax.ppermute(mine, AXES, X_DOWN)
-    from_far = lax.ppermute(from_below, AXES, X_UP)
-    own = jnp.stack([mine, from_above, from_far, from_below])
-    other = lax.ppermute(own, AXES, CORE_SWAP)
+    far = lax.ppermute(from_below, AXES, X_UP)
+    pieces = (mine, from_above, from_below, far)
+    pieces = pieces + tuple(lax.ppermute(p, AXES, CORE_SWAP) for p in pieces)
 
     tags = x_all[:, nbus:].astype(jnp.int32).reshape(buses, rows_here, TILE)
     line = tags[:, 0, :]
@@ -277,11 +279,13 @@
     swapped = ((col // 2) % 8 * 8 + col // 16) * 2 + col % 2
     rowp = (row == jnp.where(core == 0, col, swapped)).astype(BF16)
     chunk = row // 16
-    line_of = (((chunk % NX + x_here) % NX) * NC + jnp.where(chunk < NX, core, 1 - core)) * 16 + row % 16
+    piece = chunk % NX
+    offset = jnp.where(piece < 2, piece, 5 - piece)
+    line_of = (((offset + x_here) % NX) * NC + jnp.where(chunk < NX, core, 1 - core)) * 16 + row % 16
     colp = (col == line_of).astype(BF16)
 
     flows, contrib = core_call(
-        core, labels, x_all, own, other, flow_pred, line_limit.reshape(1, -1), rowp, colp, nbus
+        core, labels, x_all, pieces, flow_pred, line_limit.reshape(1, -1), rowp, colp, nbus
     )
 
     half = lax.psum_scatter(

time: 180 us -> 173 us (0.961)
  blocking collectives: 72 us -> 50 us
  starting transfers between devices: 10.4 us -> 23.5 us
  waiting for transfers between devices: 56.6 us -> 63.4 us
  local copies, waits for them, and re-layouts: 7.99 us -> 3.83 us
    all_to_all x1 -> x0, blocking collectives: 22 us -> none  [per_device(): lax.all_to_all(slots.swapaxes(0, 1), AXES, split_axis=0, concat_axis=0, t...]
    all_to_all x0 -> x1, waiting for transfers between devices: none -> 15.9 us  [per_device(): lax.all_to_all(slots.swapaxes(0, 1), AXES, split_axis=0, concat_axis=0, t...]
    ppermute x2 -> x5, waiting for transfers between devices: 10.9 us -> 2.87 us  [the longest x1 2.36 us: per_device(): far = lax.ppermute(from_below, AXES, X_UP)]
    all_to_all x0 -> x1, starting transfers between devices: none -> 7.23 us  [per_device(): lax.all_to_all(slots.swapaxes(0, 1), AXES, split_axis=0, concat_axis=0, t...]
    ppermute x2 -> x5, starting transfers between devices: 4.53 us -> 10.3 us  [the longest x4 8.16 us: per_device(): pieces = pieces + tuple((lax.ppermute(p, AXES, CORE_SWAP) for p in pieces))]
    unnamed x13 -> x5, local copies, waits for them, and re-layouts: 5.31 us -> 0.35 us
  transfers between devices with their start and end apart: 6 -> 10, of which waited for: 4 -> 5; matrix products, arithmetic and copies ran while one was open for 2% -> 1% of each run, Pallas kernels for 0% -> 0%
where the time goes in v9:
time: 173 us; the launch traced here: 172 us
  waiting for transfers between devices  63.4 us (37%)
  blocking collectives  50 us (29%)
  starting transfers between devices  23.5 us (14%)
  Pallas kernels  14.7 us (8%)
  between operations  14.3 us (8%)
  local copies, waits for them, and re-layouts  3.83 us (2%)
  other arithmetic  2.33 us (1%)
    reduce_scatter x1, waiting for transfers between devices, per_device(): lax.psum_scatter(contrib, AXES, scatter_dimension=0, tiled=True, axis_ind...  37.9 us
    all_to_all x1, blocking collectives, per_device(): lax.all_to_all(packed, AXES, split_axis=0, concat_axis=0, tiled=True, axi...  29.6 us
    all_to_all x1, blocking collectives, per_device(): lax.all_to_all(half.reshape(8, rows_here, nbus), AXES, split_axis=0, conc...  20.5 us
    all_to_all x1, waiting for transfers between devices, per_device(): lax.all_to_all(slots.swapaxes(0, 1), AXES, split_axis=0, concat_axis=0, t...  15.9 us
    pallas_call x1, Pallas kernels, core_call(): pl.pallas_call(core_kernel, out_shape=(jax.ShapeDtypeStruct((rows, lines)...  12.1 us
    ppermute x4, starting transfers between devices, per_device(): pieces = pieces + tuple((lax.ppermute(p, AXES, CORE_SWAP) for p in pieces))  8.16 us
    all_to_all x1, starting transfers between devices, per_device(): lax.all_to_all(slots.swapaxes(0, 1), AXES, split_axis=0, concat_axis=0, t...  7.23 us
    ppermute x1, waiting for transfers between devices, per_device(): from_below = lax.ppermute(mine, AXES, X_UP)  6.67 us
  transfers between devices with their start and end apart: 10, of which 5 were waited for; matrix products, arithmetic and copies ran while one was open for 1% of the time, Pallas kernels for 0%

profile of v9, /device:TPU:6, one launch (start us, length us, event | category | flops | bytes accessed | tf_op | source)
XLA Modules:
  0.0 172.2 jit_solution(8881118266415259735)
XLA Ops:
  7.2 2.6 %pack.1 = bf16[8,528,128]{2,1,0:T(8,128)(2,1)} custom-call(s32[1]{0:T(128)} %bitcast.core_ref, s32[64]{0:T(128)} %line_ref.1, s32[1,64]{1,0:T(1,128)} %bitcast.76, s32[1,64]{1,0:T(1,128)} %bitcast.78, bf16[64,16,128]{2,1,0:T(8,128)(2,1)} %tiles_ref.1, bf16[256,128]{1,0:T(8,128)(2,1)} %bitcast.74), custom_call_target="tpu_custom_call" | custom-call | tf_op jit(solution)/shard_map/pack/pallas_call | solution.py:91
  9.9 29.6 %all_to_all.15 = bf16[8,528,128]{2,1,0:T(8,128)(2,1)S(1)} all-to-all(bf16[8,528,128]{2,1,0:T(8,128)(2,1)} %pack.1), channel_id=1, replica_groups={{0,1,2,3,4,5,6,7},{8,9,10,11,12,13,14,15},{16,17,18,19,20,21,22,23},{24..., dimensions={0} | all-to-all | bytes 2162688 | tf_op jit(solution)/shard_map/all_to_all | solution.py:246
  39.6 0.3 copy.22
  40.0 0.8 pad_maximum_fusion
  40.9 0.8 copy.23
  41.7 7.2 %all-to-all-start.1 = ((bf16[8,8,2,16,128]{4,3,2,1,0:T(8,128)(2,1)}), bf16[8,8,2,16,128]{4,3,2,1,0:T(8,128)(2,1)S(1)}, u32[]{:S(2)}, u32[]{:S(2)}) async-start(bf16[8,8,2,16,128]{4,3,2,1,0:T(8,128)(2,1)} %bitcast.61), calls=%async_computation.1 | async-start | bytes 1048576 | tf_op jit(solution)/shard_map/all_to_all | solution.py:255
  49.1 15.9 %all-to-all-done.1 = bf16[8,8,2,16,128]{4,3,2,1,0:T(8,128)(2,1)S(1)} async-done(((bf16[8,8,2,16,128]{4,3,2,1,0:T(8,128)(2,1)}), bf16[8,8,2,16,128]{4,3,2,1,0:T(8,128)(2,1)S(1)}, u32[]{:S(2)}, u32[]{:S(2)}) %all-to-all-start.1) | async-done | bytes 524320 | tf_op jit(solution)/shard_map/all_to_all | solution.py:255
  65.0 2.4 %collective-permute-start.1 = (bf16[128,16,128]{2,1,0:T(8,128)(2,1)S(1)}, bf16[128,16,128]{2,1,0:T(8,128)(2,1)S(1)}, u32[]{:S(2)}, u32[]{:S(2)}) collective-permute-start(bf16[128,16,128]{2,1,0:T(8,128)(2,1)S(1)} %bitcast.62), channel_id=1, source_target_pairs={{0,128},{1,129},{2,130},{3,131},{4,132},{5,133},{6,134},{7,135},{8... | collective-permute-start | bytes 1572872 | tf_op jit(solution)/shard_map/ppermute | solution.py:258
  67.4 3.5 %collective-permute-start = (bf16[128,16,128]{2,1,0:T(8,128)(2,1)S(1)}, bf16[128,16,128]{2,1,0:T(8,128)(2,1)S(1)}, u32[]{:S(2)}, u32[]{:S(2)}) collective-permute-start(bf16[128,16,128]{2,1,0:T(8,128)(2,1)S(1)} %bitcast.63), channel_id=1, source_target_pairs={{0,384},{1,385},{2,386},{3,387},{4,388},{5,389},{6,390},{7,391},{8... | collective-permute-start | bytes 1572872 | tf_op jit(solution)/shard_map/ppermute | solution.py:259
  70.9 6.7 %collective-permute-done.1.own2 = bf16[128,16,128]{2,1,0:T(8,128)(2,1)S(1)} collective-permute-done((bf16[128,16,128]{2,1,0:T(8,128)(2,1)S(1)}, bf16[128,16,128]{2,1,0:T(8,128)(2,1)S(1)}, u32[]{:S(2)}, u32[]{:S(2)}) %collective-permute-start.1) | collective-permute-done | bytes 524320 | tf_op jit(solution)/shard_map/ppermute | solution.py:258
  77.6 2.2 %collective-permute-start.2 = (bf16[128,16,128]{2,1,0:T(8,128)(2,1)S(1)}, bf16[128,16,128]{2,1,0:T(8,128)(2,1)S(1)}, u32[]{:S(2)}, u32[]{:S(2)}) collective-permute-start(bf16[128,16,128]{2,1,0:T(8,128)(2,1)S(1)} %collective-permute-done.1.own2), channel_id=1, source_target_pairs={{0,128},{1,129},{2,130},{3,131},{4,132},{5,133},{6,134},{7,135},{8... | collective-permute-start | bytes 1572872 | tf_op jit(solution)/shard_map/ppermute | solution.py:260
  79.8 0.2 fusion.15
  80.0 1.9 %collective-permute-start.3 = (bf16[128,16,128]{2,1,0:T(8,128)(2,1)S(1)}, bf16[128,16,128]{2,1,0:T(8,128)(2,1)S(1)}, u32[]{:S(2)}, u32[]{:S(2)}) collective-permute-start(bf16[128,16,128]{2,1,0:T(8,128)(2,1)S(1)} %bitcast.64), channel_id=1, source_target_pairs={{0,64},{1,65},{2,66},{3,67},{4,68},{5,69},{6,70},{7,71},{8,72},{9,... | collective-permute-start | bytes 1572872 | tf_op jit(solution)/shard_map/ppermute | solution.py:262
  81.9 2.4 %collective-permute-start.5 = (bf16[128,16,128]{2,1,0:T(8,128)(2,1)S(1)}, bf16[128,16,128]{2,1,0:T(8,128)(2,1)S(1)}, u32[]{:S(2)}, u32[]{:S(2)}) collective-permute-start(bf16[128,16,128]{2,1,0:T(8,128)(2,1)S(1)} %collective-permute-done.1.own2), channel_id=1, source_target_pairs={{0,64},{1,65},{2,66},{3,67},{4,68},{5,69},{6,70},{7,71},{8,72},{9,... | collective-permute-start | bytes 1572872 | tf_op jit(solution)/shard_map/ppermute | solution.py:262
  84.3 1.9 %collective-permute-start.4 = (bf16[128,16,128]{2,1,0:T(8,128)(2,1)S(1)}, bf16[128,16,128]{2,1,0:T(8,128)(2,1)}, u32[]{:S(2)}, u32[]{:S(2)}) collective-permute-start(bf16[128,16,128]{2,1,0:T(8,128)(2,1)S(1)} %collective-permute-done.own1), channel_id=1, source_target_pairs={{0,64},{1,65},{2,66},{3,67},{4,68},{5,69},{6,70},{7,71},{8,72},{9,... | collective-permute-start | bytes 1572872 | tf_op jit(solution)/shard_map/ppermute | solution.py:262
  86.3 2.4 %collective-permute-done.2.own3 = bf16[128,16,128]{2,1,0:T(8,128)(2,1)S(1)} collective-permute-done((bf16[128,16,128]{2,1,0:T(8,128)(2,1)S(1)}, bf16[128,16,128]{2,1,0:T(8,128)(2,1)S(1)}, u32[]{:S(2)}, u32[]{:S(2)}) %collective-permute-start.2) | collective-permute-done | bytes 524320 | tf_op jit(solution)/shard_map/ppermute | solution.py:260
  88.6 1.9 %collective-permute-start.6 = (bf16[128,16,128]{2,1,0:T(8,128)(2,1)S(1)}, bf16[128,16,128]{2,1,0:T(8,128)(2,1)}, u32[]{:S(2)}, u32[]{:S(2)}) collective-permute-start(bf16[128,16,128]{2,1,0:T(8,128)(2,1)S(1)} %collective-permute-done.2.own3), channel_id=1, source_target_pairs={{0,64},{1,65},{2,66},{3,67},{4,68},{5,69},{6,70},{7,71},{8,72},{9,... | collective-permute-start | bytes 1572872 | tf_op jit(solution)/shard_map/ppermute | solution.py:262
  90.6 0.8 slice.58
  92.1 0.5 collective-permute-done.6.other3
  92.6 12.1 %flows_and_grad.1 = (f32[128,384]{1,0:T(8,128)}, bf16[128,16384]{1,0:T(8,128)(2,1)}) custom-call(s32[1]{0:T(128)} %bitcast.core_ref, s32[128]{0:T(128)S(1)} %reshape.113.label_ref, bf16[128,16512]{1,0:T(8,128)(2,1)} %all-gather.2.cloned.1.call-done.x_hbm, bf16[128,16,128]{2,1,0:T(8,128)(2,1)S(1)} %bitcast.65, ...), custom_call_target="tpu_custom_call" | custom-call | tf_op jit(solution)/shard_map/flows_and_grad/pallas_call | solution.py:205
  104.7 37.9 %reduce-scatter.2.cloned.1.call-done = bf16[16,16384]{1,0:T(8,128)(2,1)} async-done(((bf16[128,16384]{1,0:T(8,128)(2,1)}), bf16[16,16384]{1,0:T(8,128)(2,1)}) %reduce-scatter.2.cloned.1.call-update) | async-done | bytes 524304 | tf_op jit(solution)/shard_map/reduce_scatter | solution.py:291
  142.6 1.4 reshape.110
  144.0 20.5 %all_to_all.16 = bf16[8,2,16384]{2,1,0:T(2,128)(2,1)S(1)} all-to-all(bf16[8,2,16384]{2,1,0:T(2,128)(2,1)S(1)} %reshape.110), channel_id=1, replica_groups={{0,1,2,3,4,5,6,7},{8,9,10,11,12,13,14,15},{16,17,18,19,20,21,22,23},{24..., dimensions={0} | all-to-all | bytes 1048576 | tf_op jit(solution)/shard_map/all_to_all | solution.py:294
  164.4 0.9 fusion.17
  (33 shorter events, 1.0 us)
Async XLA Ops:
  7.2 83.4 %all-gather.2.cloned.1.call-start = ((), (), s32[]{:S(2)}) async-start(), calls=%async_computation.4 | async-start | bytes 4755456 | tf_op jit(solution)/shard_map/all_gather | solution.py:252
  40.9 8.2 %copy-start.1 = (s32[384]{0:T(512)S(1)}, s32[384]{0:T(512)}, u32[]{:S(2)}) copy-start(s32[384]{0:T(512)} %param.11) | copy-start | bytes 4612
  41.7 50.8 %copy-start = (bf16[128,384]{1,0:T(8,128)(2,1)S(1)}, bf16[128,384]{1,0:T(8,128)(2,1)}, u32[]{:S(2)}) copy-start(bf16[128,384]{1,0:T(8,128)(2,1)} %pred_ref.1) | copy-start | bytes 294916
  41.7 23.3 %all-to-all-start.1 = ((bf16[8,8,2,16,128]{4,3,2,1,0:T(8,128)(2,1)}), bf16[8,8,2,16,128]{4,3,2,1,0:T(8,128)(2,1)S(1)}, u32[]{:S(2)}, u32[]{:S(2)}) async-start(bf16[8,8,2,16,128]{4,3,2,1,0:T(8,128)(2,1)} %bitcast.61), calls=%async_computation.1 | async-start | bytes 1048576 | tf_op jit(solution)/shard_map/all_to_all | solution.py:255
  49.0 93.6 %reduce-scatter.2.cloned.1.call-start = ((), (), s32[]{:S(2)}) async-start(), calls=%async_computation.5 | async-start | bytes 4718592 | tf_op jit(solution)/shard_map/reduce_scatter | solution.py:291
  65.0 12.6 %collective-permute-start.1 = (bf16[128,16,128]{2,1,0:T(8,128)(2,1)S(1)}, bf16[128,16,128]{2,1,0:T(8,128)(2,1)S(1)}, u32[]{:S(2)}, u32[]{:S(2)}) collective-permute-start(bf16[128,16,128]{2,1,0:T(8,128)(2,1)S(1)} %bitcast.62), channel_id=1, source_target_pairs={{0,128},{1,129},{2,130},{3,131},{4,132},{5,133},{6,134},{7,135},{8... | collective-permute-start | bytes 1572872 | tf_op jit(solution)/shard_map/ppermute | solution.py:258
  67.4 16.9 %collective-permute-start = (bf16[128,16,128]{2,1,0:T(8,128)(2,1)S(1)}, bf16[128,16,128]{2,1,0:T(8,128)(2,1)S(1)}, u32[]{:S(2)}, u32[]{:S(2)}) collective-permute-start(bf16[128,16,128]{2,1,0:T(8,128)(2,1)S(1)} %bitcast.63), channel_id=1, source_target_pairs={{0,384},{1,385},{2,386},{3,387},{4,388},{5,389},{6,390},{7,391},{8... | collective-permute-start | bytes 1572872 | tf_op jit(solution)/shard_map/ppermute | solution.py:259
  77.6 11.1 %collective-permute-start.2 = (bf16[128,16,128]{2,1,0:T(8,128)(2,1)S(1)}, bf16[128,16,128]{2,1,0:T(8,128)(2,1)S(1)}, u32[]{:S(2)}, u32[]{:S(2)}) collective-permute-start(bf16[128,16,128]{2,1,0:T(8,128)(2,1)S(1)} %collective-permute-done.1.own2), channel_id=1, source_target_pairs={{0,128},{1,129},{2,130},{3,131},{4,132},{5,133},{6,134},{7,135},{8... | collective-permute-start | bytes 1572872 | tf_op jit(solution)/shard_map/ppermute | solution.py:260
  80.0 12.0 %collective-permute-start.3 = (bf16[128,16,128]{2,1,0:T(8,128)(2,1)S(1)}, bf16[128,16,128]{2,1,0:T(8,128)(2,1)S(1)}, u32[]{:S(2)}, u32[]{:S(2)}) collective-permute-start(bf16[128,16,128]{2,1,0:T(8,128)(2,1)S(1)} %bitcast.64), channel_id=1, source_target_pairs={{0,64},{1,65},{2,66},{3,67},{4,68},{5,69},{6,70},{7,71},{8,72},{9,... | collective-permute-start | bytes 1572872 | tf_op jit(solution)/shard_map/ppermute | solution.py:262
  81.9 10.1 %collective-permute-start.5 = (bf16[128,16,128]{2,1,0:T(8,128)(2,1)S(1)}, bf16[128,16,128]{2,1,0:T(8,128)(2,1)S(1)}, u32[]{:S(2)}, u32[]{:S(2)}) collective-permute-start(bf16[128,16,128]{2,1,0:T(8,128)(2,1)S(1)} %collective-permute-done.1.own2), channel_id=1, source_target_pairs={{0,64},{1,65},{2,66},{3,67},{4,68},{5,69},{6,70},{7,71},{8,72},{9,... | collective-permute-start | bytes 1572872 | tf_op jit(solution)/shard_map/ppermute | solution.py:262
  84.3 7.7 %collective-permute-start.4 = (bf16[128,16,128]{2,1,0:T(8,128)(2,1)S(1)}, bf16[128,16,128]{2,1,0:T(8,128)(2,1)}, u32[]{:S(2)}, u32[]{:S(2)}) collective-permute-start(bf16[128,16,128]{2,1,0:T(8,128)(2,1)S(1)} %collective-permute-done.own1), channel_id=1, source_target_pairs={{0,64},{1,65},{2,66},{3,67},{4,68},{5,69},{6,70},{7,71},{8,72},{9,... | collective-permute-start | bytes 1572872 | tf_op jit(solution)/shard_map/ppermute | solution.py:262
  88.6 3.9 %collective-permute-start.6 = (bf16[128,16,128]{2,1,0:T(8,128)(2,1)S(1)}, bf16[128,16,128]{2,1,0:T(8,128)(2,1)}, u32[]{:S(2)}, u32[]{:S(2)}) collective-permute-start(bf16[128,16,128]{2,1,0:T(8,128)(2,1)S(1)} %collective-permute-done.2.own3), channel_id=1, source_target_pairs={{0,64},{1,65},{2,66},{3,67},{4,68},{5,69},{6,70},{7,71},{8,72},{9,... | collective-permute-start | bytes 1572872 | tf_op jit(solution)/shard_map/ppermute | solution.py:262
Sparse Core Ops, SparseCore 0:
  41.0 45.0 all-gather.1
  104.8 37.7 reduce-scatter.1

commit v10 on v9

--- a/solution.py
+++ b/solution.py
@@ -152,7 +152,7 @@
                 acc_ref[line] = acc_ref[line] + part
         return carry
 
-    lax.fori_loop(0, CHUNKS, forward, 0)
+    lax.fori_loop(0, CHUNKS, forward, 0, unroll=2)
 
     rowp = rowp_ref[...]
     colp = colp_ref[...]
@@ -192,7 +192,7 @@
         leave(k).start()
         return carry
 
-    lax.fori_loop(0, CHUNKS, backward, 0)
+    lax.fori_loop(0, CHUNKS, backward, 0, unroll=2)
     for k in range(CHUNKS):
         leave(k).wait()
 

time: 173 us -> 172 us (level)
  no operation moved by 1% of the time
where the time goes in v10:
time: 172 us
  waiting for transfers between devices  63.4 us (37%)
  blocking collectives  50.1 us (29%)
  starting transfers between devices  23.5 us (14%)
  between operations  14.3 us (8%)
  Pallas kernels  14.2 us (8%)
  local copies, waits for them, and re-layouts  3.83 us (2%)
  other arithmetic  2.33 us (1%)
    reduce_scatter x1, waiting for transfers between devices, per_device(): lax.psum_scatter(contrib, AXES, scatter_dimension=0, tiled=True, axis_ind...  37.9 us
    all_to_all x1, blocking collectives, per_device(): lax.all_to_all(packed, AXES, split_axis=0, concat_axis=0, tiled=True, axi...  29.6 us
    all_to_all x1, blocking collectives, per_device(): lax.all_to_all(half.reshape(8, rows_here, nbus), AXES, split_axis=0, conc...  20.5 us
    all_to_all x1, waiting for transfers between devices, per_device(): lax.all_to_all(slots.swapaxes(0, 1), AXES, split_axis=0, concat_axis=0, t...  15.9 us
    pallas_call x1, Pallas kernels, core_call(): pl.pallas_call(core_kernel, out_shape=(jax.ShapeDtypeStruct((rows, lines)...  11.6 us
    ppermute x4, starting transfers between devices, per_device(): pieces = pieces + tuple((lax.ppermute(p, AXES, CORE_SWAP) for p in pieces))  8.16 us
    all_to_all x1, starting transfers between devices, per_device(): lax.all_to_all(slots.swapaxes(0, 1), AXES, split_axis=0, concat_axis=0, t...  7.23 us
    ppermute x1, waiting for transfers between devices, per_device(): from_below = lax.ppermute(mine, AXES, X_UP)  6.67 us
  transfers between devices with their start and end apart: 10, of which 5 were waited for; matrix products, arithmetic and copies ran while one was open for 1% of the time, Pallas kernels for 0%

profile of v10, /device:TPU:6, one launch (start us, length us, event | category | flops | bytes accessed | tf_op | source)
XLA Modules:
  0.0 171.7 jit_solution(15013371052606831568)
XLA Ops:
  7.2 2.6 %pack.1 = bf16[8,528,128]{2,1,0:T(8,128)(2,1)} custom-call(s32[1]{0:T(128)} %bitcast.core_ref, s32[64]{0:T(128)} %line_ref.1, s32[1,64]{1,0:T(1,128)} %bitcast.76, s32[1,64]{1,0:T(1,128)} %bitcast.78, bf16[64,16,128]{2,1,0:T(8,128)(2,1)} %tiles_ref.1, bf16[256,128]{1,0:T(8,128)(2,1)} %bitcast.74), custom_call_target="tpu_custom_call" | custom-call | tf_op jit(solution)/shard_map/pack/pallas_call | solution.py:91
  9.9 29.6 %all_to_all.15 = bf16[8,528,128]{2,1,0:T(8,128)(2,1)S(1)} all-to-all(bf16[8,528,128]{2,1,0:T(8,128)(2,1)} %pack.1), channel_id=1, replica_groups={{0,1,2,3,4,5,6,7},{8,9,10,11,12,13,14,15},{16,17,18,19,20,21,22,23},{24..., dimensions={0} | all-to-all | bytes 2162688 | tf_op jit(solution)/shard_map/all_to_all | solution.py:246
  39.6 0.3 copy.22
  40.0 0.8 pad_maximum_fusion
  40.9 0.8 copy.23
  41.7 7.2 %all-to-all-start.1 = ((bf16[8,8,2,16,128]{4,3,2,1,0:T(8,128)(2,1)}), bf16[8,8,2,16,128]{4,3,2,1,0:T(8,128)(2,1)S(1)}, u32[]{:S(2)}, u32[]{:S(2)}) async-start(bf16[8,8,2,16,128]{4,3,2,1,0:T(8,128)(2,1)} %bitcast.61), calls=%async_computation.1 | async-start | bytes 1048576 | tf_op jit(solution)/shard_map/all_to_all | solution.py:255
  49.1 15.9 %all-to-all-done.1 = bf16[8,8,2,16,128]{4,3,2,1,0:T(8,128)(2,1)S(1)} async-done(((bf16[8,8,2,16,128]{4,3,2,1,0:T(8,128)(2,1)}), bf16[8,8,2,16,128]{4,3,2,1,0:T(8,128)(2,1)S(1)}, u32[]{:S(2)}, u32[]{:S(2)}) %all-to-all-start.1) | async-done | bytes 524320 | tf_op jit(solution)/shard_map/all_to_all | solution.py:255
  65.0 2.4 %collective-permute-start.1 = (bf16[128,16,128]{2,1,0:T(8,128)(2,1)S(1)}, bf16[128,16,128]{2,1,0:T(8,128)(2,1)S(1)}, u32[]{:S(2)}, u32[]{:S(2)}) collective-permute-start(bf16[128,16,128]{2,1,0:T(8,128)(2,1)S(1)} %bitcast.62), channel_id=1, source_target_pairs={{0,128},{1,129},{2,130},{3,131},{4,132},{5,133},{6,134},{7,135},{8... | collective-permute-start | bytes 1572872 | tf_op jit(solution)/shard_map/ppermute | solution.py:258
  67.4 3.5 %collective-permute-start = (bf16[128,16,128]{2,1,0:T(8,128)(2,1)S(1)}, bf16[128,16,128]{2,1,0:T(8,128)(2,1)S(1)}, u32[]{:S(2)}, u32[]{:S(2)}) collective-permute-start(bf16[128,16,128]{2,1,0:T(8,128)(2,1)S(1)} %bitcast.63), channel_id=1, source_target_pairs={{0,384},{1,385},{2,386},{3,387},{4,388},{5,389},{6,390},{7,391},{8... | collective-permute-start | bytes 1572872 | tf_op jit(solution)/shard_map/ppermute | solution.py:259
  70.9 6.7 %collective-permute-done.1.own2 = bf16[128,16,128]{2,1,0:T(8,128)(2,1)S(1)} collective-permute-done((bf16[128,16,128]{2,1,0:T(8,128)(2,1)S(1)}, bf16[128,16,128]{2,1,0:T(8,128)(2,1)S(1)}, u32[]{:S(2)}, u32[]{:S(2)}) %collective-permute-start.1) | collective-permute-done | bytes 524320 | tf_op jit(solution)/shard_map/ppermute | solution.py:258
  77.6 2.2 %collective-permute-start.2 = (bf16[128,16,128]{2,1,0:T(8,128)(2,1)S(1)}, bf16[128,16,128]{2,1,0:T(8,128)(2,1)S(1)}, u32[]{:S(2)}, u32[]{:S(2)}) collective-permute-start(bf16[128,16,128]{2,1,0:T(8,128)(2,1)S(1)} %collective-permute-done.1.own2), channel_id=1, source_target_pairs={{0,128},{1,129},{2,130},{3,131},{4,132},{5,133},{6,134},{7,135},{8... | collective-permute-start | bytes 1572872 | tf_op jit(solution)/shard_map/ppermute | solution.py:260
  79.8 0.2 fusion.15
  80.0 1.9 %collective-permute-start.3 = (bf16[128,16,128]{2,1,0:T(8,128)(2,1)S(1)}, bf16[128,16,128]{2,1,0:T(8,128)(2,1)S(1)}, u32[]{:S(2)}, u32[]{:S(2)}) collective-permute-start(bf16[128,16,128]{2,1,0:T(8,128)(2,1)S(1)} %bitcast.64), channel_id=1, source_target_pairs={{0,64},{1,65},{2,66},{3,67},{4,68},{5,69},{6,70},{7,71},{8,72},{9,... | collective-permute-start | bytes 1572872 | tf_op jit(solution)/shard_map/ppermute | solution.py:262
  81.9 2.4 %collective-permute-start.5 = (bf16[128,16,128]{2,1,0:T(8,128)(2,1)S(1)}, bf16[128,16,128]{2,1,0:T(8,128)(2,1)S(1)}, u32[]{:S(2)}, u32[]{:S(2)}) collective-permute-start(bf16[128,16,128]{2,1,0:T(8,128)(2,1)S(1)} %collective-permute-done.1.own2), channel_id=1, source_target_pairs={{0,64},{1,65},{2,66},{3,67},{4,68},{5,69},{6,70},{7,71},{8,72},{9,... | collective-permute-start | bytes 1572872 | tf_op jit(solution)/shard_map/ppermute | solution.py:262
  84.3 1.9 %collective-permute-start.4 = (bf16[128,16,128]{2,1,0:T(8,128)(2,1)S(1)}, bf16[128,16,128]{2,1,0:T(8,128)(2,1)}, u32[]{:S(2)}, u32[]{:S(2)}) collective-permute-start(bf16[128,16,128]{2,1,0:T(8,128)(2,1)S(1)} %collective-permute-done.own1), channel_id=1, source_target_pairs={{0,64},{1,65},{2,66},{3,67},{4,68},{5,69},{6,70},{7,71},{8,72},{9,... | collective-permute-start | bytes 1572872 | tf_op jit(solution)/shard_map/ppermute | solution.py:262
  86.3 2.4 %collective-permute-done.2.own3 = bf16[128,16,128]{2,1,0:T(8,128)(2,1)S(1)} collective-permute-done((bf16[128,16,128]{2,1,0:T(8,128)(2,1)S(1)}, bf16[128,16,128]{2,1,0:T(8,128)(2,1)S(1)}, u32[]{:S(2)}, u32[]{:S(2)}) %collective-permute-start.2) | collective-permute-done | bytes 524320 | tf_op jit(solution)/shard_map/ppermute | solution.py:260
  88.6 1.9 %collective-permute-start.6 = (bf16[128,16,128]{2,1,0:T(8,128)(2,1)S(1)}, bf16[128,16,128]{2,1,0:T(8,128)(2,1)}, u32[]{:S(2)}, u32[]{:S(2)}) collective-permute-start(bf16[128,16,128]{2,1,0:T(8,128)(2,1)S(1)} %collective-permute-done.2.own3), channel_id=1, source_target_pairs={{0,64},{1,65},{2,66},{3,67},{4,68},{5,69},{6,70},{7,71},{8,72},{9,... | collective-permute-start | bytes 1572872 | tf_op jit(solution)/shard_map/ppermute | solution.py:262
  90.6 0.8 slice.58
  92.1 0.5 collective-permute-done.6.other3
  92.6 11.6 %flows_and_grad.1 = (f32[128,384]{1,0:T(8,128)}, bf16[128,16384]{1,0:T(8,128)(2,1)}) custom-call(s32[1]{0:T(128)} %bitcast.core_ref, s32[128]{0:T(128)S(1)} %reshape.113.label_ref, bf16[128,16512]{1,0:T(8,128)(2,1)} %all-gather.2.cloned.1.call-done.x_hbm, bf16[128,16,128]{2,1,0:T(8,128)(2,1)S(1)} %bitcast.65, ...), custom_call_target="tpu_custom_call" | custom-call | tf_op jit(solution)/shard_map/flows_and_grad/pallas_call | solution.py:205
  104.2 37.9 %reduce-scatter.2.cloned.1.call-done = bf16[16,16384]{1,0:T(8,128)(2,1)} async-done(((bf16[128,16384]{1,0:T(8,128)(2,1)}), bf16[16,16384]{1,0:T(8,128)(2,1)}) %reduce-scatter.2.cloned.1.call-update) | async-done | bytes 524304 | tf_op jit(solution)/shard_map/reduce_scatter | solution.py:291
  142.1 1.4 reshape.110
  143.4 20.5 %all_to_all.16 = bf16[8,2,16384]{2,1,0:T(2,128)(2,1)S(1)} all-to-all(bf16[8,2,16384]{2,1,0:T(2,128)(2,1)S(1)} %reshape.110), channel_id=1, replica_groups={{0,1,2,3,4,5,6,7},{8,9,10,11,12,13,14,15},{16,17,18,19,20,21,22,23},{24..., dimensions={0} | all-to-all | bytes 1048576 | tf_op jit(solution)/shard_map/all_to_all | solution.py:294
  163.9 0.9 fusion.17
  (33 shorter events, 1.0 us)
Async XLA Ops:
  7.2 83.4 %all-gather.2.cloned.1.call-start = ((), (), s32[]{:S(2)}) async-start(), calls=%async_computation.4 | async-start | bytes 4755456 | tf_op jit(solution)/shard_map/all_gather | solution.py:252
  40.9 8.2 %copy-start.1 = (s32[384]{0:T(512)S(1)}, s32[384]{0:T(512)}, u32[]{:S(2)}) copy-start(s32[384]{0:T(512)} %param.11) | copy-start | bytes 4612
  41.7 50.8 %copy-start = (bf16[128,384]{1,0:T(8,128)(2,1)S(1)}, bf16[128,384]{1,0:T(8,128)(2,1)}, u32[]{:S(2)}) copy-start(bf16[128,384]{1,0:T(8,128)(2,1)} %pred_ref.1) | copy-start | bytes 294916
  41.7 23.3 %all-to-all-start.1 = ((bf16[8,8,2,16,128]{4,3,2,1,0:T(8,128)(2,1)}), bf16[8,8,2,16,128]{4,3,2,1,0:T(8,128)(2,1)S(1)}, u32[]{:S(2)}, u32[]{:S(2)}) async-start(bf16[8,8,2,16,128]{4,3,2,1,0:T(8,128)(2,1)} %bitcast.61), calls=%async_computation.1 | async-start | bytes 1048576 | tf_op jit(solution)/shard_map/all_to_all | solution.py:255
  49.0 93.1 %reduce-scatter.2.cloned.1.call-start = ((), (), s32[]{:S(2)}) async-start(), calls=%async_computation.5 | async-start | bytes 4718592 | tf_op jit(solution)/shard_map/reduce_scatter | solution.py:291
  65.0 12.6 %collective-permute-start.1 = (bf16[128,16,128]{2,1,0:T(8,128)(2,1)S(1)}, bf16[128,16,128]{2,1,0:T(8,128)(2,1)S(1)}, u32[]{:S(2)}, u32[]{:S(2)}) collective-permute-start(bf16[128,16,128]{2,1,0:T(8,128)(2,1)S(1)} %bitcast.62), channel_id=1, source_target_pairs={{0,128},{1,129},{2,130},{3,131},{4,132},{5,133},{6,134},{7,135},{8... | collective-permute-start | bytes 1572872 | tf_op jit(solution)/shard_map/ppermute | solution.py:258
  67.4 16.9 %collective-permute-start = (bf16[128,16,128]{2,1,0:T(8,128)(2,1)S(1)}, bf16[128,16,128]{2,1,0:T(8,128)(2,1)S(1)}, u32[]{:S(2)}, u32[]{:S(2)}) collective-permute-start(bf16[128,16,128]{2,1,0:T(8,128)(2,1)S(1)} %bitcast.63), channel_id=1, source_target_pairs={{0,384},{1,385},{2,386},{3,387},{4,388},{5,389},{6,390},{7,391},{8... | collective-permute-start | bytes 1572872 | tf_op jit(solution)/shard_map/ppermute | solution.py:259
  77.6 11.1 %collective-permute-start.2 = (bf16[128,16,128]{2,1,0:T(8,128)(2,1)S(1)}, bf16[128,16,128]{2,1,0:T(8,128)(2,1)S(1)}, u32[]{:S(2)}, u32[]{:S(2)}) collective-permute-start(bf16[128,16,128]{2,1,0:T(8,128)(2,1)S(1)} %collective-permute-done.1.own2), channel_id=1, source_target_pairs={{0,128},{1,129},{2,130},{3,131},{4,132},{5,133},{6,134},{7,135},{8... | collective-permute-start | bytes 1572872 | tf_op jit(solution)/shard_map/ppermute | solution.py:260
  80.0 12.0 %collective-permute-start.3 = (bf16[128,16,128]{2,1,0:T(8,128)(2,1)S(1)}, bf16[128,16,128]{2,1,0:T(8,128)(2,1)S(1)}, u32[]{:S(2)}, u32[]{:S(2)}) collective-permute-start(bf16[128,16,128]{2,1,0:T(8,128)(2,1)S(1)} %bitcast.64), channel_id=1, source_target_pairs={{0,64},{1,65},{2,66},{3,67},{4,68},{5,69},{6,70},{7,71},{8,72},{9,... | collective-permute-start | bytes 1572872 | tf_op jit(solution)/shard_map/ppermute | solution.py:262
  81.9 10.1 %collective-permute-start.5 = (bf16[128,16,128]{2,1,0:T(8,128)(2,1)S(1)}, bf16[128,16,128]{2,1,0:T(8,128)(2,1)S(1)}, u32[]{:S(2)}, u32[]{:S(2)}) collective-permute-start(bf16[128,16,128]{2,1,0:T(8,128)(2,1)S(1)} %collective-permute-done.1.own2), channel_id=1, source_target_pairs={{0,64},{1,65},{2,66},{3,67},{4,68},{5,69},{6,70},{7,71},{8,72},{9,... | collective-permute-start | bytes 1572872 | tf_op jit(solution)/shard_map/ppermute | solution.py:262
  84.3 7.7 %collective-permute-start.4 = (bf16[128,16,128]{2,1,0:T(8,128)(2,1)S(1)}, bf16[128,16,128]{2,1,0:T(8,128)(2,1)}, u32[]{:S(2)}, u32[]{:S(2)}) collective-permute-start(bf16[128,16,128]{2,1,0:T(8,128)(2,1)S(1)} %collective-permute-done.own1), channel_id=1, source_target_pairs={{0,64},{1,65},{2,66},{3,67},{4,68},{5,69},{6,70},{7,71},{8,72},{9,... | collective-permute-start | bytes 1572872 | tf_op jit(solution)/shard_map/ppermute | solution.py:262
  88.6 3.9 %collective-permute-start.6 = (bf16[128,16,128]{2,1,0:T(8,128)(2,1)S(1)}, bf16[128,16,128]{2,1,0:T(8,128)(2,1)}, u32[]{:S(2)}, u32[]{:S(2)}) collective-permute-start(bf16[128,16,128]{2,1,0:T(8,128)(2,1)S(1)} %collective-permute-done.2.own3), channel_id=1, source_target_pairs={{0,64},{1,65},{2,66},{3,67},{4,68},{5,69},{6,70},{7,71},{8,72},{9,... | collective-permute-start | bytes 1572872 | tf_op jit(solution)/shard_map/ppermute | solution.py:262
Sparse Core Ops, SparseCore 0:
  41.0 45.0 all-gather.1
  104.3 37.7 reduce-scatter.1
